TPU v7x, 32 devices: a whole 2x2x4 slice. The times are simulated.
32 devices in a mesh: groups: 2 (over x), seq: 16 (over z, y, core).
Axes of the slice: x: 2, y: 2, z: 4, core: 2. Of those that a mesh axis runs over, the one named last changes fastest.
Arguments:
- query_rows: bfloat16 [16384, 1024], P(('groups', 'seq')), parts along dimension 0, may hold values from -6 to 6
- key_rows: bfloat16 [16384, 1024], P(('groups', 'seq')), parts along dimension 0, may hold values from -6 to 6
- value_rows: bfloat16 [16384, 1024], P(('groups', 'seq')), parts along dimension 0, may hold values from -6 to 6
- log_decay: float32 [8, 16384], P(None, ('groups', 'seq')), parts along dimension 1
- run_start: int32 [16384], P(('groups', 'seq')), parts along dimension 0, may hold values 0 or 1
- out_grad: bfloat16 [16384, 1024], P(('groups', 'seq')), parts along dimension 0, may hold values from -6 to 6
Outputs:
- attended: bfloat16 [16384, 1024], P(('groups', 'seq')), parts along dimension 0
- query_grad: bfloat16 [16384, 1024], P(('groups', 'seq')), parts along dimension 0
- key_grad: bfloat16 [16384, 1024], P(('groups', 'seq')), parts along dimension 0
- value_grad: bfloat16 [16384, 1024], P(('groups', 'seq')), parts along dimension 0
There are 2 independent parts, one for each index of `groups`. A program takes and returns all parts, laid end to end along the dimension named above; each array names one. Nothing has to cross between parts.
Inputs may be any that keep to these rules, and one draw needn't show every extreme that they name: `run_start`: 1 marks a position at which a new run begins and the state starts afresh.
All inputs are finite; a program needn't handle non-finite values. No bound on the sum of `run_start` on one device may be relied on, other than what follows from the above.
Results may differ from a plain program's by a relative error of at most 0.0086.
Values sent between devices are 32-bit elements; how exact they have to be, the bound alone decides.
No kernel may reach another device: no remote copies, remote signals or barrier semaphores. Data moves between devices by JAX's collectives and lax.ppermute only.
A program may use at most 128 MiB of HBM per device.

v0:
```python
import jax
import jax.numpy as jnp
from jax import lax
from jax.sharding import PartitionSpec as P

BLOCK = 256


norm_eps = 1e-05


def entering_2(part, axis, combine, identity, reverse):
    count = lax.axis_size(axis)
    place = lax.axis_index(axis)
    ahead = count - 1 - place if reverse else place
    gathered = jax.tree.map(lambda a: lax.all_gather(a, axis), part)
    state = jax.tree.map(lambda a, e: jnp.zeros_like(a) + jnp.asarray(e, a.dtype), part, identity)

    def one(step, state):
        source = count - 1 - step if reverse else step
        return combine(
            state, jax.tree.map(lambda a: lax.dynamic_index_in_dim(a, source, 0, False), gathered)
        )

    return lax.fori_loop(0, ahead, one, state)


def block_terms(decays, starts):
    cumulative = jnp.cumsum(decays, axis=-1)
    run_counts = jnp.cumsum(starts, axis=-1, dtype=jnp.int32)
    untouched = (run_counts == 0).astype(jnp.float32)
    entering = jnp.exp(cumulative) * untouched[..., None, :]
    closing = cumulative[..., -1:]
    same_tail = (run_counts == run_counts[..., -1:]).astype(jnp.float32)
    leaving = jnp.exp(closing - cumulative) * same_tail[..., None, :]
    carry_keep = jnp.exp(closing[..., 0]) * untouched[..., -1:]
    differences = cumulative[..., :, None] - cumulative[..., None, :]
    token_locations = jnp.arange(starts.shape[-1])
    permitted = (token_locations[:, None] >= token_locations[None, :]) & (
        run_counts[..., :, None] == run_counts[..., None, :]
    )
    decay_grid = jnp.where(permitted[..., None, :, :], jnp.exp(jnp.minimum(differences, 0.0)), 0.0)
    return (entering, leaving, carry_keep, decay_grid)


def join_affine(earlier, later_part):
    return (earlier[0] * later_part[0], later_part[0][:, None, None] * earlier[1] + later_part[1])


def local(query_rows, key_rows, value_rows, log_decay, run_start, out_grad):
    head_count = log_decay.shape[0]
    head_size = query_rows.shape[1] // head_count
    blocks = query_rows.shape[0] // BLOCK
    shape_four = (blocks, BLOCK, head_count, head_size)
    queries = query_rows.reshape(shape_four)
    keys_all = key_rows.reshape(shape_four)
    values_all = value_rows.reshape(shape_four)
    decays = jnp.swapaxes(log_decay.reshape(head_count, blocks, BLOCK), 0, 1)
    starts = run_start.reshape(blocks, BLOCK)
    entering, leaving, carry_keep, decay_grid = block_terms(decays, starts)
    enter_rows = jnp.swapaxes(entering, 1, 2)[..., None]
    leave_rows = jnp.swapaxes(leaving, 1, 2)[..., None]
    scores = jnp.einsum("nthd,nshd->nhts", queries, keys_all, preferred_element_type=jnp.float32)
    weighted = (scores * decay_grid).astype(jnp.bfloat16)
    within = jnp.einsum("nhts,nshd->nthd", weighted, values_all, preferred_element_type=jnp.float32)
    key_scaled = (keys_all * leave_rows).astype(jnp.bfloat16)
    local_terms = jnp.einsum(
        "nshd,nshe->nhde", key_scaled, values_all, preferred_element_type=jnp.float32
    )
    zero_state = jnp.zeros(local_terms.shape[1:], jnp.float32)
    unit_keep = jnp.ones((head_count,), jnp.float32)
    running = zero_state
    product = unit_keep
    before_list = []
    keep_list = []
    for block_number in range(blocks):
        before_list.append(running)
        keep_list.append(product)
        running = carry_keep[block_number][:, None, None] * running + local_terms[block_number]
        product = product * carry_keep[block_number]
    incoming = entering_2((product, running), "seq", join_affine, (unit_keep, zero_state), False)[1]
    states = jnp.stack(
        [
            before_list[block_number] + keep_list[block_number][:, None, None] * incoming
            for block_number in range(blocks)
        ]
    )
    states_low = states.astype(jnp.bfloat16)
    carried = (
        jnp.einsum("nthd,nhde->nthe", queries, states_low, preferred_element_type=jnp.float32)
        * enter_rows
    )
    mixture = within + carried
    inverse_rms = lax.rsqrt(jnp.mean(mixture * mixture, axis=-1, keepdims=True) + norm_eps)
    normed = mixture * inverse_rms
    attended = normed.astype(jnp.bfloat16)
    grad_wide = out_grad.reshape(shape_four).astype(jnp.float32)
    mixture_low = (
        inverse_rms * (grad_wide - normed * jnp.mean(grad_wide * normed, axis=-1, keepdims=True))
    ).astype(jnp.bfloat16)
    prob_grad = jnp.einsum(
        "nthe,nshe->nhts", mixture_low, values_all, preferred_element_type=jnp.float32
    )
    masked_grad = (prob_grad * decay_grid).astype(jnp.bfloat16)
    query_scaled = (queries * enter_rows).astype(jnp.bfloat16)
    back_terms = jnp.einsum(
        "nthd,nthe->nhde", query_scaled, mixture_low, preferred_element_type=jnp.float32
    )
    running = zero_state
    product = unit_keep
    after_list = [zero_state] * blocks
    keep_after = [unit_keep] * blocks
    for block_number in reversed(range(blocks)):
        after_list[block_number] = running
        keep_after[block_number] = product
        running = carry_keep[block_number][:, None, None] * running + back_terms[block_number]
        product = product * carry_keep[block_number]
    outgoing = entering_2((product, running), "seq", join_affine, (unit_keep, zero_state), True)[1]
    afters_low = jnp.stack(
        [
            after_list[block_number] + keep_after[block_number][:, None, None] * outgoing
            for block_number in range(blocks)
        ]
    ).astype(jnp.bfloat16)
    query_grad = (
        jnp.einsum("nhts,nshd->nthd", masked_grad, keys_all, preferred_element_type=jnp.float32)
        + jnp.einsum("nthe,nhde->nthd", mixture_low, states_low, preferred_element_type=jnp.float32)
        * enter_rows
    )
    key_grad = (
        jnp.einsum("nhts,nthd->nshd", masked_grad, queries, preferred_element_type=jnp.float32)
        + jnp.einsum("nshe,nhde->nshd", values_all, afters_low, preferred_element_type=jnp.float32)
        * leave_rows
    )
    value_grad = (
        jnp.einsum("nhts,nthe->nshe", weighted, mixture_low, preferred_element_type=jnp.float32)
        + jnp.einsum("nshd,nhde->nshe", keys_all, afters_low, preferred_element_type=jnp.float32)
        * leave_rows
    )
    flat_shape = query_rows.shape
    return (
        attended.reshape(flat_shape),
        query_grad.astype(jnp.bfloat16).reshape(flat_shape),
        key_grad.astype(jnp.bfloat16).reshape(flat_shape),
        value_grad.astype(jnp.bfloat16).reshape(flat_shape),
    )


def solution(mesh):
    placed = (
        P(("groups", "seq"), None),
        P(("groups", "seq"), None),
        P(("groups", "seq"), None),
        P(None, ("groups", "seq")),
        P(("groups", "seq")),
        P(("groups", "seq"), None),
    )
    return jax.shard_map(
        local,
        mesh=mesh,
        in_specs=placed,
        out_specs=(
            P(("groups", "seq"), None),
            P(("groups", "seq"), None),
            P(("groups", "seq"), None),
            P(("groups", "seq"), None),
        ),
        check_vma=False,
    )
```

profile of v0, /device:TPU:0, one launch (start us, length us, event | category | flops | bytes accessed | tf_op | source)
XLA Modules:
  0.0 229.5 jit_solution(4873724288296719088)
XLA Ops:
  7.2 1.4 reduce-window.14
  9.5 2.2 reduce-window.16
  12.3 1.5 copy.221
  15.2 2.1 fusion.7
  20.7 1.8 copy.225
  22.6 1.9 copy.187
  24.5 23.2 %all-gather = f32[16,1,8]{2,1,0:T(1,128)S(1)} all-gather(f32[1,1,8]{2,1,0:T(1,128)S(1)} %get-tuple-element.228), channel_id=1, replica_groups=mesh['groups'=2,'seq'=16] {'seq'}, dimensions={0}, use_global_device_ids=true | all-gather | bytes 544 | tf_op jit(solution)/shard_map/all_gather | solution.py:16
  47.9 2.9 %multiply_convert_fusion.1 = bf16[2,8,256,256]{3,2,1,0:T(8,128)(2,1)S(1)} fusion(bf16[2,256,8,128]{1,3,2,0:T(8,128)(2,1)S(1)} %copy.196, f32[2,8,256]{2,1,0:T(8,128)S(1)} %get-tuple-element.215, pred[2,256,256]{2,1,0:T(8,128)(4,1)S(1)} %compare_and_fusion, bf16[2,256,8,128]{3,2,1,0:T(8,128)(2,1)} %bitcast.153), kind=kOutput, calls=%fused_computation.5 | convolution fusion | flops 273678336 | bytes 4341760 | tf_op jit(solution)/shard_map/nthd,nshd->nhts/dot_general | solution.py:63
  50.9 1.4 copy-done.9
  52.2 2.2 fusion.11
  54.4 42.6 %all-gather.4.cloned.1.call-done = f32[16,8,128,128]{3,2,1,0:T(8,128)} async-done(((f32[1,8,128,128]{3,2,1,0:T(8,128)}), f32[16,8,128,128]{3,2,1,0:T(8,128)}) %all-gather.4.cloned.1.call-update) | async-done | bytes 8388624 | tf_op jit(solution)/shard_map/all_gather | solution.py:16
  98.4 2.2 multiply_reduce_fusion.1
  101.0 1.5 multiply_convert_fusion.3
  104.2 2.4 %copy.185 = bf16[2,256,8,128]{3,2,1,0:T(8,128)(2,1)} copy(bf16[2,256,8,128]{1,3,2,0:T(8,128)(2,1)} %get-tuple-element.217) | data formatting | bytes 2097152 | tf_op jit(solution)/shard_map/convert_element_type | solution.py:96
  106.6 2.5 %multiply_convert_fusion = bf16[2,8,256,256]{3,2,1,0:T(8,128)(2,1)S(1)} fusion(bf16[2,256,8,128]{1,3,2,0:T(8,128)(2,1)S(1)} %get-tuple-element.216, f32[2,8,256]{2,1,0:T(8,128)S(1)} %get-tuple-element.215, pred[2,256,256]{2,1,0:T(8,128)(4,1)} %copy-done.23, bf16[2,256,8,128]{3,2,1,0:T(8,128)(2,1)S(1)} %bitcast.150), kind=kOutput, calls=%fused_computation.4 | convolution fusion | flops 273678336 | bytes 4341760 | tf_op jit(solution)/shard_map/nthe,nshe->nhts/dot_general | solution.py:101
  110.5 1.4 fusion.5
  111.9 2.5 %copy.193 = bf16[2,256,8,128]{3,2,1,0:T(8,128)(2,1)} copy(bf16[2,256,8,128]{1,3,2,0:T(8,128)(2,1)} %fusion.5) | data formatting | bytes 2097152 | tf_op jit(solution)/shard_map/convert_element_type | solution.py:143
  114.4 3.2 %copy_bitcast_fusion.2 = (bf16[512,1024]{1,0:T(8,128)(2,1)}, bf16[512,1024]{1,0:T(8,128)(2,1)}) fusion(bf16[64,8,8,128]{3,2,1,0:T(8,128)(2,1)} %bitcast.160, bf16[64,8,8,128]{3,2,1,0:T(8,128)(2,1)S(1)} %bitcast.158), kind=kLoop, calls=%fused_computation.29 | loop fusion | bytes 4194304 | tf_op jit(solution)/shard_map/reshape | solution.py:143
  117.6 2.2 fusion.32
  119.9 2.1 fusion.31
  122.0 73.7 %all-gather.6.cloned.1.call-done = f32[16,8,128,128]{3,2,1,0:T(8,128)} async-done(((f32[1,8,128,128]{3,2,1,0:T(8,128)}), f32[16,8,128,128]{3,2,1,0:T(8,128)}) %all-gather.6.cloned.1.call-update) | async-done | bytes 8388624 | tf_op jit(solution)/shard_map/all_gather | solution.py:16
  195.7 18.7 %while.27 = (s32[]{:T(128)}, f32[8,128,128]{2,1,0:T(8,128)S(1)}, s32[]{:T(128)}, f32[16,8]{1,0:T(8,128)S(1)}, f32[16,8,128,128]{3,2,1,0:T(8,128)}, /*index=5*/s32[]{:T(128)}, s32[]{:T(128)}, s32[]{:T(128)}, s32[]{:T(128)}) while((s32[]{:T(128)}, f32[8,128,128]{2,1,0:T(8,128)S(1)}, s32[]{:T(128)}, f32[16,8]{1,0:T(8,128)S(1)}, ...), condition=%wide.region_9.10_spmd, body=%wide.region_8.9_spmd.sunk | while | flops 262150 | bytes 1573115 | solution.py:25
  215.7 2.0 fusion.1
  220.8 1.8 copy_bitcast_fusion
  (118 shorter events, 33.7 us)
Async XLA Ops:
  7.2 6.7 %copy-start.21 = (bf16[512,1024]{1,0:T(8,128)(2,1)S(1)}, bf16[512,1024]{1,0:T(8,128)(2,1)}, u32[]{:S(2)}) copy-start(bf16[512,1024]{1,0:T(8,128)(2,1)} %param.12) | copy-start | bytes 3145732
  7.2 89.8 %all-gather.4.cloned.1.call-start = ((), (), s32[]{:S(2)}) async-start(), calls=%async_computation | async-start | bytes 8912896 | tf_op jit(solution)/shard_map/all_gather | solution.py:16
  13.8 3.4 %copy-start.6 = (bf16[64,8,8,128]{3,2,1,0:T(8,128)(2,1)}, bf16[64,8,8,128]{3,2,1,0:T(8,128)(2,1)S(1)}, u32[]{:S(2)}) copy-start(bf16[64,8,8,128]{3,2,1,0:T(8,128)(2,1)S(1)} %copy.221) | copy-start | bytes 3145732
  15.2 4.1 %copy-start.22 = (bf16[512,1024]{1,0:T(8,128)(2,1)S(1)}, bf16[512,1024]{1,0:T(8,128)(2,1)}, u32[]{:S(2)}) copy-start(bf16[512,1024]{1,0:T(8,128)(2,1)} %param.10) | copy-start | bytes 3145732
  19.2 176.5 %all-gather.6.cloned.1.call-start = ((), (), s32[]{:S(2)}) async-start(), calls=%async_computation.1 | async-start | bytes 8912896 | tf_op jit(solution)/shard_map/all_gather | solution.py:16
  19.2 1.2 copy-start.20
  20.5 27.4 %copy-start = (bf16[2,256,8,128]{1,3,2,0:T(8,128)(2,1)}, bf16[2,256,8,128]{1,3,2,0:T(8,128)(2,1)S(1)}, u32[]{:S(2)}) copy-start(bf16[2,256,8,128]{1,3,2,0:T(8,128)(2,1)S(1)} %copy.196) | copy-start | bytes 3145732
  47.9 2.9 %copy-start.23 = (pred[2,256,256]{2,1,0:T(8,128)(4,1)}, pred[2,256,256]{2,1,0:T(8,128)(4,1)S(1)}, u32[]{:S(2)}) copy-start(pred[2,256,256]{2,1,0:T(8,128)(4,1)S(1)} %compare_and_fusion) | copy-start | bytes 393220
  47.9 4.3 %copy-start.4 = (bf16[64,8,8,128]{3,2,1,0:T(8,128)(2,1)S(1)}, bf16[64,8,8,128]{3,2,1,0:T(8,128)(2,1)}, u32[]{:S(2)}) copy-start(bf16[64,8,8,128]{3,2,1,0:T(8,128)(2,1)} %copy-done.3) | copy-start | bytes 3145732
  50.8 1.4 copy-start.9
  97.0 1.4 copy-start.1
  98.3 2.3 copy-start.17
  103.0 1.2 copy-start.14
  103.0 3.6 %copy-start.5 = (bf16[64,8,8,128]{3,2,1,0:T(8,128)(2,1)S(1)}, bf16[64,8,8,128]{3,2,1,0:T(8,128)(2,1)}, u32[]{:S(2)}) copy-start(bf16[64,8,8,128]{3,2,1,0:T(8,128)(2,1)} %copy-done.3) | copy-start | bytes 3145732
  106.6 2.5 %copy-start.7 = (bf16[64,8,8,128]{3,2,1,0:T(8,128)(2,1)S(1)}, bf16[64,8,8,128]{3,2,1,0:T(8,128)(2,1)}, u32[]{:S(2)}) copy-start(bf16[64,8,8,128]{3,2,1,0:T(8,128)(2,1)} %copy-done.6) | copy-start | bytes 3145732
  109.1 1.3 copy-start.12
  109.1 1.3 copy-start.18
  111.9 2.5 %copy-start.16 = (bf16[2,256,8,128]{3,2,1,0:T(8,128)(2,1)S(1)}, bf16[2,256,8,128]{3,2,1,0:T(8,128)(2,1)}, u32[]{:S(2)}) copy-start(bf16[2,256,8,128]{3,2,1,0:T(8,128)(2,1)} %copy.185) | copy-start | bytes 3145732
  114.4 3.2 %copy-start.10 = (bf16[2,8,256,256]{3,2,1,0:T(8,128)(2,1)S(1)}, bf16[2,8,256,256]{3,2,1,0:T(8,128)(2,1)}, u32[]{:S(2)}) copy-start(bf16[2,8,256,256]{3,2,1,0:T(8,128)(2,1)} %copy-done.9) | copy-start | bytes 6291460
  117.6 2.2 copy-start.2
  117.6 2.2 copy-start.13
  195.7 18.8 %copy-start.15 = (f32[2,8,128,128]{3,2,1,0:T(8,128)S(1)}, f32[2,8,128,128]{3,2,1,0:T(8,128)}, u32[]{:S(2)}) copy-start(f32[2,8,128,128]{3,2,1,0:T(8,128)} %copy-done.14) | copy-start | bytes 3145732
  214.4 1.2 copy-start.8
  217.7 1.6 copy-start.11
  (2 other events, 2.0 us)
Sparse Core Ops, SparseCore 0:
  19.3 77.6 all-gather.3
  104.1 91.4 all-gather.5
where the time goes:
time: 231 us; the launch traced here: 229 us
  waiting for transfers between devices  116 us (50%)
  other arithmetic  27.8 us (12%)
  local copies, waits for them, and re-layouts  25.4 us (11%)
  blocking collectives  23.2 us (10%)
  matrix products  21.6 us (9%)
  between operations  14.5 us (6%)
    all_gather x2, waiting for transfers between devices, entering_2(): gathered = jax.tree.map(lambda a: lax.all_gather(a, axis), part)  116 us
    all_gather x1, blocking collectives, entering_2(): gathered = jax.tree.map(lambda a: lax.all_gather(a, axis), part)  23.2 us
    add x15, other arithmetic, join_affine(): later_part[0][:, None, None] * earlier[1] + later_part[1]  17.9 us
    unnamed x53, local copies, waits for them, and re-layouts  10.3 us
  transfers between devices with their start and end apart: 2, of which 2 were waited for; matrix products, arithmetic and copies ran while one was open for 12% of the time, Pallas kernels for 0%

commit v1 on v0

v1 whole, which is shorter than its diff:
```python
import functools

import jax
import jax.numpy as jnp
from jax import lax
from jax.experimental import pallas as pl
from jax.experimental.pallas import tpu as pltpu
from jax.sharding import PartitionSpec as P

BLOCK = 256
DH = 128
EPS = 1e-05
F32 = jnp.float32
BF16 = jnp.bfloat16

NN = (((1,), (0,)), ((), ()))
NT = (((1,), (1,)), ((), ()))
TN = (((0,), (0,)), ((), ()))


def mm(a, b, dims=NN):
    return lax.dot_general(a, b, dims, preferred_element_type=F32)


def whole(shape):
    return pl.BlockSpec(shape, lambda *_: (0,) * len(shape))


def prepare(decay_ref, start_ref, rows_ref, cols_ref):
    tri = (
        lax.broadcasted_iota(jnp.int32, (BLOCK, BLOCK), 0)
        <= lax.broadcasted_iota(jnp.int32, (BLOCK, BLOCK), 1)
    ).astype(F32)
    for b in range(decay_ref.shape[1] // BLOCK):
        at = pl.ds(b * BLOCK, BLOCK)
        starts = jnp.broadcast_to(start_ref[:, at].astype(F32), (8, BLOCK))
        both = jnp.concatenate([decay_ref[:, at], starts], axis=0)
        sums = lax.dot_general(
            both, tri, NN, precision=lax.Precision.HIGHEST, preferred_element_type=F32
        )
        cumul, marks = sums[:8], sums[8:]
        last, last_mark = cumul[:, BLOCK - 1 :], marks[:, BLOCK - 1 :]
        rows_ref[0:8, at] = cumul
        rows_ref[8:16, at] = jnp.where(marks == 0.0, jnp.exp(cumul), 0.0)
        rows_ref[16:24, at] = jnp.where(marks == last_mark, jnp.exp(last - cumul), 0.0)
        rows_ref[24:32, at] = marks
        block = jnp.concatenate([rows_ref[:, at], jnp.zeros((96, BLOCK), F32)], axis=0)
        cols_ref[at, :] = block.T


def put_message(own_ref, send_ref, group, k, j, value, keep):
    body = 2 * k * DH

    @pl.when(group < 2)
    def _():
        at = group * k + j
        own_ref[pl.ds(pl.multiple_of(at * DH, DH), DH), :] = value
        own_ref[pl.ds(body + at, 1), :] = keep

    @pl.when(group >= 2)
    def _():
        at = (group - 2) * k + j
        send_ref[pl.ds(pl.multiple_of(at * DH, DH), DH), :] = value
        send_ref[pl.ds(body + at, 1), :] = keep


def keeps(rows_ref, head):
    enter = rows_ref[pl.ds(8 + head, 1), :]
    k0 = jnp.broadcast_to(enter[:, BLOCK - 1 : BLOCK], (1, DH))
    k1 = jnp.broadcast_to(enter[:, 2 * BLOCK - 1 : 2 * BLOCK], (1, DH))
    return k0, k1


def k1_body(k, info, key_ref, value_ref, decay_ref, start_ref, own_ref, send_ref, loc_ref, rows_ref, cols_ref):
    g = pl.program_id(0)

    @pl.when(g == 0)
    def _():
        prepare(decay_ref, start_ref, rows_ref, cols_ref)
        own_ref[pl.ds(2 * k * DH, 8), :] = jnp.ones((8, DH), F32)
        send_ref[pl.ds(2 * k * DH, 8), :] = jnp.ones((8, DH), F32)

    base = (g ^ info[0]) * k
    for j in range(k):
        head = base + j
        cut = slice(j * DH, (j + 1) * DH)
        leave = rows_ref[pl.ds(16 + head, 1), :]
        terms = []
        for b in range(2):
            rows = slice(b * BLOCK, (b + 1) * BLOCK)
            keys = key_ref[rows, cut].T.astype(F32)
            scaled = (keys * leave[:, rows]).astype(BF16)
            terms.append(mm(scaled, value_ref[rows, cut]))
        k0, k1 = keeps(rows_ref, head)
        loc_ref[j] = terms[0]
        put_message(own_ref, send_ref, g, k, j, k1 * terms[0] + terms[1], k0 * k1)


def k2_body(query_ref, key_ref, value_ref, rows_ref, cols_ref, within_ref, weighted_ref):
    head = pl.program_id(0)
    lane = lax.broadcasted_iota(jnp.int32, (1, DH), 1) == head
    lower = lax.broadcasted_iota(jnp.int32, (BLOCK, BLOCK), 0) >= lax.broadcasted_iota(
        jnp.int32, (BLOCK, BLOCK), 1
    )
    for b in range(2):
        rows = slice(b * BLOCK, (b + 1) * BLOCK)
        grid = grid_of(rows_ref, cols_ref, head, lane, lower, rows)
        scores = mm(query_ref[rows, :], key_ref[rows, :], NT)
        weighted = (scores * grid).astype(BF16)
        weighted_ref[b] = weighted
        within_ref[rows, :] = mm(weighted, value_ref[rows, :])


def column(cols_ref, rows, lane):
    return jnp.sum(jnp.where(lane, cols_ref[rows, :], 0.0), axis=1, keepdims=True)


def grid_of(rows_ref, cols_ref, head, lane, lower, rows):
    cum_row = rows_ref[pl.ds(head, 1), rows]
    mark_row = rows_ref[24:25, rows]
    cum_col = column(cols_ref, rows, lane)
    mark_col = cols_ref[rows, 24:25]
    allowed = lower & (mark_col == mark_row)
    return jnp.where(allowed, jnp.exp(jnp.minimum(cum_col - cum_row, 0.0)), 0.0)


def pick(own_ref, other_ref, g, k, j):
    at = pl.ds(pl.multiple_of(((g & 1) * k + j) * DH, DH), DH)
    return jnp.where(g < 2, own_ref[at, :], other_ref[at, :])


def k3_body(k, info, query_ref, grad_ref, within_ref, loc_ref, rows_ref, cols_ref, mine_ref, other_ref,
            attended_ref, mixgrad_ref, states_ref, own_ref, send_ref, back_ref):
    g = pl.program_id(0)

    @pl.when(g == 0)
    def _():
        own_ref[pl.ds(2 * k * DH, 8), :] = jnp.ones((8, DH), F32)
        send_ref[pl.ds(2 * k * DH, 8), :] = jnp.ones((8, DH), F32)

    base = (g ^ info[0]) * k
    for j in range(k):
        head = base + j
        cut = slice(j * DH, (j + 1) * DH)
        lane = lax.broadcasted_iota(jnp.int32, (1, DH), 1) == 8 + head
        k0, k1 = keeps(rows_ref, head)
        incoming = pick(mine_ref, other_ref, g, k, j)
        states = (incoming, k0 * incoming + loc_ref[j])
        backs = []
        for b in range(2):
            rows = slice(b * BLOCK, (b + 1) * BLOCK)
            low = states[b].astype(BF16)
            states_ref[j, b] = low
            enter = column(cols_ref, rows, lane)
            query = query_ref[rows, cut]
            mixture = within_ref[rows, cut] + mm(query, low) * enter
            inverse = lax.rsqrt(jnp.mean(mixture * mixture, axis=1, keepdims=True) + EPS)
            normed = mixture * inverse
            attended_ref[rows, cut] = normed.astype(BF16)
            wide = grad_ref[rows, cut].astype(F32)
            mixgrad = (inverse * (wide - normed * jnp.mean(wide * normed, axis=1, keepdims=True))).astype(BF16)
            mixgrad_ref[rows, cut] = mixgrad
            scaled = (query.astype(F32) * enter).astype(BF16)
            backs.append(mm(scaled, mixgrad, TN))
        back_ref[j] = backs[1]
        put_message(own_ref, send_ref, g, k, j, k0 * backs[1] + backs[0], k0 * k1)


def k4_body(query_ref, key_ref, value_ref, mixgrad_ref, weighted_ref, states_ref, rows_ref, cols_ref,
            query_grad_ref, key_part_ref, value_part_ref):
    head = pl.program_id(0)
    iota = lax.broadcasted_iota(jnp.int32, (1, DH), 1)
    lower = lax.broadcasted_iota(jnp.int32, (BLOCK, BLOCK), 0) >= lax.broadcasted_iota(
        jnp.int32, (BLOCK, BLOCK), 1
    )
    for b in range(2):
        rows = slice(b * BLOCK, (b + 1) * BLOCK)
        grid = grid_of(rows_ref, cols_ref, head, iota == head, lower, rows)
        mixgrad = mixgrad_ref[rows, :]
        masked = (mm(mixgrad, value_ref[rows, :], NT) * grid).astype(BF16)
        enter = column(cols_ref, rows, iota == 8 + head)
        query_grad_ref[rows, :] = (
            mm(masked, key_ref[rows, :]) + mm(mixgrad, states_ref[0, b], NT) * enter
        ).astype(BF16)
        key_part_ref[rows, :] = mm(masked, query_ref[rows, :], TN)
        value_part_ref[rows, :] = mm(weighted_ref[b], mixgrad, TN)


def k5_body(k, info, key_ref, value_ref, key_part_ref, value_part_ref, back_ref, rows_ref, cols_ref, mine_ref,
            other_ref, key_grad_ref, value_grad_ref):
    g = pl.program_id(0)
    base = (g ^ info[0]) * k
    for j in range(k):
        head = base + j
        cut = slice(j * DH, (j + 1) * DH)
        lane = lax.broadcasted_iota(jnp.int32, (1, DH), 1) == 16 + head
        k0, k1 = keeps(rows_ref, head)
        outgoing = pick(mine_ref, other_ref, g, k, j)
        afters = (k1 * outgoing + back_ref[j], outgoing)
        for b in range(2):
            rows = slice(b * BLOCK, (b + 1) * BLOCK)
            low = afters[b].astype(BF16)
            leave = column(cols_ref, rows, lane)
            key_grad_ref[rows, cut] = (
                key_part_ref[rows, cut] + mm(value_ref[rows, cut], low, NT) * leave
            ).astype(BF16)
            value_grad_ref[rows, cut] = (
                value_part_ref[rows, cut] + mm(key_ref[rows, cut], low) * leave
            ).astype(BF16)


def rows_of(ref, j):
    return ref[j * DH : (j + 1) * DH, :]


def joined(later, got_ref, held_ref, heads, j):
    a_got = got_ref[heads * DH + j : heads * DH + j + 1, :]
    a_held = held_ref[heads * DH + j : heads * DH + j + 1, :]
    state = jnp.where(later, a_held, 1.0) * rows_of(got_ref, j) + jnp.where(later, 1.0, a_got) * rows_of(held_ref, j)
    return state, a_got * a_held


def c1_body(heads, pos, own_ref, got_ref, keep_ref, send_ref):
    later = (pos[0] & 1) == 1
    k = heads // 2
    for out in (keep_ref, send_ref):
        out[k * DH :, :] = jnp.ones((8, DH), F32)
    for j in range(heads):
        out, at = (keep_ref, j) if j < k else (send_ref, j - k)
        state, a = joined(later, got_ref, own_ref, heads, j)
        out[at * DH : (at + 1) * DH, :] = state
        out[k * DH + at : k * DH + at + 1, :] = a


def c2_body(k, pos, own_ref, got_ref, total_ref):
    later = (pos[0] & 2) == 2
    total_ref[k * DH :, :] = jnp.ones((8, DH), F32)
    for j in range(k):
        state, a = joined(later, got_ref, own_ref, k, j)
        total_ref[j * DH : (j + 1) * DH, :] = state
        total_ref[k * DH + j : k * DH + j + 1, :] = a


def before(later, got_ref, prefix_ref, k, j):
    a_got = got_ref[k * DH + j : k * DH + j + 1, :]
    if prefix_ref is None:
        return jnp.where(later, 1.0, 0.0) * rows_of(got_ref, j), jnp.where(later, a_got, 1.0)
    a = prefix_ref[k * DH + j : k * DH + j + 1, :]
    state = jnp.where(later, a, 0.0) * rows_of(got_ref, j) + rows_of(prefix_ref, j)
    return state, jnp.where(later, a * a_got, a)


def cz_body(k, bit, first, pos, *refs):
    if first:
        total_ref, got_ref, new_total_ref, new_prefix_ref = refs
        prefix_ref = None
    else:
        total_ref, got_ref, prefix_ref, new_total_ref, new_prefix_ref = refs
    later = (pos[0] & bit) == bit
    for out in (new_total_ref, new_prefix_ref):
        out[k * DH :, :] = jnp.ones((8, DH), F32)
    for j in range(k):
        at, one = slice(j * DH, (j + 1) * DH), slice(k * DH + j, k * DH + j + 1)
        new_total_ref[at, :], new_total_ref[one, :] = joined(later, got_ref, total_ref, k, j)
        new_prefix_ref[at, :], new_prefix_ref[one, :] = before(later, got_ref, prefix_ref, k, j)


def c3_body(k, bit, first, pos, *refs):
    if first:
        got_ref, own_ref, chip_ref, mine_ref, send_ref = refs
        prefix_ref = None
    else:
        got_ref, prefix_ref, own_ref, chip_ref, mine_ref, send_ref = refs
    later = (pos[0] & bit) == bit
    upper = (pos[0] & 2) == 2
    for j in range(k):
        at, one = slice(j * DH, (j + 1) * DH), slice(k * DH + j, k * DH + j + 1)
        prefix, _ = before(later, got_ref, prefix_ref, k, j)
        chip_a, chip = chip_ref[one, :], rows_of(chip_ref, j)
        own_a, own = own_ref[one, :], rows_of(own_ref, j)
        mine_ref[at, :] = jnp.where(upper, chip_a, 1.0) * prefix + jnp.where(upper, 1.0, 0.0) * chip
        send_ref[at, :] = jnp.where(upper, 1.0, own_a) * prefix + jnp.where(upper, 0.0, 1.0) * own


def c4_body(k, pos, half_ref, got_half_ref, own_ref, got_ref, mine_ref, send_ref):
    later = (pos[0] & 1) == 1
    heads = 2 * k
    for j in range(heads):
        at, one = slice(j * DH, (j + 1) * DH), slice(heads * DH + j, heads * DH + j + 1)
        chip = rows_of(half_ref, j) if j < k else rows_of(got_half_ref, j - k)
        mine_ref[at, :] = jnp.where(later, got_ref[one, :], 1.0) * chip + jnp.where(later, 1.0, 0.0) * rows_of(got_ref, j)
        send_ref[at, :] = jnp.where(later, 1.0, own_ref[one, :]) * chip + jnp.where(later, 0.0, 1.0) * rows_of(own_ref, j)


def small(body, pos, arrays, rows):
    return pl.pallas_call(
        body,
        in_specs=[pl.BlockSpec(memory_space=pltpu.SMEM)] + [pl.BlockSpec(memory_space=pltpu.VMEM)] * len(arrays),
        out_specs=[pl.BlockSpec(memory_space=pltpu.VMEM)] * len(rows),
        out_shape=[jax.ShapeDtypeStruct((r, DH), F32) for r in rows],
    )(pos, *arrays)


def exchange(x, bit, count):
    return lax.ppermute(x, "seq", [(i, i ^ bit) for i in range(count)])


def scan_devices(own, send, pos, k, count):
    full, half = 2 * k * DH + 8, k * DH + 8
    got = exchange(send, 1, count)
    chip, chip_send = small(functools.partial(c1_body, 2 * k), pos, (own, got), (half, half))
    chip_got = exchange(chip_send, 2, count)
    (total,) = small(functools.partial(c2_body, k), pos, (chip, chip_got), (half,))
    prefix = None
    bit = 4
    while bit < count:
        got_total = exchange(total, bit, count)
        held = () if prefix is None else (prefix,)
        if bit * 2 < count:
            total, prefix = small(
                functools.partial(cz_body, k, bit, prefix is None), pos, (total, got_total) + held, (half, half)
            )
        else:
            mine, mine_send = small(
                functools.partial(c3_body, k, bit, prefix is None),
                pos,
                (got_total,) + held + (chip, chip_got),
                (k * DH, k * DH),
            )
        bit *= 2
    mine_got = exchange(mine_send, 2, count)
    state, state_send = small(
        functools.partial(c4_body, k), pos, (mine, mine_got, own, got), (2 * k * DH, 2 * k * DH)
    )
    return state, exchange(state_send, 1, count)


def local(query_rows, key_rows, value_rows, log_decay, run_start, out_grad):
    heads = log_decay.shape[0]
    tokens, width = query_rows.shape
    count = lax.axis_size("seq")
    place = lax.axis_index("seq")
    k = heads // 4
    info = (((place & 1) << 1) | ((place >> 1) & 1)).reshape(1)
    forward_pos = place.reshape(1)
    backward_pos = (count - 1 - place).reshape(1)
    full = 2 * k * DH + 8

    grouped = pl.BlockSpec((tokens, k * DH), lambda g, q: (0, g ^ q[0]))
    grouped_state = pl.BlockSpec((k, DH, DH), lambda g, q: (g ^ q[0], 0, 0))
    grouped_low = pl.BlockSpec((k, 2, DH, DH), lambda g, q: (g ^ q[0], 0, 0, 0))
    by_head = pl.BlockSpec((tokens, DH), lambda h: (0, h))
    rows_spec, cols_spec = whole((32, tokens)), whole((tokens, DH))
    message = jax.ShapeDtypeStruct((full, DH), F32)
    states_f32 = jax.ShapeDtypeStruct((heads, DH, DH), F32)
    flat_bf16 = jax.ShapeDtypeStruct((tokens, width), BF16)
    flat_f32 = jax.ShapeDtypeStruct((tokens, width), F32)

    own, send, loc, rows, cols = pl.pallas_call(
        functools.partial(k1_body, k),
        grid_spec=pltpu.PrefetchScalarGridSpec(
            num_scalar_prefetch=1,
            grid=(4,),
            in_specs=[grouped, grouped, whole((heads, tokens)), whole((1, tokens))],
            out_specs=[whole((full, DH)), whole((full, DH)), grouped_state, rows_spec, cols_spec],
        ),
        out_shape=[
            message,
            message,
            states_f32,
            jax.ShapeDtypeStruct((32, tokens), F32),
            jax.ShapeDtypeStruct((tokens, DH), F32),
        ],
    )(info, key_rows, value_rows, log_decay, run_start.reshape(1, tokens))

    mine, other = scan_devices(own, send, forward_pos, k, count)

    weighted_spec = pl.BlockSpec((None, 2, BLOCK, BLOCK), lambda h: (h, 0, 0, 0))
    within, weighted = pl.pallas_call(
        k2_body,
        grid=(heads,),
        in_specs=[by_head, by_head, by_head, rows_spec, cols_spec],
        out_specs=[by_head, weighted_spec],
        out_shape=[flat_f32, jax.ShapeDtypeStruct((heads, 2, BLOCK, BLOCK), BF16)],
        cost_estimate=pl.CostEstimate(flops=800_000_000, bytes_accessed=8_000_000, transcendentals=1_000_000),
    )(query_rows, key_rows, value_rows, rows, cols)

    attended, mixgrad, states_low, own, send, back = pl.pallas_call(
        functools.partial(k3_body, k),
        grid_spec=pltpu.PrefetchScalarGridSpec(
            num_scalar_prefetch=1,
            grid=(4,),
            in_specs=[grouped, grouped, grouped, grouped_state, rows_spec, cols_spec]
            + [whole((2 * k * DH, DH))] * 2,
            out_specs=[grouped, grouped, grouped_low, whole((full, DH)), whole((full, DH)), grouped_state],
        ),
        out_shape=[
            flat_bf16,
            flat_bf16,
            jax.ShapeDtypeStruct((heads, 2, DH, DH), BF16),
            message,
            message,
            states_f32,
        ],
    )(info, query_rows, out_grad, within, loc, rows, cols, mine, other)

    mine, other = scan_devices(own, send, backward_pos, k, count)

    query_grad, key_part, value_part = pl.pallas_call(
        k4_body,
        grid=(heads,),
        in_specs=[
            by_head,
            by_head,
            by_head,
            by_head,
            weighted_spec,
            pl.BlockSpec((1, 2, DH, DH), lambda h: (h, 0, 0, 0)),
            rows_spec,
            cols_spec,
        ],
        out_specs=[by_head, by_head, by_head],
        out_shape=[flat_bf16, flat_f32, flat_f32],
        cost_estimate=pl.CostEstimate(flops=1_600_000_000, bytes_accessed=12_000_000, transcendentals=1_000_000),
    )(query_rows, key_rows, value_rows, mixgrad, weighted, states_low, rows, cols)

    key_grad, value_grad = pl.pallas_call(
        functools.partial(k5_body, k),
        grid_spec=pltpu.PrefetchScalarGridSpec(
            num_scalar_prefetch=1,
            grid=(4,),
            in_specs=[grouped] * 4 + [grouped_state, rows_spec, cols_spec] + [whole((2 * k * DH, DH))] * 2,
            out_specs=[grouped, grouped],
        ),
        out_shape=[flat_bf16, flat_bf16],
    )(info, key_rows, value_rows, key_part, value_part, back, rows, cols, mine, other)
    return attended, query_grad, key_grad, value_grad


def solution(mesh):
    rows = P(("groups", "seq"), None)
    return jax.shard_map(
        local,
        mesh=mesh,
        in_specs=(rows, rows, rows, P(None, ("groups", "seq")), P(("groups", "seq")), rows),
        out_specs=(rows, rows, rows, rows),
        check_vma=False,
    )
```

time: 231 us -> 119 us (0.52)
  waiting for transfers between devices: 116 us -> 39.8 us
  Pallas kernels: 0 us -> 55.9 us
  other arithmetic: 27.8 us -> 0 us
  blocking collectives: 23.2 us -> 0 us
  matrix products: 21.6 us -> 0 us
  local copies, waits for them, and re-layouts: 25.4 us -> 8.03 us
  starting transfers between devices: 0.08 us -> 14.1 us
  between operations: 14.5 us -> 0.69 us
    all_gather x2 -> x0, waiting for transfers between devices: 116 us -> none  [entering_2(): gathered = jax.tree.map(lambda a: lax.all_gather(a, axis), part)]
    pallas_call x0 -> x15, Pallas kernels: none -> 55.9 us  [the longest x10 18 us: small(): pl.pallas_call(body, in_specs=[pl.BlockSpec(memory_space=pltpu.SMEM)] + [...]
    ppermute x0 -> x12, waiting for transfers between devices: none -> 39.8 us  [exchange(): return lax.ppermute(x, 'seq', [(i, i ^ bit) for i in range(count)])]
    all_gather x1 -> x0, blocking collectives: 23.2 us -> none  [entering_2(): gathered = jax.tree.map(lambda a: lax.all_gather(a, axis), part)]
    dot_general x12 -> x0, matrix products: 21.6 us -> none  [the longest x1 2.92 us: local(): jnp.einsum('nthd,nshd->nhts', queries, keys_all, preferred_element_type=j...]
    add x17 -> x0, other arithmetic: 19.8 us -> none  [the longest x15 17.9 us: join_affine(): later_part[0][:, None, None] * earlier[1] + later_part[1]]
    ppermute x0 -> x12, starting transfers between devices: none -> 14.1 us  [exchange(): return lax.ppermute(x, 'seq', [(i, i ^ bit) for i in range(count)])]
    convert_element_type x5 -> x0, local copies, waits for them, and re-layouts: 8.24 us -> none  [the longest x1 2.52 us: local(): query_grad.astype(jnp.bfloat16).reshape(flat_shape)]
  transfers between devices with their start and end apart: 2 -> 12, of which waited for: 2 -> 10; matrix products, arithmetic and copies ran while one was open for 12% -> 0% of each run, Pallas kernels for 0% -> 16%
where the time goes in v1:
time: 119 us
  Pallas kernels  55.9 us (47%)
  waiting for transfers between devices  39.8 us (33%)
  starting transfers between devices  14.1 us (12%)
  local copies, waits for them, and re-layouts  8.03 us (7%)
    ppermute x12, waiting for transfers between devices, exchange(): return lax.ppermute(x, 'seq', [(i, i ^ bit) for i in range(count)])  39.8 us
    pallas_call x10, Pallas kernels, small(): pl.pallas_call(body, in_specs=[pl.BlockSpec(memory_space=pltpu.SMEM)] + [...  18 us
    ppermute x12, starting transfers between devices, exchange(): return lax.ppermute(x, 'seq', [(i, i ^ bit) for i in range(count)])  14.1 us
    pallas_call x1, Pallas kernels, local(): pl.pallas_call(k4_body, grid=(heads,), in_specs=[by_head, by_head, by_hea...  10.5 us
    pallas_call x1, Pallas kernels, local(): pl.pallas_call(k2_body, grid=(heads,), in_specs=[by_head, by_head, by_hea...  8.3 us
    unnamed x24, local copies, waits for them, and re-layouts  8.03 us
    pallas_call x1, Pallas kernels, local(): pl.pallas_call(functools.partial(k3_body, k), grid_spec=pltpu.PrefetchSca...  8.02 us
    pallas_call x1, Pallas kernels, local(): pl.pallas_call(functools.partial(k5_body, k), grid_spec=pltpu.PrefetchSca...  5.93 us
  transfers between devices with their start and end apart: 12, of which 10 were waited for; matrix products, arithmetic and copies ran while one was open for 0% of the time, Pallas kernels for 16%

profile of v1, /device:TPU:0, one launch (start us, length us, event | category | flops | bytes accessed | tf_op | source)
XLA Modules:
  0.0 118.5 jit_solution(9017784702051138893)
XLA Ops:
  0.6 5.2 %shard_map.93 = (f32[520,128]{1,0:T(8,128)}, f32[520,128]{1,0:T(8,128)}, f32[8,128,128]{2,1,0:T(8,128)}, f32[32,512]{1,0:T(8,128)}, f32[512,128]{1,0:T(8,128)}) custom-call(s32[1]{0:T(128)} %bitcast.info, bf16[512,1024]{1,0:T(8,128)(2,1)} %key_ref.7, bf16[512,1024]{1,0:T(8,128)(2,1)} %value_ref.7, f32[8,512]{1,0:T(8,128)} %decay_ref.1, s32[1,512]{1,0:T(1,128)} %bitcast.4), custom_call_target="tpu_custom_call" | custom-call | tf_op jit(solution)/shard_map/pallas_call | solution.py:359
  8.4 1.7 %shard_map.95 = (f32[264,128]{1,0:T(8,128)}, f32[264,128]{1,0:T(8,128)}) custom-call(s32[1]{0:T(128)} %bitcast.2.pos, f32[520,128]{1,0:T(8,128)} %get-tuple-element.42.own_ref, f32[520,128]{1,0:T(8,128)} %copy-done.1), custom_call_target="tpu_custom_call" | custom-call | tf_op jit(solution)/shard_map/pallas_call | solution.py:296
  10.2 2.9 %collective-permute-start.1 = (f32[264,128]{1,0:T(8,128)}, f32[264,128]{1,0:T(8,128)S(1)}, u32[]{:S(2)}, u32[]{:S(2)}) collective-permute-start(f32[264,128]{1,0:T(8,128)} %get-tuple-element.45), channel_id=1, source_target_pairs={{0,2},{1,3},{2,0},{3,1},{4,6},{5,7},{6,4},{7,5},{8,10},{9,11},{10,... | collective-permute-start | bytes 405512 | tf_op jit(solution)/shard_map/ppermute | solution.py:305
  13.0 4.1 %collective-permute-done.1.got_ref.refs_3_ = f32[264,128]{1,0:T(8,128)S(1)} collective-permute-done((f32[264,128]{1,0:T(8,128)}, f32[264,128]{1,0:T(8,128)S(1)}, u32[]{:S(2)}, u32[]{:S(2)}) %collective-permute-start.1) | collective-permute-done | bytes 135200 | tf_op jit(solution)/shard_map/ppermute | solution.py:305
  19.4 1.8 %collective-permute-start.2 = (f32[264,128]{1,0:T(8,128)}, f32[264,128]{1,0:T(8,128)S(1)}, u32[]{:S(2)}, u32[]{:S(2)}) collective-permute-start(f32[264,128]{1,0:T(8,128)} %shard_map.96.refs_0_), channel_id=1, source_target_pairs={{0,4},{1,5},{2,6},{3,7},{4,0},{5,1},{6,2},{7,3},{8,12},{9,13},{10,... | collective-permute-start | bytes 405512 | tf_op jit(solution)/shard_map/ppermute | solution.py:305
  21.2 3.5 %collective-permute-done.2.refs_1_ = f32[264,128]{1,0:T(8,128)S(1)} collective-permute-done((f32[264,128]{1,0:T(8,128)}, f32[264,128]{1,0:T(8,128)S(1)}, u32[]{:S(2)}, u32[]{:S(2)}) %collective-permute-start.2) | collective-permute-done | bytes 135200 | tf_op jit(solution)/shard_map/ppermute | solution.py:305
  27.1 2.7 %collective-permute-start.3 = (f32[264,128]{1,0:T(8,128)}, f32[264,128]{1,0:T(8,128)S(1)}, u32[]{:S(2)}, u32[]{:S(2)}) collective-permute-start(f32[264,128]{1,0:T(8,128)} %get-tuple-element.46), channel_id=1, source_target_pairs={{0,8},{1,9},{2,10},{3,11},{4,12},{5,13},{6,14},{7,15},{8,0},{9,1},... | collective-permute-start | bytes 405512 | tf_op jit(solution)/shard_map/ppermute | solution.py:305
  29.8 5.5 %collective-permute-done.3.refs_0_ = f32[264,128]{1,0:T(8,128)S(1)} collective-permute-done((f32[264,128]{1,0:T(8,128)}, f32[264,128]{1,0:T(8,128)S(1)}, u32[]{:S(2)}, u32[]{:S(2)}) %collective-permute-start.3) | collective-permute-done | bytes 135200 | tf_op jit(solution)/shard_map/ppermute | solution.py:305
  36.0 1.8 %shard_map.98 = (f32[256,128]{1,0:T(8,128)}, f32[256,128]{1,0:T(8,128)}) custom-call(s32[1]{0:T(128)} %bitcast.2.pos, f32[264,128]{1,0:T(8,128)} %copy-done.6, f32[264,128]{1,0:T(8,128)} %get-tuple-element.47.refs_1_, f32[264,128]{1,0:T(8,128)} %get-tuple-element.44.own_ref.refs_2_, f32[264,128]{1,0:T(8,128)} %copy-done.2), custom_call_target="tpu_custom_call" | custom-call | tf_op jit(solution)/shard_map/pallas_call | solution.py:296
  38.9 4.1 %collective-permute-done.4.got_half_ref = f32[256,128]{1,0:T(8,128)S(1)} collective-permute-done((f32[256,128]{1,0:T(8,128)}, f32[256,128]{1,0:T(8,128)S(1)}, u32[]{:S(2)}, u32[]{:S(2)}) %collective-permute-start.4) | collective-permute-done | bytes 131104 | tf_op jit(solution)/shard_map/ppermute | solution.py:305
  43.7 2.0 %shard_map.99 = (f32[512,128]{1,0:T(8,128)}, f32[512,128]{1,0:T(8,128)}) custom-call(s32[1]{0:T(128)} %bitcast.2.pos, f32[256,128]{1,0:T(8,128)} %get-tuple-element.48.half_ref, f32[256,128]{1,0:T(8,128)} %copy-done.11, f32[520,128]{1,0:T(8,128)} %get-tuple-element.42.own_ref, f32[520,128]{1,0:T(8,128)} %copy-done.1), custom_call_target="tpu_custom_call" | custom-call | tf_op jit(solution)/shard_map/pallas_call | solution.py:296
  45.7 8.3 %shard_map.94 = (f32[512,1024]{1,0:T(8,128)}, bf16[8,2,256,256]{3,2,1,0:T(8,128)(2,1)}) custom-call(bf16[512,1024]{1,0:T(8,128)(2,1)} %query_ref.5, bf16[512,1024]{1,0:T(8,128)(2,1)} %key_ref.7, bf16[512,1024]{1,0:T(8,128)(2,1)} %value_ref.7, f32[32,512]{1,0:T(8,128)} %get-tuple-element.38.rows_ref, f32[512,128]{1,0:T(8,128)} %get-tuple-element.39.cols_ref), custom_call_target="tpu_custom_call" | custom-call | flops 800000000 | bytes 8000000 | tf_op jit(solution)/shard_map/pallas_call | solution.py:379
  54.7 8.0 %shard_map.100 = (bf16[512,1024]{1,0:T(8,128)(2,1)}, bf16[512,1024]{1,0:T(8,128)(2,1)}, bf16[8,2,128,128]{3,2,1,0:T(8,128)(2,1)}, f32[520,128]{1,0:T(8,128)}, f3...) custom-call(s32[1]{0:T(128)} %bitcast.info, bf16[512,1024]{1,0:T(8,128)(2,1)} %query_ref.5, bf16[512,1024]{1,0:T(8,128)(2,1)} %grad_ref.1, ...), custom_call_target="tpu_custom_call" | custom-call | tf_op jit(solution)/shard_map/pallas_call | solution.py:388
  65.4 1.8 %shard_map.102 = (f32[264,128]{1,0:T(8,128)}, f32[264,128]{1,0:T(8,128)}) custom-call(s32[1]{0:T(128)} %bitcast.3.pos, f32[520,128]{1,0:T(8,128)} %get-tuple-element.60.own_ref, f32[520,128]{1,0:T(8,128)} %copy-done), custom_call_target="tpu_custom_call" | custom-call | tf_op jit(solution)/shard_map/pallas_call | solution.py:296
  68.2 5.0 %collective-permute-done.7.got_ref.refs_3_ = f32[264,128]{1,0:T(8,128)S(1)} collective-permute-done((f32[264,128]{1,0:T(8,128)}, f32[264,128]{1,0:T(8,128)S(1)}, u32[]{:S(2)}, u32[]{:S(2)}) %collective-permute-start.7) | collective-permute-done | bytes 135200 | tf_op jit(solution)/shard_map/ppermute | solution.py:305
  75.8 4.9 %collective-permute-done.8.refs_1_ = f32[264,128]{1,0:T(8,128)S(1)} collective-permute-done((f32[264,128]{1,0:T(8,128)}, f32[264,128]{1,0:T(8,128)S(1)}, u32[]{:S(2)}, u32[]{:S(2)}) %collective-permute-start.8) | collective-permute-done | bytes 135200 | tf_op jit(solution)/shard_map/ppermute | solution.py:305
  81.4 1.7 %shard_map.104 = (f32[264,128]{1,0:T(8,128)}, f32[264,128]{1,0:T(8,128)}) custom-call(s32[1]{0:T(128)} %bitcast.3.pos, f32[264,128]{1,0:T(8,128)} %shard_map.103.refs_0_, f32[264,128]{1,0:T(8,128)} %copy-done.9), custom_call_target="tpu_custom_call" | custom-call | tf_op jit(solution)/shard_map/pallas_call | solution.py:296
  83.1 1.9 %collective-permute-start.9 = (f32[264,128]{1,0:T(8,128)}, f32[264,128]{1,0:T(8,128)S(1)}, u32[]{:S(2)}, u32[]{:S(2)}) collective-permute-start(f32[264,128]{1,0:T(8,128)} %get-tuple-element.64), channel_id=1, source_target_pairs={{0,8},{1,9},{2,10},{3,11},{4,12},{5,13},{6,14},{7,15},{8,0},{9,1},... | collective-permute-start | bytes 405512 | tf_op jit(solution)/shard_map/ppermute | solution.py:305
  85.0 6.0 %collective-permute-done.9.refs_0_ = f32[264,128]{1,0:T(8,128)S(1)} collective-permute-done((f32[264,128]{1,0:T(8,128)}, f32[264,128]{1,0:T(8,128)S(1)}, u32[]{:S(2)}, u32[]{:S(2)}) %collective-permute-start.9) | collective-permute-done | bytes 135200 | tf_op jit(solution)/shard_map/ppermute | solution.py:305
  91.6 1.8 %shard_map.105 = (f32[256,128]{1,0:T(8,128)}, f32[256,128]{1,0:T(8,128)}) custom-call(s32[1]{0:T(128)} %bitcast.3.pos, f32[264,128]{1,0:T(8,128)} %copy-done.7, f32[264,128]{1,0:T(8,128)} %get-tuple-element.65.refs_1_, f32[264,128]{1,0:T(8,128)} %get-tuple-element.62.own_ref.refs_2_, f32[264,128]{1,0:T(8,128)} %copy-done.3), custom_call_target="tpu_custom_call" | custom-call | tf_op jit(solution)/shard_map/pallas_call | solution.py:296
  94.8 3.8 %collective-permute-done.10.got_half_ref = f32[256,128]{1,0:T(8,128)S(1)} collective-permute-done((f32[256,128]{1,0:T(8,128)}, f32[256,128]{1,0:T(8,128)S(1)}, u32[]{:S(2)}, u32[]{:S(2)}) %collective-permute-start.10) | collective-permute-done | bytes 131104 | tf_op jit(solution)/shard_map/ppermute | solution.py:305
  99.3 2.1 %shard_map.106 = (f32[512,128]{1,0:T(8,128)}, f32[512,128]{1,0:T(8,128)}) custom-call(s32[1]{0:T(128)} %bitcast.3.pos, f32[256,128]{1,0:T(8,128)} %get-tuple-element.66.half_ref, f32[256,128]{1,0:T(8,128)} %copy-done.10, f32[520,128]{1,0:T(8,128)} %get-tuple-element.60.own_ref, f32[520,128]{1,0:T(8,128)} %copy-done), custom_call_target="tpu_custom_call" | custom-call | tf_op jit(solution)/shard_map/pallas_call | solution.py:296
  101.4 10.5 %shard_map.101 = (bf16[512,1024]{1,0:T(8,128)(2,1)}, f32[512,1024]{1,0:T(8,128)}, f32[512,1024]{1,0:T(8,128)}) custom-call(bf16[512,1024]{1,0:T(8,128)(2,1)} %query_ref.5, bf16[512,1024]{1,0:T(8,128)(2,1)} %key_ref.7, bf16[512,1024]{1,0:T(8,128)(2,1)} %value_ref.7, bf16[512,1024]{1,0:T(8,128)(2,1)} %get-tuple-element.53.mixgrad_ref, ...), custom_call_target="tpu_custom_call" | custom-call | flops 1600000000 | bytes 12000000 | tf_op jit(solution)/shard_map/pallas_call | solution.py:409
  112.6 5.9 %shard_map.107 = (bf16[512,1024]{1,0:T(8,128)(2,1)}, bf16[512,1024]{1,0:T(8,128)(2,1)}) custom-call(s32[1]{0:T(128)} %bitcast.info, bf16[512,1024]{1,0:T(8,128)(2,1)} %key_ref.7, bf16[512,1024]{1,0:T(8,128)(2,1)} %value_ref.7, f32[512,1024]{1,0:T(8,128)} %get-tuple-element.57.key_part_ref, f32[512,1024]{1,0:T(8,128)} %get-tuple-element.58.value_part_ref, ...), custom_call_target="tpu_custom_call" | custom-call | tf_op jit(solution)/shard_map/pallas_call | solution.py:427
  (39 shorter events, 20.7 us)
Async XLA Ops:
  5.8 1.9 %collective-permute-start = (f32[520,128]{1,0:T(8,128)}, f32[520,128]{1,0:T(8,128)S(1)}, u32[]{:S(2)}, u32[]{:S(2)}) collective-permute-start(f32[520,128]{1,0:T(8,128)} %get-tuple-element.43), channel_id=1, source_target_pairs={{0,1},{1,0},{2,3},{3,2},{4,5},{5,4},{6,7},{7,6},{8,9},{9,8},{10,11... | collective-permute-start | bytes 798728 | tf_op jit(solution)/shard_map/ppermute | solution.py:305
  7.7 0.7 copy-start.1
  10.2 7.0 %collective-permute-start.1 = (f32[264,128]{1,0:T(8,128)}, f32[264,128]{1,0:T(8,128)S(1)}, u32[]{:S(2)}, u32[]{:S(2)}) collective-permute-start(f32[264,128]{1,0:T(8,128)} %get-tuple-element.45), channel_id=1, source_target_pairs={{0,2},{1,3},{2,0},{3,1},{4,6},{5,7},{6,4},{7,5},{8,10},{9,11},{10,... | collective-permute-start | bytes 405512 | tf_op jit(solution)/shard_map/ppermute | solution.py:305
  17.1 0.7 copy-start.2
  19.4 5.3 %collective-permute-start.2 = (f32[264,128]{1,0:T(8,128)}, f32[264,128]{1,0:T(8,128)S(1)}, u32[]{:S(2)}, u32[]{:S(2)}) collective-permute-start(f32[264,128]{1,0:T(8,128)} %shard_map.96.refs_0_), channel_id=1, source_target_pairs={{0,4},{1,5},{2,6},{3,7},{4,0},{5,1},{6,2},{7,3},{8,12},{9,13},{10,... | collective-permute-start | bytes 405512 | tf_op jit(solution)/shard_map/ppermute | solution.py:305
  24.8 0.7 copy-start.8
  27.1 8.2 %collective-permute-start.3 = (f32[264,128]{1,0:T(8,128)}, f32[264,128]{1,0:T(8,128)S(1)}, u32[]{:S(2)}, u32[]{:S(2)}) collective-permute-start(f32[264,128]{1,0:T(8,128)} %get-tuple-element.46), channel_id=1, source_target_pairs={{0,8},{1,9},{2,10},{3,11},{4,12},{5,13},{6,14},{7,15},{8,0},{9,1},... | collective-permute-start | bytes 405512 | tf_op jit(solution)/shard_map/ppermute | solution.py:305
  35.4 0.7 copy-start.6
  37.8 5.2 %collective-permute-start.4 = (f32[256,128]{1,0:T(8,128)}, f32[256,128]{1,0:T(8,128)S(1)}, u32[]{:S(2)}, u32[]{:S(2)}) collective-permute-start(f32[256,128]{1,0:T(8,128)} %get-tuple-element.49), channel_id=1, source_target_pairs={{0,2},{1,3},{2,0},{3,1},{4,6},{5,7},{6,4},{7,5},{8,10},{9,11},{10,... | collective-permute-start | bytes 393224 | tf_op jit(solution)/shard_map/ppermute | solution.py:305
  43.0 0.7 copy-start.11
  45.7 8.3 %collective-permute-start.5 = (f32[512,128]{1,0:T(8,128)}, f32[512,128]{1,0:T(8,128)S(1)}, u32[]{:S(2)}, u32[]{:S(2)}) collective-permute-start(f32[512,128]{1,0:T(8,128)} %get-tuple-element.51), channel_id=1, source_target_pairs={{0,1},{1,0},{2,3},{3,2},{4,5},{5,4},{6,7},{7,6},{8,9},{9,8},{10,11... | collective-permute-start | bytes 786440 | tf_op jit(solution)/shard_map/ppermute | solution.py:305
  54.0 0.7 copy-start.5
  62.7 1.9 %collective-permute-start.6 = (f32[520,128]{1,0:T(8,128)}, f32[520,128]{1,0:T(8,128)S(1)}, u32[]{:S(2)}, u32[]{:S(2)}) collective-permute-start(f32[520,128]{1,0:T(8,128)} %get-tuple-element.61), channel_id=1, source_target_pairs={{0,1},{1,0},{2,3},{3,2},{4,5},{5,4},{6,7},{7,6},{8,9},{9,8},{10,11... | collective-permute-start | bytes 798728 | tf_op jit(solution)/shard_map/ppermute | solution.py:305
  64.6 0.7 copy-start
  67.1 6.1 %collective-permute-start.7 = (f32[264,128]{1,0:T(8,128)}, f32[264,128]{1,0:T(8,128)S(1)}, u32[]{:S(2)}, u32[]{:S(2)}) collective-permute-start(f32[264,128]{1,0:T(8,128)} %get-tuple-element.63), channel_id=1, source_target_pairs={{0,2},{1,3},{2,0},{3,1},{4,6},{5,7},{6,4},{7,5},{8,10},{9,11},{10,... | collective-permute-start | bytes 405512 | tf_op jit(solution)/shard_map/ppermute | solution.py:305
  73.2 0.6 copy-start.3
  75.5 5.3 %collective-permute-start.8 = (f32[264,128]{1,0:T(8,128)}, f32[264,128]{1,0:T(8,128)S(1)}, u32[]{:S(2)}, u32[]{:S(2)}) collective-permute-start(f32[264,128]{1,0:T(8,128)} %shard_map.103.refs_0_), channel_id=1, source_target_pairs={{0,4},{1,5},{2,6},{3,7},{4,0},{5,1},{6,2},{7,3},{8,12},{9,13},{10,... | collective-permute-start | bytes 405512 | tf_op jit(solution)/shard_map/ppermute | solution.py:305
  80.7 0.7 copy-start.9
  83.1 7.9 %collective-permute-start.9 = (f32[264,128]{1,0:T(8,128)}, f32[264,128]{1,0:T(8,128)S(1)}, u32[]{:S(2)}, u32[]{:S(2)}) collective-permute-start(f32[264,128]{1,0:T(8,128)} %get-tuple-element.64), channel_id=1, source_target_pairs={{0,8},{1,9},{2,10},{3,11},{4,12},{5,13},{6,14},{7,15},{8,0},{9,1},... | collective-permute-start | bytes 405512 | tf_op jit(solution)/shard_map/ppermute | solution.py:305
  91.0 0.6 copy-start.7
  93.5 5.2 %collective-permute-start.10 = (f32[256,128]{1,0:T(8,128)}, f32[256,128]{1,0:T(8,128)S(1)}, u32[]{:S(2)}, u32[]{:S(2)}) collective-permute-start(f32[256,128]{1,0:T(8,128)} %get-tuple-element.67), channel_id=1, source_target_pairs={{0,2},{1,3},{2,0},{3,1},{4,6},{5,7},{6,4},{7,5},{8,10},{9,11},{10,... | collective-permute-start | bytes 393224 | tf_op jit(solution)/shard_map/ppermute | solution.py:305
  98.6 0.7 copy-start.10
  101.4 10.5 %collective-permute-start.11 = (f32[512,128]{1,0:T(8,128)}, f32[512,128]{1,0:T(8,128)S(1)}, u32[]{:S(2)}, u32[]{:S(2)}) collective-permute-start(f32[512,128]{1,0:T(8,128)} %get-tuple-element.69), channel_id=1, source_target_pairs={{0,1},{1,0},{2,3},{3,2},{4,5},{5,4},{6,7},{7,6},{8,9},{9,8},{10,11... | collective-permute-start | bytes 786440 | tf_op jit(solution)/shard_map/ppermute | solution.py:305
  111.9 0.7 copy-start.4

commit v2 on v0

v2 whole, which is shorter than its diff:
```python
import functools

import jax
import jax.numpy as jnp
from jax import lax
from jax.experimental import pallas as pl
from jax.experimental.pallas import tpu as pltpu
from jax.sharding import PartitionSpec as P

BLOCK = 256
HALF = 128
DH = 128
EPS = 1e-05
FAR = -1e30
GROUPS = 4
CHUNKS = 1
PIECES = 4
F32 = jnp.float32
BF16 = jnp.bfloat16

NN = (((1,), (0,)), ((), ()))
NT = (((1,), (1,)), ((), ()))
TN = (((0,), (0,)), ((), ()))


def mm(a, b, dims=NN):
    return lax.dot_general(a, b, dims, preferred_element_type=F32)


def cut(j):
    return slice(j * DH, (j + 1) * DH)


def block(b):
    return slice(b * BLOCK, (b + 1) * BLOCK)


SMEM = pl.BlockSpec(memory_space=pltpu.SMEM)
VMEM = pl.BlockSpec(memory_space=pltpu.VMEM)
ANY = pl.BlockSpec(memory_space=pl.ANY)


def run(body, scalar, inside, outs, outside=(), after=(), aliases=None, scratch=(), megabytes=8):
    taken = len(inside) + len(outside)

    def kernel(scalar_ref, *refs):
        body(scalar_ref, *refs[:taken], *refs[taken + len(after) :])

    shapes = [o if isinstance(o, jax.ShapeDtypeStruct) else pltpu.VMEM(*o) for o in outs]
    return pl.pallas_call(
        kernel,
        in_specs=[SMEM] + [VMEM] * len(inside) + [ANY] * (len(outside) + len(after)),
        out_specs=[ANY if isinstance(o, jax.ShapeDtypeStruct) else VMEM for o in outs],
        out_shape=shapes,
        input_output_aliases={1 + len(inside) + i: o for i, o in (aliases or {}).items()},
        scratch_shapes=list(scratch),
        compiler_params=pltpu.CompilerParams(vmem_limit_bytes=megabytes << 20),
    )(scalar, *[pltpu.with_memory_space_constraint(a, pltpu.VMEM) for a in inside], *outside, *after)


def prepare(decay_ref, start_ref, rows_ref, cols_ref):
    tri = (
        lax.broadcasted_iota(jnp.int32, (BLOCK, BLOCK), 0) <= lax.broadcasted_iota(jnp.int32, (BLOCK, BLOCK), 1)
    ).astype(F32)
    for b in range(decay_ref.shape[1] // BLOCK):
        at = block(b)
        starts = jnp.broadcast_to(start_ref[:, at].astype(F32), (8, BLOCK))
        both = jnp.concatenate([decay_ref[:, at], starts], axis=0)
        sums = lax.dot_general(both, tri, NN, precision=lax.Precision.HIGHEST, preferred_element_type=F32)
        cumul, marks = sums[:8], sums[8:]
        last, last_mark = cumul[:, BLOCK - 1 :], marks[:, BLOCK - 1 :]
        entering = jnp.where(marks == 0.0, jnp.exp(cumul), 0.0)
        leaving = jnp.where(marks == last_mark, jnp.exp(last - cumul), 0.0)
        stack = jnp.concatenate([cumul, entering, leaving, marks], axis=0)
        rows_ref[:, at] = stack
        cols_ref[at, :] = jnp.concatenate([stack, jnp.zeros((96, BLOCK), F32)], axis=0).T


def keeps(rows_ref, head):
    enter = rows_ref[8 + head : 9 + head, :]
    k0 = jnp.broadcast_to(enter[:, BLOCK - 1 : BLOCK], (1, DH))
    k1 = jnp.broadcast_to(enter[:, 2 * BLOCK - 1 : 2 * BLOCK], (1, DH))
    return k0, k1


def send_out(info, k, terms_ref, keep_ref, own_ref, send_ref):
    for out, first in ((own_ref, 0), (send_ref, 2 * k)):
        for r in range(2 * k):
            group, j = (first + r) // k, (first + r) % k
            head = (group ^ info[0]) * k + j
            out[cut(r), :] = terms_ref[head]
            out[pl.ds(2 * k * DH + r, 1), :] = keep_ref[pl.ds(head, 1), :]
        rest = 8 - 2 * k
        out[2 * k * DH + 2 * k :, :] = jnp.ones((rest, DH), F32)


def k1_body(k, head0, info, decay_ref, start_ref, key_hbm, value_hbm,
            own_ref, send_ref, loc_ref, rows_ref, cols_ref, key_ref, value_ref, terms_ref, keep_ref, sems):
    heads = GROUPS * k
    copies = []
    for j in range(heads):
        pair = []
        for i, (source, target) in enumerate(((key_hbm, key_ref), (value_hbm, value_ref))):
            copy = pltpu.make_async_copy(source.at[:, cut(head0 + j)], target.at[:, cut(j)], sems.at[2 * j + i])
            copy.start()
            pair.append(copy)
        copies.append(pair)
    prepare(decay_ref, start_ref, rows_ref, cols_ref)
    for j in range(heads):
        for copy in copies[j]:
            copy.wait()
        head = head0 + j
        leave = rows_ref[16 + head : 17 + head, :]
        terms = []
        for b in range(2):
            keys = key_ref[block(b), cut(j)].T.astype(F32)
            scaled = (keys * leave[:, block(b)]).astype(BF16)
            terms.append(mm(scaled, value_ref[block(b), cut(j)]))
        k0, k1 = keeps(rows_ref, head)
        loc_ref[j] = terms[0]
        terms_ref[j] = k1 * terms[0] + terms[1]
        keep_ref[j : j + 1, :] = k0 * k1
    send_out(info, k, terms_ref, keep_ref, own_ref, send_ref)


def make_bias(cols_ref, rows_ref, bias_ref):
    lower = lax.broadcasted_iota(jnp.int32, (BLOCK, BLOCK), 0) >= lax.broadcasted_iota(jnp.int32, (BLOCK, BLOCK), 1)
    for b in range(2):
        same = cols_ref[block(b), 24:25] == rows_ref[24:25, block(b)]
        bias_ref[b] = jnp.where(lower & same, 0.0, FAR)


def k2_body(first, head0, base, count, info, query_ref, key_ref, value_ref, rows_ref, cols_ref, *refs):
    if first:
        within_ref, weighted_ref, grid_ref, scaled_ref, bias_ref = refs
        make_bias(cols_ref, rows_ref, bias_ref)
    else:
        bias_ref, within_ref, weighted_ref, grid_ref, scaled_ref = refs
    for j in range(count):
        head = head0 + j
        inner = head - base
        for b in range(2):
            at = block(b)
            query = query_ref[at, cut(head)]
            scores = mm(query, key_ref[at, cut(inner)], NT)
            cum_row = rows_ref[head : head + 1, at]
            for part, width in ((0, HALF), (1, BLOCK)):
                up = slice(part * HALF, (part + 1) * HALF)
                cum_col = cols_ref[b * BLOCK + part * HALF : b * BLOCK + (part + 1) * HALF, head : head + 1]
                grid = jnp.exp(jnp.minimum(cum_col - cum_row[:, :width], bias_ref[b, up, :width]))
                grid_ref[j, b, up, :width] = grid
                weighted_ref[j, b, up, :width] = (scores[up, :width] * grid).astype(BF16)
            grid_ref[j, b, :HALF, HALF:] = jnp.zeros((HALF, HALF), F32)
            weighted_ref[j, b, :HALF, HALF:] = jnp.zeros((HALF, HALF), BF16)
            within_ref[at, cut(j)] = mm(weighted_ref[j, b], value_ref[at, cut(inner)])
            enter = rows_ref[8 + head : 9 + head, at]
            scaled_ref[j, b] = (query.T.astype(F32) * enter).astype(BF16)


def k3_body(k, head0, pieces, per, has_alias, info, query_ref, grad_ref, loc_ref, rows_ref, cols_ref, mine_ref,
            other_ref, *refs):
    withins, scaleds = refs[:pieces], refs[pieces : 2 * pieces]
    refs = refs[2 * pieces + has_alias :]
    own_ref, send_ref, mixgrad_ref, states_ref, back_ref, attended_hbm = refs[:6]
    attended_ref, terms_ref, keep_ref, state_ref, sems = refs[6:]
    heads = GROUPS * k
    for r in range(heads):
        group, j = r // k, r % k
        source = mine_ref if r < 2 * k else other_ref
        state_ref[(group ^ info[0]) * k + j] = source[cut(r % (2 * k)), :]
    copies = []
    for j in range(heads):
        head = head0 + j
        within_ref, scaled_ref, i = withins[j // per], scaleds[j // per], j % per
        k0, k1 = keeps(rows_ref, head)
        incoming = state_ref[j]
        states = (incoming, k0 * incoming + loc_ref[j])
        backs = []
        for b in range(2):
            at = block(b)
            low = states[b].astype(BF16)
            states_ref[j, b] = low
            enter = cols_ref[at, 8 + head : 9 + head]
            mixture = within_ref[at, cut(i)] + mm(query_ref[at, cut(head)], low) * enter
            inverse = lax.rsqrt(jnp.mean(mixture * mixture, axis=1, keepdims=True) + EPS)
            normed = mixture * inverse
            attended_ref[at, cut(j)] = normed.astype(BF16)
            wide = grad_ref[at, cut(head)].astype(F32)
            mixgrad = (inverse * (wide - normed * jnp.mean(wide * normed, axis=1, keepdims=True))).astype(BF16)
            mixgrad_ref[at, cut(j)] = mixgrad
            backs.append(mm(scaled_ref[i, b], mixgrad))
        copy = pltpu.make_async_copy(attended_ref.at[:, cut(j)], attended_hbm.at[:, cut(head)], sems.at[j])
        copy.start()
        copies.append(copy)
        back_ref[j] = backs[1]
        terms_ref[j] = k0 * backs[1] + backs[0]
        keep_ref[j : j + 1, :] = k0 * k1
    send_out(info, k, terms_ref, keep_ref, own_ref, send_ref)
    for copy in copies:
        copy.wait()


def k4_body(head0, base, count, has_alias, info, query_ref, key_ref, value_ref, mixgrad_ref, weighted_ref, grid_ref,
            states_ref, cols_ref, *refs):
    key_part_ref, value_part_ref, query_grad_hbm, query_grad_ref, sems = refs[has_alias:]
    copies = []
    for j in range(count):
        head = head0 + j
        inner = head - base
        for b in range(2):
            at = block(b)
            mixgrad = mixgrad_ref[at, cut(inner)]
            masked = (mm(mixgrad, value_ref[at, cut(inner)], NT) * grid_ref[j, b]).astype(BF16)
            enter = cols_ref[at, 8 + head : 9 + head]
            query_grad_ref[at, cut(j)] = (
                mm(masked, key_ref[at, cut(inner)]) + mm(mixgrad, states_ref[inner, b], NT) * enter
            ).astype(BF16)
            key_part_ref[at, cut(j)] = mm(masked, query_ref[at, cut(head)], TN)
            value_part_ref[at, cut(j)] = mm(weighted_ref[j, b], mixgrad, TN)
        copy = pltpu.make_async_copy(query_grad_ref.at[:, cut(j)], query_grad_hbm.at[:, cut(head)], sems.at[j])
        copy.start()
        copies.append(copy)
    for copy in copies:
        copy.wait()


def k5_body(k, head0, pieces, per, has_alias, info, key_ref, value_ref, back_ref, rows_ref, cols_ref, mine_ref,
            other_ref, *refs):
    key_parts, value_parts = refs[:pieces], refs[pieces : 2 * pieces]
    refs = refs[2 * pieces + 2 * has_alias :]
    key_grad_hbm, value_grad_hbm, key_grad_ref, value_grad_ref, state_ref, sems = refs
    heads = GROUPS * k
    for r in range(heads):
        group, j = r // k, r % k
        source = mine_ref if r < 2 * k else other_ref
        state_ref[(group ^ info[0]) * k + j] = source[cut(r % (2 * k)), :]
    copies = []
    for j in range(heads):
        head = head0 + j
        i = j % per
        k0, k1 = keeps(rows_ref, head)
        outgoing = state_ref[j]
        afters = (k1 * outgoing + back_ref[j], outgoing)
        for b in range(2):
            at = block(b)
            low = afters[b].astype(BF16)
            leave = cols_ref[at, 16 + head : 17 + head]
            key_grad_ref[at, cut(j)] = (
                key_parts[j // per][at, cut(i)] + mm(value_ref[at, cut(j)], low, NT) * leave
            ).astype(BF16)
            value_grad_ref[at, cut(j)] = (
                value_parts[j // per][at, cut(i)] + mm(key_ref[at, cut(j)], low) * leave
            ).astype(BF16)
        for n, (source, target) in enumerate(((key_grad_ref, key_grad_hbm), (value_grad_ref, value_grad_hbm))):
            copy = pltpu.make_async_copy(source.at[:, cut(j)], target.at[:, cut(head)], sems.at[2 * j + n])
            copy.start()
            copies.append(copy)
    for copy in copies:
        copy.wait()


def joined(later, got_ref, held_ref, heads, j):
    one = slice(heads * DH + j, heads * DH + j + 1)
    a_got, a_held = got_ref[one, :], held_ref[one, :]
    state = jnp.where(later, a_held, 1.0) * got_ref[cut(j), :] + jnp.where(later, 1.0, a_got) * held_ref[cut(j), :]
    return state, a_got * a_held


def before(later, got_ref, prefix_ref, k, j):
    one = slice(k * DH + j, k * DH + j + 1)
    a_got = got_ref[one, :]
    if prefix_ref is None:
        return jnp.where(later, 1.0, 0.0) * got_ref[cut(j), :], jnp.where(later, a_got, 1.0)
    a = prefix_ref[one, :]
    state = jnp.where(later, a, 0.0) * got_ref[cut(j), :] + prefix_ref[cut(j), :]
    return state, jnp.where(later, a * a_got, a)


def put(out, heads, j, value):
    out[cut(j), :], out[heads * DH + j : heads * DH + j + 1, :] = value


def c1_body(k, pos, own_ref, got_ref, keep_ref, send_ref):
    later = (pos[0] & 1) == 1
    for out in (keep_ref, send_ref):
        out[k * DH :, :] = jnp.ones((8, DH), F32)
    for j in range(2 * k):
        put(keep_ref if j < k else send_ref, k, j % k, joined(later, got_ref, own_ref, 2 * k, j))


def c2_body(k, pos, own_ref, got_ref, total_ref):
    later = (pos[0] & 2) == 2
    total_ref[k * DH :, :] = jnp.ones((8, DH), F32)
    for j in range(k):
        put(total_ref, k, j, joined(later, got_ref, own_ref, k, j))


def cz_body(k, bit, first, pos, *refs):
    total_ref, got_ref = refs[:2]
    prefix_ref = None if first else refs[2]
    new_total_ref, new_prefix_ref = refs[-2:]
    later = (pos[0] & bit) == bit
    for out in (new_total_ref, new_prefix_ref):
        out[k * DH :, :] = jnp.ones((8, DH), F32)
    for j in range(k):
        put(new_total_ref, k, j, joined(later, got_ref, total_ref, k, j))
        put(new_prefix_ref, k, j, before(later, got_ref, prefix_ref, k, j))


def c3_body(k, bit, first, pos, *refs):
    got_ref = refs[0]
    prefix_ref = None if first else refs[1]
    own_ref, chip_ref, mine_ref, send_ref = refs[-4:]
    later = (pos[0] & bit) == bit
    upper = (pos[0] & 2) == 2
    for j in range(k):
        at, one = cut(j), slice(k * DH + j, k * DH + j + 1)
        prefix, _ = before(later, got_ref, prefix_ref, k, j)
        mine_ref[at, :] = jnp.where(upper, chip_ref[one, :], 1.0) * prefix + jnp.where(upper, 1.0, 0.0) * chip_ref[at, :]
        send_ref[at, :] = jnp.where(upper, 1.0, own_ref[one, :]) * prefix + jnp.where(upper, 0.0, 1.0) * own_ref[at, :]


def c4_body(k, pos, half_ref, got_half_ref, own_ref, got_ref, mine_ref, send_ref):
    later = (pos[0] & 1) == 1
    for j in range(2 * k):
        at, one = cut(j), slice(2 * k * DH + j, 2 * k * DH + j + 1)
        chip = half_ref[cut(j), :] if j < k else got_half_ref[cut(j - k), :]
        mine_ref[at, :] = jnp.where(later, got_ref[one, :], 1.0) * chip + jnp.where(later, 1.0, 0.0) * got_ref[at, :]
        send_ref[at, :] = jnp.where(later, 1.0, own_ref[one, :]) * chip + jnp.where(later, 0.0, 1.0) * own_ref[at, :]


def exchange(x, bit, count):
    return lax.ppermute(x, "seq", [(i, i ^ bit) for i in range(count)])


def scan_devices(own, send, pos, k, count, fillers):
    half = ((k * DH + 8, DH), F32)
    got = exchange(send, 1, count)
    yield send
    chip, chip_send = run(functools.partial(c1_body, k), pos, (own, got), (half, half))
    chip_got = exchange(chip_send, 2, count)
    filled = yield chip_send
    (total,) = run(functools.partial(c2_body, k), pos, (chip, chip_got), (half,), after=filled)
    prefix = ()
    bit = 4
    while bit < count:
        got_total = exchange(total, bit, count)
        filled = yield total
        if bit * 2 < count:
            body = functools.partial(cz_body, k, bit, not prefix)
            total, *prefix = run(body, pos, (total, got_total, *prefix), (half, half), after=filled)
        else:
            body = functools.partial(c3_body, k, bit, not prefix)
            outs = (((k * DH, DH), F32),) * 2
            mine, mine_send = run(body, pos, (got_total, *prefix, chip, chip_got), outs, after=filled)
        bit *= 2
    mine_got = exchange(mine_send, 2, count)
    filled = yield mine_send
    outs = (((2 * k * DH, DH), F32),) * 2
    state, state_send = run(
        functools.partial(c4_body, k), pos, (mine, mine_got, own, got), outs, after=filled
    )
    yield state, exchange(state_send, 1, count)


def drive(scan, fillers):
    out = next(scan)
    fillers = list(fillers)
    out = next(scan)
    while not isinstance(out, tuple):
        done = ()
        if fillers:
            done = tuple(fillers.pop(0)(out))
        out = scan.send(done)
    for filler in fillers:
        filler(None)
    return out


def local(query_rows, key_rows, value_rows, log_decay, run_start, out_grad):
    all_heads = log_decay.shape[0]
    tokens, width = query_rows.shape
    count = lax.axis_size("seq")
    place = lax.axis_index("seq")
    info = (((place & 1) << 1) | ((place >> 1) & 1)).reshape(1)
    forward_pos = place.reshape(1)
    backward_pos = (count - 1 - place).reshape(1)
    k = all_heads // GROUPS
    heads = all_heads
    per = heads // PIECES
    dma = pltpu.SemaphoreType.DMA
    message = ((2 * k * DH + 8, DH), F32)
    states = ((heads, DH, DH), F32)
    flat = jax.ShapeDtypeStruct((tokens, width), BF16)
    chunk_bf16 = ((tokens, heads * DH), BF16)
    piece_f32 = ((tokens, per * DH), F32)
    scratch_terms = (pltpu.VMEM((heads, DH, DH), F32), pltpu.VMEM((8, DH), F32))

    own, send, loc, rows, cols, keys, values = run(
        functools.partial(k1_body, k, 0),
        info,
        (log_decay, run_start.reshape(1, tokens)),
        (message, message, states, ((32, tokens), F32), ((tokens, DH), F32), chunk_bf16, chunk_bf16),
        outside=(key_rows, value_rows),
        scratch=scratch_terms + (dma((2 * heads,)),),
    )

    forward = []

    def k2(p, sent):
        grids = ((per, 2, BLOCK, BLOCK), F32)
        outs = (piece_f32, ((per, 2, BLOCK, BLOCK), BF16), grids, ((per, 2, DH, BLOCK), BF16))
        inputs = (query_rows, keys, values, rows, cols)
        if p == 0:
            outs += (((2, BLOCK, BLOCK), F32),)
        else:
            inputs += (forward[0][4],)
        result = run(
            functools.partial(k2_body, p == 0, p * per, 0, per),
            info, inputs, outs, after=() if sent is None else (sent,),
        )
        forward.append(result)
        return result[:1]

    mine, other = drive(
        scan_devices(own, send, forward_pos, k, count, None), [functools.partial(k2, p) for p in range(PIECES)]
    )
    own, send, mixgrad, states_low, back, attended = run(
        functools.partial(k3_body, k, 0, PIECES, per, 0),
        info,
        (query_rows, out_grad, loc, rows, cols, mine, other, *[f[0] for f in forward], *[f[3] for f in forward]),
        (message, message, chunk_bf16, ((heads, 2, DH, DH), BF16), states, flat),
        scratch=(pltpu.VMEM((tokens, heads * DH), BF16),) + scratch_terms
        + (pltpu.VMEM((heads, DH, DH), F32), dma((heads,))),
    )

    backward = []

    def k4(p, sent):
        has_alias = int(bool(backward))
        result = run(
            functools.partial(k4_body, p * per, 0, per, has_alias),
            info,
            (query_rows, keys, values, mixgrad, forward[p][1], forward[p][2], states_low, cols),
            (piece_f32, piece_f32, flat),
            outside=(backward[-1][2],) if backward else (),
            after=() if sent is None else (sent,),
            aliases={0: 2} if backward else None,
            scratch=(pltpu.VMEM((tokens, per * DH), BF16), dma((per,))),
        )
        backward.append(result)
        return result[:1]

    mine, other = drive(
        scan_devices(own, send, backward_pos, k, count, None), [functools.partial(k4, p) for p in range(PIECES)]
    )
    key_grad, value_grad = run(
        functools.partial(k5_body, k, 0, PIECES, per, 0),
        info,
        (keys, values, back, rows, cols, mine, other, *[b[0] for b in backward], *[b[1] for b in backward]),
        (flat, flat),
        scratch=(pltpu.VMEM((tokens, heads * DH), BF16),) * 2
        + (pltpu.VMEM((heads, DH, DH), F32), dma((2 * heads,))),
    )
    return attended, backward[-1][2], key_grad, value_grad


def solution(mesh):
    rows = P(("groups", "seq"), None)
    return jax.shard_map(
        local,
        mesh=mesh,
        in_specs=(rows, rows, rows, P(None, ("groups", "seq")), P(("groups", "seq")), rows),
        out_specs=(rows, rows, rows, rows),
        check_vma=False,
    )
```

time: 231 us -> 79.2 us (0.34)
  waiting for transfers between devices: 116 us -> 22.2 us
  other arithmetic: 27.8 us -> 0 us
  Pallas kernels: 0 us -> 24.2 us
  blocking collectives: 23.2 us -> 0 us
  matrix products: 21.6 us -> 0 us
  starting transfers between devices: 0.08 us -> 14.8 us
  between operations: 14.5 us -> 1.07 us
  local copies, waits for them, and re-layouts: 25.4 us -> 16.5 us
    all_gather x2 -> x0, waiting for transfers between devices: 116 us -> none  [entering_2(): gathered = jax.tree.map(lambda a: lax.all_gather(a, axis), part)]
    pallas_call x0 -> x21, Pallas kernels: none -> 24.2 us  [run(): pl.pallas_call(kernel, in_specs=[SMEM] + [VMEM] * len(inside) + [ANY] * (...]
    all_gather x1 -> x0, blocking collectives: 23.2 us -> none  [entering_2(): gathered = jax.tree.map(lambda a: lax.all_gather(a, axis), part)]
    ppermute x0 -> x12, waiting for transfers between devices: none -> 22.2 us  [exchange(): return lax.ppermute(x, 'seq', [(i, i ^ bit) for i in range(count)])]
    dot_general x12 -> x0, matrix products: 21.6 us -> none  [the longest x1 2.92 us: local(): jnp.einsum('nthd,nshd->nhts', queries, keys_all, preferred_element_type=j...]
    add x17 -> x0, other arithmetic: 19.8 us -> none  [the longest x15 17.9 us: join_affine(): later_part[0][:, None, None] * earlier[1] + later_part[1]]
    ppermute x0 -> x12, starting transfers between devices: none -> 14.8 us  [exchange(): return lax.ppermute(x, 'seq', [(i, i ^ bit) for i in range(count)])]
    convert_element_type x5 -> x0, local copies, waits for them, and re-layouts: 8.24 us -> none  [the longest x1 2.52 us: local(): query_grad.astype(jnp.bfloat16).reshape(flat_shape)]
  transfers between devices with their start and end apart: 2 -> 12, of which waited for: 2 -> 11; matrix products, arithmetic and copies ran while one was open for 12% -> 0% of each run, Pallas kernels for 0% -> 14%
where the time goes in v2:
time: 79.2 us; the launch traced here: 78.7 us
  Pallas kernels  24.2 us (31%)
  waiting for transfers between devices  22.2 us (28%)
  local copies, waits for them, and re-layouts  16.5 us (21%)
  starting transfers between devices  14.8 us (19%)
  between operations  1.07 us (1%)
    pallas_call x21, Pallas kernels, run(): pl.pallas_call(kernel, in_specs=[SMEM] + [VMEM] * len(inside) + [ANY] * (...  24.2 us
    ppermute x12, waiting for transfers between devices, exchange(): return lax.ppermute(x, 'seq', [(i, i ^ bit) for i in range(count)])  22.2 us
    unnamed x62, local copies, waits for them, and re-layouts  16.5 us
    ppermute x12, starting transfers between devices, exchange(): return lax.ppermute(x, 'seq', [(i, i ^ bit) for i in range(count)])  14.8 us
  transfers between devices with their start and end apart: 12, of which 11 were waited for; matrix products, arithmetic and copies ran while one was open for 0% of the time, Pallas kernels for 14%

profile of v2, /device:TPU:0, one launch (start us, length us, event | category | flops | bytes accessed | tf_op | source)
XLA Modules:
  0.0 78.7 jit_solution(10117721585135595575)
XLA Ops:
  1.4 1.2 %copy-done.12 = bf16[512,1024]{1,0:T(8,128)(2,1)S(1)} copy-done((bf16[512,1024]{1,0:T(8,128)(2,1)S(1)}, bf16[512,1024]{1,0:T(8,128)(2,1)}, u32[]{:S(2)}) %copy-start.12) | copy-done | bytes 1048600
  2.6 1.2 %copy-done.13 = bf16[512,1024]{1,0:T(8,128)(2,1)S(1)} copy-done((bf16[512,1024]{1,0:T(8,128)(2,1)S(1)}, bf16[512,1024]{1,0:T(8,128)(2,1)}, u32[]{:S(2)}) %copy-start.13) | copy-done | bytes 1048600
  3.8 3.3 %shard_map.93 = (f32[520,128]{1,0:T(8,128)S(1)}, f32[520,128]{1,0:T(8,128)S(1)}, f32[8,128,128]{2,1,0:T(8,128)S(1)}, f32[32,512]{1,0:T(8,128)S(1)}, f32[512,128]...) custom-call(s32[1]{0:T(128)} %bitcast.scalar_ref, f32[8,512]{1,0:T(8,128)S(1)} %copy-done.29, ...), custom_call_target="tpu_custom_call" | custom-call | tf_op jit(solution)/shard_map/pallas_call | solution.py:50
  8.9 3.0 %collective-permute-start.1 = (f32[264,128]{1,0:T(8,128)S(1)}, f32[264,128]{1,0:T(8,128)S(1)}, u32[]{:S(2)}, u32[]{:S(2)}) collective-permute-start(f32[264,128]{1,0:T(8,128)S(1)} %get-tuple-element.70.refs_5_), channel_id=1, source_target_pairs={{0,2},{1,3},{2,0},{3,1},{4,6},{5,7},{6,4},{7,5},{8,10},{9,11},{10,... | collective-permute-start | bytes 405512 | tf_op jit(solution)/shard_map/ppermute | solution.py:333
  13.6 2.2 %collective-permute-done.1.refs_1_.refs_3_ = f32[264,128]{1,0:T(8,128)S(1)} collective-permute-done((f32[264,128]{1,0:T(8,128)S(1)}, f32[264,128]{1,0:T(8,128)S(1)}, u32[]{:S(2)}, u32[]{:S(2)}) %collective-permute-start.1) | collective-permute-done | bytes 135200 | tf_op jit(solution)/shard_map/ppermute | solution.py:333
  15.8 1.9 %collective-permute-start.2 = (f32[264,128]{1,0:T(8,128)S(1)}, f32[264,128]{1,0:T(8,128)S(1)}, u32[]{:S(2)}, u32[]{:S(2)}) collective-permute-start(f32[264,128]{1,0:T(8,128)S(1)} %shard_map.96.refs_6_.refs_0_), channel_id=1, source_target_pairs={{0,4},{1,5},{2,6},{3,7},{4,0},{5,1},{6,2},{7,3},{8,12},{9,13},{10,... | collective-permute-start | bytes 405512 | tf_op jit(solution)/shard_map/ppermute | solution.py:333
  21.0 2.8 %collective-permute-start.3 = (f32[264,128]{1,0:T(8,128)S(1)}, f32[264,128]{1,0:T(8,128)S(1)}, u32[]{:S(2)}, u32[]{:S(2)}) collective-permute-start(f32[264,128]{1,0:T(8,128)S(1)} %get-tuple-element.76.refs_6_), channel_id=1, source_target_pairs={{0,8},{1,9},{2,10},{3,11},{4,12},{5,13},{6,14},{7,15},{8,0},{9,1},... | collective-permute-start | bytes 405512 | tf_op jit(solution)/shard_map/ppermute | solution.py:333
  25.3 3.8 %collective-permute-done.3.refs_0_ = f32[264,128]{1,0:T(8,128)S(1)} collective-permute-done((f32[264,128]{1,0:T(8,128)S(1)}, f32[264,128]{1,0:T(8,128)S(1)}, u32[]{:S(2)}, u32[]{:S(2)}) %collective-permute-start.3) | collective-permute-done | bytes 135200 | tf_op jit(solution)/shard_map/ppermute | solution.py:333
  32.8 1.4 %collective-permute-done.4.refs_1_ = f32[256,128]{1,0:T(8,128)S(1)} collective-permute-done((f32[256,128]{1,0:T(8,128)S(1)}, f32[256,128]{1,0:T(8,128)S(1)}, u32[]{:S(2)}, u32[]{:S(2)}) %collective-permute-start.4) | collective-permute-done | bytes 131104 | tf_op jit(solution)/shard_map/ppermute | solution.py:333
  34.3 1.5 %collective-permute-done.5.refs_6_ = f32[512,128]{1,0:T(8,128)S(1)} collective-permute-done((f32[512,128]{1,0:T(8,128)S(1)}, f32[512,128]{1,0:T(8,128)S(1)}, u32[]{:S(2)}, u32[]{:S(2)}) %collective-permute-start.5) | collective-permute-done | bytes 262176 | tf_op jit(solution)/shard_map/ppermute | solution.py:333
  35.8 5.1 %shard_map.103 = (f32[520,128]{1,0:T(8,128)S(1)}, f32[520,128]{1,0:T(8,128)}, bf16[512,1024]{1,0:T(8,128)(2,1)S(1)}, bf16[8,2,128,128]{3,2,1,0:T(8,128)(2,1)S(1)...) custom-call(s32[1]{0:T(128)} %bitcast.scalar_ref, bf16[512,1024]{1,0:T(8,128)(2,1)S(1)} %copy-done, ...), custom_call_target="tpu_custom_call" | custom-call | tf_op jit(solution)/shard_map/pallas_call | solution.py:50
  44.4 1.7 %collective-permute-done.6.refs_1_.refs_3_ = f32[520,128]{1,0:T(8,128)} collective-permute-done((f32[520,128]{1,0:T(8,128)}, f32[520,128]{1,0:T(8,128)}, u32[]{:S(2)}, u32[]{:S(2)}) %collective-permute-start.6) | collective-permute-done | bytes 266272 | tf_op jit(solution)/shard_map/ppermute | solution.py:333
  49.2 1.2 %copy-done.2 = bf16[512,1024]{1,0:T(8,128)(2,1)S(1)} copy-done((bf16[512,1024]{1,0:T(8,128)(2,1)S(1)}, bf16[512,1024]{1,0:T(8,128)(2,1)}, u32[]{:S(2)}) %copy-start.2) | copy-done | bytes 1048600
  50.4 1.2 %copy-done.18 = f32[2,2,256,256]{3,2,1,0:T(8,128)S(1)} copy-done((f32[2,2,256,256]{3,2,1,0:T(8,128)S(1)}, f32[2,2,256,256]{3,2,1,0:T(8,128)}, u32[]{:S(2)}) %copy-start.18) | copy-done | bytes 1048600
  52.7 2.0 %shard_map.105 = (f32[512,256]{1,0:T(8,128)S(1)}, f32[512,256]{1,0:T(8,128)S(1)}, bf16[512,1024]{1,0:T(8,128)(2,1)}) custom-call(s32[1]{0:T(128)} %bitcast.scalar_ref, bf16[512,1024]{1,0:T(8,128)(2,1)S(1)} %copy-done, bf16[512,1024]{1,0:T(8,128)(2,1)S(1)} %get-tuple-element.71.refs_1_.refs_0_, bf16[512,1024]{1,0:T(8,128)(2,1)S(1)} %get-tuple-element.72.refs_2_.refs_1_, ...), custom_call_target="tpu_custom_call" | custom-call | tf_op jit(solution)/shard_map/pallas_call | solution.py:50
  55.8 2.0 %shard_map.107 = (f32[512,256]{1,0:T(8,128)S(1)}, f32[512,256]{1,0:T(8,128)S(1)}, bf16[512,1024]{1,0:T(8,128)(2,1)}) custom-call(s32[1]{0:T(128)} %bitcast.scalar_ref, bf16[512,1024]{1,0:T(8,128)(2,1)S(1)} %copy-done, bf16[512,1024]{1,0:T(8,128)(2,1)S(1)} %get-tuple-element.71.refs_1_.refs_0_, ...), custom_call_target="tpu_custom_call", output_to_operand_aliasing={{2}: (9, {})} | custom-call | tf_op jit(solution)/shard_map/pallas_call | solution.py:50
  57.8 2.4 %collective-permute-done.8.refs_1_ = f32[264,128]{1,0:T(8,128)S(1)} collective-permute-done((f32[264,128]{1,0:T(8,128)S(1)}, f32[264,128]{1,0:T(8,128)S(1)}, u32[]{:S(2)}, u32[]{:S(2)}) %collective-permute-start.8) | collective-permute-done | bytes 135200 | tf_op jit(solution)/shard_map/ppermute | solution.py:333
  60.2 2.4 %collective-permute-start.9 = (f32[264,128]{1,0:T(8,128)S(1)}, f32[264,128]{1,0:T(8,128)S(1)}, u32[]{:S(2)}, u32[]{:S(2)}) collective-permute-start(f32[264,128]{1,0:T(8,128)S(1)} %get-tuple-element.107.refs_9_), channel_id=1, source_target_pairs={{0,8},{1,9},{2,10},{3,11},{4,12},{5,13},{6,14},{7,15},{8,0},{9,1},... | collective-permute-start | bytes 405512 | tf_op jit(solution)/shard_map/ppermute | solution.py:333
  62.6 2.2 %shard_map.109 = (f32[512,256]{1,0:T(8,128)S(1)}, f32[512,256]{1,0:T(8,128)S(1)}, bf16[512,1024]{1,0:T(8,128)(2,1)}) custom-call(s32[1]{0:T(128)} %bitcast.scalar_ref, bf16[512,1024]{1,0:T(8,128)(2,1)S(1)} %copy-done, bf16[512,1024]{1,0:T(8,128)(2,1)S(1)} %get-tuple-element.71.refs_1_.refs_0_, ...), custom_call_target="tpu_custom_call", output_to_operand_aliasing={{2}: (9, {})} | custom-call | tf_op jit(solution)/shard_map/pallas_call | solution.py:50
  64.8 3.7 %collective-permute-done.9.refs_0_ = f32[264,128]{1,0:T(8,128)S(1)} collective-permute-done((f32[264,128]{1,0:T(8,128)S(1)}, f32[264,128]{1,0:T(8,128)S(1)}, u32[]{:S(2)}, u32[]{:S(2)}) %collective-permute-start.9) | collective-permute-done | bytes 135200 | tf_op jit(solution)/shard_map/ppermute | solution.py:333
  69.7 2.0 %shard_map.111 = (f32[512,256]{1,0:T(8,128)S(1)}, f32[512,256]{1,0:T(8,128)S(1)}, bf16[512,1024]{1,0:T(8,128)(2,1)}) custom-call(s32[1]{0:T(128)} %bitcast.scalar_ref, bf16[512,1024]{1,0:T(8,128)(2,1)S(1)} %copy-done, bf16[512,1024]{1,0:T(8,128)(2,1)S(1)} %get-tuple-element.71.refs_1_.refs_0_, ...), custom_call_target="tpu_custom_call", output_to_operand_aliasing={{2}: (9, {})} | custom-call | tf_op jit(solution)/shard_map/pallas_call | solution.py:50
  71.7 2.0 %collective-permute-done.10.refs_1_ = f32[256,128]{1,0:T(8,128)S(1)} collective-permute-done((f32[256,128]{1,0:T(8,128)S(1)}, f32[256,128]{1,0:T(8,128)S(1)}, u32[]{:S(2)}, u32[]{:S(2)}) %collective-permute-start.10) | collective-permute-done | bytes 131104 | tf_op jit(solution)/shard_map/ppermute | solution.py:333
  74.8 1.5 %collective-permute-done.11.refs_6_ = f32[512,128]{1,0:T(8,128)S(1)} collective-permute-done((f32[512,128]{1,0:T(8,128)S(1)}, f32[512,128]{1,0:T(8,128)S(1)}, u32[]{:S(2)}, u32[]{:S(2)}) %collective-permute-start.11) | collective-permute-done | bytes 262176 | tf_op jit(solution)/shard_map/ppermute | solution.py:333
  76.4 2.2 %shard_map.113 = (bf16[512,1024]{1,0:T(8,128)(2,1)}, bf16[512,1024]{1,0:T(8,128)(2,1)}) custom-call(s32[1]{0:T(128)} %bitcast.scalar_ref, bf16[512,1024]{1,0:T(8,128)(2,1)S(1)} %get-tuple-element.71.refs_1_.refs_0_, bf16[512,1024]{1,0:T(8,128)(2,1)S(1)} %get-tuple-element.72.refs_2_.refs_1_, f32[8,128,128]{2,1,0:T(8,128)S(1)} %copy-done.26, ...), custom_call_target="tpu_custom_call" | custom-call | tf_op jit(solution)/shard_map/pallas_call | solution.py:50
  (83 shorter events, 23.6 us)
Async XLA Ops:
  3.8 8.0 %copy-start = (bf16[512,1024]{1,0:T(8,128)(2,1)S(1)}, bf16[512,1024]{1,0:T(8,128)(2,1)}, u32[]{:S(2)}) copy-start(bf16[512,1024]{1,0:T(8,128)(2,1)} %refs_0_.19) | copy-start | bytes 3145732
  7.2 1.7 %collective-permute-start = (f32[520,128]{1,0:T(8,128)S(1)}, f32[520,128]{1,0:T(8,128)S(1)}, u32[]{:S(2)}, u32[]{:S(2)}) collective-permute-start(f32[520,128]{1,0:T(8,128)S(1)} %get-tuple-element.68), channel_id=1, source_target_pairs={{0,1},{1,0},{2,3},{3,2},{4,5},{5,4},{6,7},{7,6},{8,9},{9,8},{10,11... | collective-permute-start | bytes 798728 | tf_op jit(solution)/shard_map/ppermute | solution.py:333
  8.9 6.8 %collective-permute-start.1 = (f32[264,128]{1,0:T(8,128)S(1)}, f32[264,128]{1,0:T(8,128)S(1)}, u32[]{:S(2)}, u32[]{:S(2)}) collective-permute-start(f32[264,128]{1,0:T(8,128)S(1)} %get-tuple-element.70.refs_5_), channel_id=1, source_target_pairs={{0,2},{1,3},{2,0},{3,1},{4,6},{5,7},{6,4},{7,5},{8,10},{9,11},{10,... | collective-permute-start | bytes 405512 | tf_op jit(solution)/shard_map/ppermute | solution.py:333
  13.6 4.8 %copy-start.23 = (bf16[2,2,256,256]{3,2,1,0:T(8,128)(2,1)}, bf16[2,2,256,256]{3,2,1,0:T(8,128)(2,1)S(1)}, u32[]{:S(2)}) copy-start(bf16[2,2,256,256]{3,2,1,0:T(8,128)(2,1)S(1)} %get-tuple-element.97.refs_4_) | copy-start | bytes 1572868
  15.8 5.2 %collective-permute-start.2 = (f32[264,128]{1,0:T(8,128)S(1)}, f32[264,128]{1,0:T(8,128)S(1)}, u32[]{:S(2)}, u32[]{:S(2)}) collective-permute-start(f32[264,128]{1,0:T(8,128)S(1)} %shard_map.96.refs_6_.refs_0_), channel_id=1, source_target_pairs={{0,4},{1,5},{2,6},{3,7},{4,0},{5,1},{6,2},{7,3},{8,12},{9,13},{10,... | collective-permute-start | bytes 405512 | tf_op jit(solution)/shard_map/ppermute | solution.py:333
  21.0 8.1 %collective-permute-start.3 = (f32[264,128]{1,0:T(8,128)S(1)}, f32[264,128]{1,0:T(8,128)S(1)}, u32[]{:S(2)}, u32[]{:S(2)}) collective-permute-start(f32[264,128]{1,0:T(8,128)S(1)} %get-tuple-element.76.refs_6_), channel_id=1, source_target_pairs={{0,8},{1,9},{2,10},{3,11},{4,12},{5,13},{6,14},{7,15},{8,0},{9,1},... | collective-permute-start | bytes 405512 | tf_op jit(solution)/shard_map/ppermute | solution.py:333
  25.3 3.8 %copy-start.8 = (f32[2,2,256,256]{3,2,1,0:T(8,128)}, f32[2,2,256,256]{3,2,1,0:T(8,128)S(1)}, u32[]{:S(2)}) copy-start(f32[2,2,256,256]{3,2,1,0:T(8,128)S(1)} %get-tuple-element.94.refs_5_) | copy-start | bytes 3145732
  29.1 5.0 %collective-permute-start.4 = (f32[256,128]{1,0:T(8,128)S(1)}, f32[256,128]{1,0:T(8,128)S(1)}, u32[]{:S(2)}, u32[]{:S(2)}) collective-permute-start(f32[256,128]{1,0:T(8,128)S(1)} %get-tuple-element.80.refs_6_), channel_id=1, source_target_pairs={{0,2},{1,3},{2,0},{3,1},{4,6},{5,7},{6,4},{7,5},{8,10},{9,11},{10,... | collective-permute-start | bytes 393224 | tf_op jit(solution)/shard_map/ppermute | solution.py:333
  32.8 3.1 %copy-start.14 = (bf16[512,1024]{1,0:T(8,128)(2,1)S(1)}, bf16[512,1024]{1,0:T(8,128)(2,1)}, u32[]{:S(2)}) copy-start(bf16[512,1024]{1,0:T(8,128)(2,1)} %refs_1_.1) | copy-start | bytes 3145732
  34.2 1.6 %collective-permute-start.5 = (f32[512,128]{1,0:T(8,128)S(1)}, f32[512,128]{1,0:T(8,128)S(1)}, u32[]{:S(2)}, u32[]{:S(2)}) collective-permute-start(f32[512,128]{1,0:T(8,128)S(1)} %get-tuple-element.83), channel_id=1, source_target_pairs={{0,1},{1,0},{2,3},{3,2},{4,5},{5,4},{6,7},{7,6},{8,9},{9,8},{10,11... | collective-permute-start | bytes 786440 | tf_op jit(solution)/shard_map/ppermute | solution.py:333
  44.2 1.9 %collective-permute-start.6 = (f32[520,128]{1,0:T(8,128)}, f32[520,128]{1,0:T(8,128)}, u32[]{:S(2)}, u32[]{:S(2)}) collective-permute-start(f32[520,128]{1,0:T(8,128)} %get-tuple-element.100), channel_id=1, source_target_pairs={{0,1},{1,0},{2,3},{3,2},{4,5},{5,4},{6,7},{7,6},{8,9},{9,8},{10,11... | collective-permute-start | bytes 798728 | tf_op jit(solution)/shard_map/ppermute | solution.py:333
  44.4 4.8 %copy-start.4 = (bf16[8,2,128,128]{3,2,1,0:T(8,128)(2,1)S(1)}, bf16[8,2,128,128]{3,2,1,0:T(8,128)(2,1)}, u32[]{:S(2)}) copy-start(bf16[8,2,128,128]{3,2,1,0:T(8,128)(2,1)} %copy-done.3) | copy-start | bytes 1572868
  48.1 6.7 %collective-permute-start.7 = (f32[264,128]{1,0:T(8,128)S(1)}, f32[264,128]{1,0:T(8,128)S(1)}, u32[]{:S(2)}, u32[]{:S(2)}) collective-permute-start(f32[264,128]{1,0:T(8,128)S(1)} %get-tuple-element.101.refs_8_), channel_id=1, source_target_pairs={{0,2},{1,3},{2,0},{3,1},{4,6},{5,7},{6,4},{7,5},{8,10},{9,11},{10,... | collective-permute-start | bytes 405512 | tf_op jit(solution)/shard_map/ppermute | solution.py:333
  52.7 2.8 %copy-start.11 = (f32[2,2,256,256]{3,2,1,0:T(8,128)S(1)}, f32[2,2,256,256]{3,2,1,0:T(8,128)}, u32[]{:S(2)}) copy-start(f32[2,2,256,256]{3,2,1,0:T(8,128)} %copy-done.10) | copy-start | bytes 3145732
  54.8 5.4 %collective-permute-start.8 = (f32[264,128]{1,0:T(8,128)S(1)}, f32[264,128]{1,0:T(8,128)S(1)}, u32[]{:S(2)}, u32[]{:S(2)}) collective-permute-start(f32[264,128]{1,0:T(8,128)S(1)} %shard_map.106.refs_9_.refs_0_), channel_id=1, source_target_pairs={{0,4},{1,5},{2,6},{3,7},{4,0},{5,1},{6,2},{7,3},{8,12},{9,13},{10,... | collective-permute-start | bytes 405512 | tf_op jit(solution)/shard_map/ppermute | solution.py:333
  55.8 6.8 %copy-start.9 = (f32[2,2,256,256]{3,2,1,0:T(8,128)S(1)}, f32[2,2,256,256]{3,2,1,0:T(8,128)}, u32[]{:S(2)}) copy-start(f32[2,2,256,256]{3,2,1,0:T(8,128)} %copy-done.8) | copy-start | bytes 3145732
  57.8 4.8 %copy-start.20 = (bf16[2,2,256,256]{3,2,1,0:T(8,128)(2,1)S(1)}, bf16[2,2,256,256]{3,2,1,0:T(8,128)(2,1)}, u32[]{:S(2)}) copy-start(bf16[2,2,256,256]{3,2,1,0:T(8,128)(2,1)} %copy-done.19) | copy-start | bytes 1572868
  60.2 8.3 %collective-permute-start.9 = (f32[264,128]{1,0:T(8,128)S(1)}, f32[264,128]{1,0:T(8,128)S(1)}, u32[]{:S(2)}, u32[]{:S(2)}) collective-permute-start(f32[264,128]{1,0:T(8,128)S(1)} %get-tuple-element.107.refs_9_), channel_id=1, source_target_pairs={{0,8},{1,9},{2,10},{3,11},{4,12},{5,13},{6,14},{7,15},{8,0},{9,1},... | collective-permute-start | bytes 405512 | tf_op jit(solution)/shard_map/ppermute | solution.py:333
  62.6 7.0 %copy-start.28 = (bf16[2,2,256,256]{3,2,1,0:T(8,128)(2,1)S(1)}, bf16[2,2,256,256]{3,2,1,0:T(8,128)(2,1)}, u32[]{:S(2)}) copy-start(bf16[2,2,256,256]{3,2,1,0:T(8,128)(2,1)} %copy-done.27) | copy-start | bytes 1572868
  64.8 4.8 %copy-start.16 = (f32[2,2,256,256]{3,2,1,0:T(8,128)S(1)}, f32[2,2,256,256]{3,2,1,0:T(8,128)}, u32[]{:S(2)}) copy-start(f32[2,2,256,256]{3,2,1,0:T(8,128)} %copy-done.15) | copy-start | bytes 3145732
  68.6 5.0 %collective-permute-start.10 = (f32[256,128]{1,0:T(8,128)S(1)}, f32[256,128]{1,0:T(8,128)S(1)}, u32[]{:S(2)}, u32[]{:S(2)}) collective-permute-start(f32[256,128]{1,0:T(8,128)S(1)} %get-tuple-element.111.refs_9_), channel_id=1, source_target_pairs={{0,2},{1,3},{2,0},{3,1},{4,6},{5,7},{6,4},{7,5},{8,10},{9,11},{10,... | collective-permute-start | bytes 393224 | tf_op jit(solution)/shard_map/ppermute | solution.py:333
  69.7 4.0 %copy-start.7 = (f32[520,128]{1,0:T(8,128)S(1)}, f32[520,128]{1,0:T(8,128)}, u32[]{:S(2)}) copy-start(f32[520,128]{1,0:T(8,128)} %copy-done.5) | copy-start | bytes 798724
  73.7 2.7 %copy-start.26 = (f32[8,128,128]{2,1,0:T(8,128)S(1)}, f32[8,128,128]{2,1,0:T(8,128)}, u32[]{:S(2)}) copy-start(f32[8,128,128]{2,1,0:T(8,128)} %copy-done.25) | copy-start | bytes 1572868
  74.8 1.6 %collective-permute-start.11 = (f32[512,128]{1,0:T(8,128)S(1)}, f32[512,128]{1,0:T(8,128)S(1)}, u32[]{:S(2)}, u32[]{:S(2)}) collective-permute-start(f32[512,128]{1,0:T(8,128)S(1)} %get-tuple-element.117), channel_id=1, source_target_pairs={{0,1},{1,0},{2,3},{3,2},{4,5},{5,4},{6,7},{7,6},{8,9},{9,8},{10,11... | collective-permute-start | bytes 786440 | tf_op jit(solution)/shard_map/ppermute | solution.py:333
  (19 other events, 18.0 us)

commit v3 on v2

v3 whole, which is shorter than its diff:
```python
import functools

import jax
import jax.numpy as jnp
from jax import lax
from jax.experimental import pallas as pl
from jax.experimental.pallas import tpu as pltpu
from jax.sharding import PartitionSpec as P

BLOCK = 256
HALF = 128
DH = 128
EPS = 1e-05
FAR = -1e30
GROUPS = 4
CHUNKS = 2
PIECES = 2
F32 = jnp.float32
BF16 = jnp.bfloat16

NN = (((1,), (0,)), ((), ()))
NT = (((1,), (1,)), ((), ()))
TN = (((0,), (0,)), ((), ()))


def mm(a, b, dims=NN):
    return lax.dot_general(a, b, dims, preferred_element_type=F32)


def cut(j):
    return slice(j * DH, (j + 1) * DH)


def block(b):
    return slice(b * BLOCK, (b + 1) * BLOCK)


SMEM = pl.BlockSpec(memory_space=pltpu.SMEM)
VMEM = pl.BlockSpec(memory_space=pltpu.VMEM)
ANY = pl.BlockSpec(memory_space=pl.ANY)
HBM = pl.BlockSpec(memory_space=pltpu.HBM)


def run(body, scalar, inside, outs, outside=(), after=(), aliases=None, scratch=(), megabytes=8):
    taken = len(inside) + len(outside)

    def kernel(scalar_ref, *refs):
        body(scalar_ref, *refs[:taken], *refs[taken + len(after) :])

    shapes = [pltpu.HBM(o.shape, o.dtype) if isinstance(o, jax.ShapeDtypeStruct) else pltpu.VMEM(*o) for o in outs]
    return pl.pallas_call(
        kernel,
        in_specs=[SMEM] + [VMEM] * len(inside) + [HBM] * len(outside) + [ANY] * len(after),
        out_specs=[HBM if isinstance(o, jax.ShapeDtypeStruct) else VMEM for o in outs],
        out_shape=shapes,
        input_output_aliases={1 + len(inside) + i: o for i, o in (aliases or {}).items()},
        scratch_shapes=list(scratch),
        compiler_params=pltpu.CompilerParams(vmem_limit_bytes=megabytes << 20),
    )(scalar, *[pltpu.with_memory_space_constraint(a, pltpu.VMEM) for a in inside],
      *[pltpu.with_memory_space_constraint(a, pltpu.HBM) for a in outside], *after)


def prepare(decay_ref, start_ref, rows_ref, cols_ref):
    tri = (
        lax.broadcasted_iota(jnp.int32, (BLOCK, BLOCK), 0) <= lax.broadcasted_iota(jnp.int32, (BLOCK, BLOCK), 1)
    ).astype(F32)
    for b in range(decay_ref.shape[1] // BLOCK):
        at = block(b)
        starts = jnp.broadcast_to(start_ref[:, at].astype(F32), (8, BLOCK))
        both = jnp.concatenate([decay_ref[:, at], starts], axis=0)
        sums = lax.dot_general(both, tri, NN, precision=lax.Precision.HIGHEST, preferred_element_type=F32)
        cumul, marks = sums[:8], sums[8:]
        last, last_mark = cumul[:, BLOCK - 1 :], marks[:, BLOCK - 1 :]
        entering = jnp.where(marks == 0.0, jnp.exp(cumul), 0.0)
        leaving = jnp.where(marks == last_mark, jnp.exp(last - cumul), 0.0)
        stack = jnp.concatenate([cumul, entering, leaving, marks], axis=0)
        rows_ref[:, at] = stack
        cols_ref[at, :] = jnp.concatenate([stack, jnp.zeros((96, BLOCK), F32)], axis=0).T


def keeps(rows_ref, head):
    enter = rows_ref[8 + head : 9 + head, :]
    k0 = jnp.broadcast_to(enter[:, BLOCK - 1 : BLOCK], (1, DH))
    k1 = jnp.broadcast_to(enter[:, 2 * BLOCK - 1 : 2 * BLOCK], (1, DH))
    return k0, k1


def send_out(place, k, terms_ref, keep_ref, own_ref, send_ref):
    for out, first in ((own_ref, 0), (send_ref, 2 * k)):
        for r in range(2 * k):
            group, j = (first + r) // k, (first + r) % k
            head = (group ^ place[0]) * k + j
            out[cut(r), :] = terms_ref[head]
            out[pl.ds(2 * k * DH + r, 1), :] = keep_ref[pl.ds(head, 1), :]
        rest = 8 - 2 * k
        out[2 * k * DH + 2 * k :, :] = jnp.ones((rest, DH), F32)


def take_in(place, k, mine_ref, other_ref, state_ref):
    for r in range(GROUPS * k):
        source = mine_ref if r < 2 * k else other_ref
        state_ref[((r // k) ^ place[0]) * k + r % k] = source[cut(r % (2 * k)), :]


def k1_body(k, head0, place, *refs):
    heads = GROUPS * k
    loads = []
    if head0 == 0:
        (decay_hbm, start_hbm, key_hbm, value_hbm, own_ref, send_ref, loc_ref, key_ref, value_ref, rows_ref, cols_ref,
         terms_ref, keep_ref, sems, decay_ref, start_ref) = refs
        loads = [
            pltpu.make_async_copy(decay_hbm, decay_ref, sems.at[2 * heads]),
            pltpu.make_async_copy(start_hbm, start_ref, sems.at[2 * heads + 1]),
        ]
    else:
        (rows_ref, key_hbm, value_hbm, own_ref, send_ref, loc_ref, key_ref, value_ref,
         terms_ref, keep_ref, sems) = refs
    for j in range(heads):
        for i, (source, target) in enumerate(((key_hbm, key_ref), (value_hbm, value_ref))):
            loads.append(
                pltpu.make_async_copy(source.at[:, cut(head0 + j)], target.at[:, cut(j)], sems.at[2 * j + i])
            )
    for load in loads:
        load.start()
    if head0 == 0:
        loads[0].wait()
        loads[1].wait()
        prepare(decay_ref, start_ref, rows_ref, cols_ref)
    for load in loads[-2 * heads :]:
        load.wait()
    for j in range(heads):
        head = head0 + j
        leave = rows_ref[16 + head : 17 + head, :]
        terms = []
        for b in range(2):
            keys = key_ref[block(b), cut(j)].T.astype(F32)
            scaled = (keys * leave[:, block(b)]).astype(BF16)
            terms.append(mm(scaled, value_ref[block(b), cut(j)]))
        k0, k1 = keeps(rows_ref, head)
        loc_ref[j] = terms[0]
        terms_ref[j] = k1 * terms[0] + terms[1]
        keep_ref[j : j + 1, :] = k0 * k1
    send_out(place, k, terms_ref, keep_ref, own_ref, send_ref)


def make_bias(rows_ref, cols_ref, bias_ref, turned_ref):
    down = lax.broadcasted_iota(jnp.int32, (BLOCK, BLOCK), 0)
    along = lax.broadcasted_iota(jnp.int32, (BLOCK, BLOCK), 1)
    for b in range(2):
        same = cols_ref[block(b), 24:25] == rows_ref[24:25, block(b)]
        bias_ref[b] = jnp.where((down >= along) & same, 0.0, FAR)
        turned_ref[b] = jnp.where((down <= along) & same, 0.0, FAR)


def k2_body(first, head0, base, count, place, query_ref, key_ref, value_ref, rows_ref, cols_ref, *refs):
    if first:
        (within_ref, grid_ref, turned_ref, weighted_ref, scaled_ref, enter_ref, leave_ref,
         bias_ref, bias_turned_ref) = refs
        make_bias(rows_ref, cols_ref, bias_ref, bias_turned_ref)
    else:
        (bias_ref, bias_turned_ref, within_ref, grid_ref, turned_ref, weighted_ref, scaled_ref, enter_ref,
         leave_ref) = refs
    zeros = jnp.zeros((HALF, HALF), F32)
    for j in range(count):
        head = head0 + j
        inner = head - base
        for b in range(2):
            at = block(b)
            query, key = query_ref[at, cut(head)], key_ref[at, cut(inner)]
            cum_row = rows_ref[head : head + 1, at]
            top, low = slice(0, HALF), slice(HALF, BLOCK)
            cum_top = jnp.broadcast_to(cols_ref[b * BLOCK : b * BLOCK + HALF, head : head + 1], (HALF, HALF))
            cum_low = jnp.broadcast_to(cols_ref[b * BLOCK + HALF : (b + 1) * BLOCK, head : head + 1], (HALF, HALF))
            row_top, row_low = cum_row[:, :HALF], cum_row[:, HALF:]

            def decay(difference, limit):
                return jnp.exp(jnp.minimum(difference, limit))

            grid_ref[j, b, top, top] = decay(cum_top - row_top, bias_ref[b, top, top])
            grid_ref[j, b, low, top] = decay(cum_low - row_top, bias_ref[b, low, top])
            grid_ref[j, b, low, low] = decay(cum_low - row_low, bias_ref[b, low, low])
            grid_ref[j, b, top, low] = zeros
            turned_ref[j, b, top, top] = decay(row_top - cum_top, bias_turned_ref[b, top, top])
            turned_ref[j, b, top, low] = decay(row_low - cum_top, bias_turned_ref[b, top, low])
            turned_ref[j, b, low, low] = decay(row_low - cum_low, bias_turned_ref[b, low, low])
            turned_ref[j, b, low, top] = zeros
            weighted = (mm(query, key, NT) * grid_ref[j, b]).astype(BF16)
            weighted_ref[j, b] = (mm(key, query, NT) * turned_ref[j, b]).astype(BF16)
            within_ref[at, cut(j)] = mm(weighted, value_ref[at, cut(inner)])
            enter = rows_ref[8 + head : 9 + head, at]
            scaled_ref[j, b] = (query.T.astype(F32) * enter).astype(BF16)
            enter_ref[at, cut(j)] = jnp.broadcast_to(cols_ref[at, 8 + head : 9 + head], (BLOCK, DH))
            leave_ref[at, cut(j)] = jnp.broadcast_to(cols_ref[at, 16 + head : 17 + head], (BLOCK, DH))


def k3_body(k, head0, pieces, per, place, query_ref, grad_ref, loc_ref, rows_ref, mine_ref, other_ref, *refs):
    withins, scaleds, enters = refs[:pieces], refs[pieces : 2 * pieces], refs[2 * pieces : 3 * pieces]
    own_ref, send_ref, mixgrad_ref, states_ref, back_ref, attended_ref = refs[3 * pieces : 3 * pieces + 6]
    terms_ref, keep_ref, state_ref = refs[3 * pieces + 6 :]
    take_in(place, k, mine_ref, other_ref, state_ref)
    for j in range(GROUPS * k):
        head = head0 + j
        p, i = j // per, j % per
        k0, k1 = keeps(rows_ref, head)
        incoming = state_ref[j]
        states = (incoming, k0 * incoming + loc_ref[j])
        backs = []
        for b in range(2):
            at = block(b)
            low = states[b].astype(BF16)
            states_ref[j, b] = low
            mixture = withins[p][at, cut(i)] + mm(query_ref[at, cut(head)], low) * enters[p][at, cut(i)]
            wide = grad_ref[at, cut(head)].astype(F32)
            inverse = lax.rsqrt(jnp.mean(mixture * mixture, axis=1, keepdims=True) + EPS)
            along = jnp.mean(wide * mixture, axis=1, keepdims=True) * inverse
            normed = mixture * inverse
            attended_ref[at, cut(j)] = normed.astype(BF16)
            mixgrad = (inverse * (wide - normed * along)).astype(BF16)
            mixgrad_ref[at, cut(j)] = mixgrad
            backs.append(mm(scaleds[p][i, b], mixgrad))
        back_ref[j] = backs[1]
        terms_ref[j] = k0 * backs[1] + backs[0]
        keep_ref[j : j + 1, :] = k0 * k1
    send_out(place, k, terms_ref, keep_ref, own_ref, send_ref)


def k4_body(head0, base, count, has_alias, place, query_ref, key_ref, value_ref, mixgrad_ref, attended_ref, grid_ref,
            turned_ref, weighted_ref, states_ref, enter_ref, *refs):
    key_part_ref, value_part_ref, attended_hbm, query_grad_hbm, query_grad_ref, sems = refs[2 * has_alias :]
    inner0 = head0 - base
    ours = slice(head0 * DH, (head0 + count) * DH)
    attend = pltpu.make_async_copy(
        attended_ref.at[:, inner0 * DH : (inner0 + count) * DH], attended_hbm.at[:, ours], sems.at[0]
    )
    attend.start()
    for j in range(count):
        head = head0 + j
        inner = head - base
        for b in range(2):
            at = block(b)
            mixgrad = mixgrad_ref[at, cut(inner)]
            value = value_ref[at, cut(inner)]
            masked = (mm(mixgrad, value, NT) * grid_ref[j, b]).astype(BF16)
            query_grad_ref[at, cut(j)] = (
                mm(masked, key_ref[at, cut(inner)]) + mm(mixgrad, states_ref[inner, b], NT) * enter_ref[at, cut(j)]
            ).astype(BF16)
            turned = (mm(value, mixgrad, NT) * turned_ref[j, b]).astype(BF16)
            key_part_ref[at, cut(j)] = mm(turned, query_ref[at, cut(head)])
            value_part_ref[at, cut(j)] = mm(weighted_ref[j, b], mixgrad)
    grads = pltpu.make_async_copy(query_grad_ref, query_grad_hbm.at[:, ours], sems.at[1])
    grads.start()
    attend.wait()
    grads.wait()


def k5_body(k, head0, pieces, per, has_alias, place, key_ref, value_ref, back_ref, rows_ref, mine_ref, other_ref,
            *refs):
    key_parts, value_parts, leaves = refs[:pieces], refs[pieces : 2 * pieces], refs[2 * pieces : 3 * pieces]
    key_grad_hbm, value_grad_hbm, key_grad_ref, value_grad_ref, state_ref, sems = refs[3 * pieces + 2 * has_alias :]
    take_in(place, k, mine_ref, other_ref, state_ref)
    copies = []
    for j in range(GROUPS * k):
        head = head0 + j
        p, i = j // per, j % per
        k0, k1 = keeps(rows_ref, head)
        outgoing = state_ref[j]
        afters = (k1 * outgoing + back_ref[j], outgoing)
        for b in range(2):
            at = block(b)
            low = afters[b].astype(BF16)
            leave = leaves[p][at, cut(i)]
            key_grad_ref[at, cut(j)] = (
                key_parts[p][at, cut(i)] + mm(value_ref[at, cut(j)], low, NT) * leave
            ).astype(BF16)
            value_grad_ref[at, cut(j)] = (
                value_parts[p][at, cut(i)] + mm(key_ref[at, cut(j)], low) * leave
            ).astype(BF16)
        for n, (source, target) in enumerate(((key_grad_ref, key_grad_hbm), (value_grad_ref, value_grad_hbm))):
            copy = pltpu.make_async_copy(source.at[:, cut(j)], target.at[:, cut(head)], sems.at[2 * j + n])
            copy.start()
            copies.append(copy)
    for copy in copies:
        copy.wait()


def joined(later, got_ref, held_ref, heads, j):
    one = slice(heads * DH + j, heads * DH + j + 1)
    a_got, a_held = got_ref[one, :], held_ref[one, :]
    state = jnp.where(later, a_held, 1.0) * got_ref[cut(j), :] + jnp.where(later, 1.0, a_got) * held_ref[cut(j), :]
    return state, a_got * a_held


def before(later, got_ref, prefix_ref, k, j):
    one = slice(k * DH + j, k * DH + j + 1)
    a_got = got_ref[one, :]
    if prefix_ref is None:
        return jnp.where(later, 1.0, 0.0) * got_ref[cut(j), :], jnp.where(later, a_got, 1.0)
    a = prefix_ref[one, :]
    state = jnp.where(later, a, 0.0) * got_ref[cut(j), :] + prefix_ref[cut(j), :]
    return state, jnp.where(later, a * a_got, a)


def put(out, heads, j, value):
    out[cut(j), :], out[heads * DH + j : heads * DH + j + 1, :] = value


def c1_body(turn, k, place, own_ref, got_ref, keep_ref, send_ref):
    later = (place[turn] & 1) == 1
    for out in (keep_ref, send_ref):
        out[k * DH :, :] = jnp.ones((8, DH), F32)
    for j in range(2 * k):
        put(keep_ref if j < k else send_ref, k, j % k, joined(later, got_ref, own_ref, 2 * k, j))


def c2_body(turn, k, place, own_ref, got_ref, total_ref):
    later = (place[turn] & 2) == 2
    total_ref[k * DH :, :] = jnp.ones((8, DH), F32)
    for j in range(k):
        put(total_ref, k, j, joined(later, got_ref, own_ref, k, j))


def cz_body(turn, k, bit, first, place, *refs):
    total_ref, got_ref = refs[:2]
    prefix_ref = None if first else refs[2]
    new_total_ref, new_prefix_ref = refs[-2:]
    later = (place[turn] & bit) == bit
    for out in (new_total_ref, new_prefix_ref):
        out[k * DH :, :] = jnp.ones((8, DH), F32)
    for j in range(k):
        put(new_total_ref, k, j, joined(later, got_ref, total_ref, k, j))
        put(new_prefix_ref, k, j, before(later, got_ref, prefix_ref, k, j))


def c3_body(turn, k, bit, first, place, *refs):
    got_ref = refs[0]
    prefix_ref = None if first else refs[1]
    own_ref, chip_ref, mine_ref, send_ref = refs[-4:]
    later = (place[turn] & bit) == bit
    upper = (place[turn] & 2) == 2
    for j in range(k):
        at, one = cut(j), slice(k * DH + j, k * DH + j + 1)
        prefix, _ = before(later, got_ref, prefix_ref, k, j)
        mine_ref[at, :] = jnp.where(upper, chip_ref[one, :], 1.0) * prefix + jnp.where(upper, 1.0, 0.0) * chip_ref[at, :]
        send_ref[at, :] = jnp.where(upper, 1.0, own_ref[one, :]) * prefix + jnp.where(upper, 0.0, 1.0) * own_ref[at, :]


def c4_body(turn, k, place, half_ref, got_half_ref, own_ref, got_ref, mine_ref, send_ref):
    later = (place[turn] & 1) == 1
    for j in range(2 * k):
        at, one = cut(j), slice(2 * k * DH + j, 2 * k * DH + j + 1)
        chip = half_ref[cut(j), :] if j < k else got_half_ref[cut(j - k), :]
        mine_ref[at, :] = jnp.where(later, got_ref[one, :], 1.0) * chip + jnp.where(later, 1.0, 0.0) * got_ref[at, :]
        send_ref[at, :] = jnp.where(later, 1.0, own_ref[one, :]) * chip + jnp.where(later, 0.0, 1.0) * own_ref[at, :]


def exchange(x, bit, count):
    return lax.ppermute(x, "seq", [(i, i ^ bit) for i in range(count)])


class Order:
    def __init__(self, place):
        self.place, self.last = place, ()

    def __call__(self, body, inside, outs, **options):
        taken = [id(a) for a in options.get("outside", ())]
        after = tuple(a for a in self.last if id(a) not in taken)
        out = run(body, self.place, inside, outs, after=after, **options)
        self.last = (out[0],)
        return out


def scan_devices(call, own, send, turn, k, count):
    half = ((k * DH + 8, DH), F32)
    got = exchange(send, 1, count)
    yield
    chip, chip_send = call(functools.partial(c1_body, turn, k), (own, got), (half, half))
    chip_got = exchange(chip_send, 2, count)
    yield
    (total,) = call(functools.partial(c2_body, turn, k), (chip, chip_got), (half,))
    prefix = ()
    bit = 4
    while bit < count:
        got_total = exchange(total, bit, count)
        yield
        if bit * 2 < count:
            body = functools.partial(cz_body, turn, k, bit, not prefix)
            total, *prefix = call(body, (total, got_total, *prefix), (half, half))
        else:
            body = functools.partial(c3_body, turn, k, bit, not prefix)
            mine, mine_send = call(body, (got_total, *prefix, chip, chip_got), (((k * DH, DH), F32),) * 2)
        bit *= 2
    mine_got = exchange(mine_send, 2, count)
    yield
    body = functools.partial(c4_body, turn, k)
    state, state_send = call(body, (mine, mine_got, own, got), (((2 * k * DH, DH), F32),) * 2)
    yield state, exchange(state_send, 1, count)


def drive(scans, fillers):
    fillers = list(fillers)
    step = 0
    while True:
        results = [next(scan) for scan in scans]
        if results[0] is not None:
            break
        if step and fillers:
            fillers.pop(0)()
        step += 1
    for filler in fillers:
        filler()
    return results


def local(query_rows, key_rows, value_rows, log_decay, run_start, out_grad):
    all_heads = log_decay.shape[0]
    tokens, width = query_rows.shape
    count = lax.axis_size("seq")
    seat = lax.axis_index("seq")
    place = jnp.stack([((seat & 1) << 1) | ((seat >> 1) & 1), seat, count - 1 - seat])
    call = Order(place)
    heads = all_heads // CHUNKS
    k = heads // GROUPS
    per = heads // PIECES
    chunks = range(CHUNKS)
    dma = pltpu.SemaphoreType.DMA
    message = ((2 * k * DH + 8, DH), F32)
    states = ((heads, DH, DH), F32)
    flat = jax.ShapeDtypeStruct((tokens, width), BF16)
    chunk_bf16 = ((tokens, heads * DH), BF16)
    piece_f32 = ((tokens, per * DH), F32)
    square = (per, 2, BLOCK, BLOCK)
    mask = ((2, BLOCK, BLOCK), F32)
    scratch_terms = (pltpu.VMEM((heads, DH, DH), F32), pltpu.VMEM((8, DH), F32))

    own, send, loc, keys, values, scans = [], [], [], [], [], []
    for c in chunks:
        outs = (message, message, states, chunk_bf16, chunk_bf16)
        scratch = scratch_terms + (dma((2 * heads + 2,)),)
        if c == 0:
            outs += (((32, tokens), F32), ((tokens, DH), F32))
            scratch += (pltpu.VMEM(log_decay.shape, F32), pltpu.VMEM((1, tokens), jnp.int32))
            inside, outside = (), (log_decay, run_start.reshape(1, tokens), key_rows, value_rows)
        else:
            inside, outside = (rows,), (key_rows, value_rows)
        out = call(functools.partial(k1_body, k, c * heads), inside, outs, outside=outside, scratch=scratch)
        if c == 0:
            rows, cols = out[5:]
        own.append(out[0])
        send.append(out[1])
        loc.append(out[2])
        keys.append(out[3])
        values.append(out[4])
        scans.append(scan_devices(call, out[0], out[1], 1, k, count))

    forward = []

    def k2(n):
        c = n // PIECES
        outs = (piece_f32, (square, F32), (square, F32), (square, BF16), ((per, 2, DH, BLOCK), BF16))
        outs += (piece_f32, piece_f32)
        inputs = (query_rows, keys[c], values[c], rows, cols)
        if n == 0:
            outs += (mask, mask)
        else:
            inputs += tuple(forward[0][7:])
        forward.append(call(functools.partial(k2_body, n == 0, n * per, c * heads, per), inputs, outs))

    fillers = range(CHUNKS * PIECES)
    results = drive(scans, [functools.partial(k2, n) for n in fillers])
    middle, scans = [], []
    for c, (mine, other) in enumerate(results):
        mid = forward[c * PIECES : (c + 1) * PIECES]
        out = call(
            functools.partial(k3_body, k, c * heads, PIECES, per),
            (query_rows, out_grad, loc[c], rows, mine, other)
            + tuple(f[0] for f in mid) + tuple(f[4] for f in mid) + tuple(f[5] for f in mid),
            (message, message, chunk_bf16, ((heads, 2, DH, DH), BF16), states, chunk_bf16),
            scratch=scratch_terms + (pltpu.VMEM((heads, DH, DH), F32),),
        )
        middle.append(out)
        scans.append(scan_devices(call, out[0], out[1], 2, k, count))

    backward = []

    def k4(n):
        c = n // PIECES
        _, _, mixgrad, states_low, _, attended = middle[c]
        f = forward[n]
        backward.append(
            call(
                functools.partial(k4_body, n * per, c * heads, per, int(n > 0)),
                (query_rows, keys[c], values[c], mixgrad, attended, f[1], f[2], f[3], states_low, f[5]),
                (piece_f32, piece_f32, flat, flat),
                outside=tuple(backward[-1][2:]) if backward else (),
                aliases={0: 2, 1: 3} if backward else None,
                scratch=(pltpu.VMEM((tokens, per * DH), BF16), dma((2,))),
            )
        )

    results = drive(scans, [functools.partial(k4, n) for n in fillers])
    grads = ()
    for c, (mine, other) in enumerate(results):
        back = backward[c * PIECES : (c + 1) * PIECES]
        mid = forward[c * PIECES : (c + 1) * PIECES]
        grads = call(
            functools.partial(k5_body, k, c * heads, PIECES, per, int(c > 0)),
            (keys[c], values[c], middle[c][4], rows, mine, other)
            + tuple(b[0] for b in back) + tuple(b[1] for b in back) + tuple(f[6] for f in mid),
            (flat, flat),
            outside=tuple(grads),
            aliases={0: 0, 1: 1} if grads else None,
            scratch=(pltpu.VMEM((tokens, heads * DH), BF16),) * 2
            + (pltpu.VMEM((heads, DH, DH), F32), dma((2 * heads,))),
        )
    return (*backward[-1][2:], *grads)


def solution(mesh):
    rows = P(("groups", "seq"), None)
    return jax.shard_map(
        local,
        mesh=mesh,
        in_specs=(rows, rows, rows, P(None, ("groups", "seq")), P(("groups", "seq")), rows),
        out_specs=(rows, rows, rows, rows),
        check_vma=False,
    )
```

time: 79.2 us -> 68.9 us (0.87)
  waiting for transfers between devices: 22.2 us -> 5 us
  local copies, waits for them, and re-layouts: 16.5 us -> 0.01 us
  Pallas kernels: 24.2 us -> 38.1 us
  starting transfers between devices: 14.8 us -> 24.5 us
    ppermute x12 -> x24, waiting for transfers between devices: 22.2 us -> 5 us  [exchange(): return lax.ppermute(x, 'seq', [(i, i ^ bit) for i in range(count)])]
    unnamed x62 -> x4, local copies, waits for them, and re-layouts: 16.5 us -> 0.01 us
    pallas_call x21 -> x34, Pallas kernels: 24.2 us -> 38.1 us  [run(): pl.pallas_call(kernel, in_specs=[SMEM] + [VMEM] * len(inside) + [HBM] * l...]
    ppermute x12 -> x24, starting transfers between devices: 14.8 us -> 24.5 us  [exchange(): return lax.ppermute(x, 'seq', [(i, i ^ bit) for i in range(count)])]
  transfers between devices with their start and end apart: 12 -> 24, of which waited for: 11 -> 6; matrix products, arithmetic and copies ran while one was open for 0% -> 0% of each run, Pallas kernels for 14% -> 49%
where the time goes in v3:
time: 68.9 us; the launch traced here: 68.7 us
  Pallas kernels  38.1 us (55%)
  starting transfers between devices  24.5 us (36%)
  waiting for transfers between devices  5 us (7%)
  between operations  0.98 us (1%)
    pallas_call x34, Pallas kernels, run(): pl.pallas_call(kernel, in_specs=[SMEM] + [VMEM] * len(inside) + [HBM] * l...  38.1 us
    ppermute x24, starting transfers between devices, exchange(): return lax.ppermute(x, 'seq', [(i, i ^ bit) for i in range(count)])  24.5 us
    ppermute x24, waiting for transfers between devices, exchange(): return lax.ppermute(x, 'seq', [(i, i ^ bit) for i in range(count)])  5 us
  transfers between devices with their start and end apart: 24, of which 6 were waited for; matrix products, arithmetic and copies ran while one was open for 0% of the time, Pallas kernels for 49%

profile of v3, /device:TPU:0, one launch (start us, length us, event | category | flops | bytes accessed | tf_op | source)
XLA Modules:
  0.0 68.7 jit_solution(4491489095032129401)
XLA Ops:
  0.7 2.3 %shard_map.93 = (f32[264,128]{1,0:T(8,128)S(1)}, f32[264,128]{1,0:T(8,128)S(1)}, f32[4,128,128]{2,1,0:T(8,128)S(1)}, bf16[512,512]{1,0:T(8,128)(2,1)S(1)}, bf16[...) custom-call(s32[3]{0:T(128)S(1)} %pad_add_fusion.scalar_ref, f32[8,512]{1,0:T(8,128)} %refs_0_.11, ...), custom_call_target="tpu_custom_call" | custom-call | tf_op jit(solution)/shard_map/pallas_call | solution.py:51
  3.6 2.3 %shard_map.94 = (f32[264,128]{1,0:T(8,128)S(1)}, f32[264,128]{1,0:T(8,128)S(1)}, f32[4,128,128]{2,1,0:T(8,128)S(1)}, bf16[512,512]{1,0:T(8,128)(2,1)S(1)}, bf16[512,512]{1,0:T(8,128)(2,1)S(1)}) custom-call(s32[3]{0:T(128)S(1)} %pad_add_fusion.scalar_ref, f32[32,512]{1,0:T(8,128)S(1)} %get-tuple-element.110.refs_0_.refs_3_, bf16[512,1024]{1,0:T(8,128)(2,1)} %refs_1_.3, ...), custom_call_target="tpu_custom_call" | custom-call | tf_op jit(solution)/shard_map/pallas_call | solution.py:51
  6.6 3.0 %collective-permute-start.3 = (f32[136,128]{1,0:T(8,128)S(1)}, f32[136,128]{1,0:T(8,128)S(1)}, u32[]{:S(2)}, u32[]{:S(2)}) collective-permute-start(f32[136,128]{1,0:T(8,128)S(1)} %get-tuple-element.121), channel_id=1, source_target_pairs={{0,2},{1,3},{2,0},{3,1},{4,6},{5,7},{6,4},{7,5},{8,10},{9,11},{10,... | collective-permute-start | bytes 208904 | tf_op jit(solution)/shard_map/ppermute | solution.py:357
  10.6 1.4 %shard_map.97 = (f32[512,256]{1,0:T(8,128)S(1)}, f32[2,2,256,256]{3,2,1,0:T(8,128)S(1)}, f32[2,2,256,256]{3,2,1,0:T(8,128)S(1)}, bf16[2,2,256,256]{3,2,1,0:T(8,1...) custom-call(s32[3]{0:T(128)S(1)} %pad_add_fusion.scalar_ref, ...), custom_call_target="tpu_custom_call" | custom-call | tf_op jit(solution)/shard_map/pallas_call | solution.py:51
  12.6 2.0 %collective-permute-start.5 = (f32[136,128]{1,0:T(8,128)S(1)}, f32[136,128]{1,0:T(8,128)S(1)}, u32[]{:S(2)}, u32[]{:S(2)}) collective-permute-start(f32[136,128]{1,0:T(8,128)S(1)} %shard_map.98.refs_2_.refs_0_), channel_id=1, source_target_pairs={{0,4},{1,5},{2,6},{3,7},{4,0},{5,1},{6,2},{7,3},{8,12},{9,13},{10,... | collective-permute-start | bytes 208904 | tf_op jit(solution)/shard_map/ppermute | solution.py:357
  15.2 1.6 %collective-permute-start.4 = (f32[136,128]{1,0:T(8,128)S(1)}, f32[136,128]{1,0:T(8,128)S(1)}, u32[]{:S(2)}, u32[]{:S(2)}) collective-permute-start(f32[136,128]{1,0:T(8,128)S(1)} %shard_map.99.refs_7_.refs_0_), channel_id=1, source_target_pairs={{0,4},{1,5},{2,6},{3,7},{4,0},{5,1},{6,2},{7,3},{8,12},{9,13},{10,... | collective-permute-start | bytes 208904 | tf_op jit(solution)/shard_map/ppermute | solution.py:357
  16.8 1.3 %shard_map.100 = (f32[512,256]{1,0:T(8,128)S(1)}, f32[2,2,256,256]{3,2,1,0:T(8,128)S(1)}, f32[2,2,256,256]{3,2,1,0:T(8,128)S(1)}, bf16[2,2,256,256]{3,2,1,0:T(8,...) custom-call(s32[3]{0:T(128)S(1)} %pad_add_fusion.scalar_ref, ...), custom_call_target="tpu_custom_call" | custom-call | tf_op jit(solution)/shard_map/pallas_call | solution.py:51
  18.7 2.7 %collective-permute-start.7 = (f32[136,128]{1,0:T(8,128)S(1)}, f32[136,128]{1,0:T(8,128)S(1)}, u32[]{:S(2)}, u32[]{:S(2)}) collective-permute-start(f32[136,128]{1,0:T(8,128)S(1)} %get-tuple-element.129.refs_2_), channel_id=1, source_target_pairs={{0,8},{1,9},{2,10},{3,11},{4,12},{5,13},{6,14},{7,15},{8,0},{9,1},... | collective-permute-start | bytes 208904 | tf_op jit(solution)/shard_map/ppermute | solution.py:357
  21.9 1.3 %collective-permute-start.6 = (f32[136,128]{1,0:T(8,128)S(1)}, f32[136,128]{1,0:T(8,128)S(1)}, u32[]{:S(2)}, u32[]{:S(2)}) collective-permute-start(f32[136,128]{1,0:T(8,128)S(1)} %get-tuple-element.130.refs_7_), channel_id=1, source_target_pairs={{0,8},{1,9},{2,10},{3,11},{4,12},{5,13},{6,14},{7,15},{8,0},{9,1},... | collective-permute-start | bytes 208904 | tf_op jit(solution)/shard_map/ppermute | solution.py:357
  23.2 1.3 %shard_map.103 = (f32[512,256]{1,0:T(8,128)S(1)}, f32[2,2,256,256]{3,2,1,0:T(8,128)S(1)}, f32[2,2,256,256]{3,2,1,0:T(8,128)S(1)}, bf16[2,2,256,256]{3,2,1,0:T(8,...) custom-call(s32[3]{0:T(128)S(1)} %pad_add_fusion.scalar_ref, ...), custom_call_target="tpu_custom_call" | custom-call | tf_op jit(solution)/shard_map/pallas_call | solution.py:51
  24.5 1.4 %collective-permute-done.7.refs_0_ = f32[136,128]{1,0:T(8,128)S(1)} collective-permute-done((f32[136,128]{1,0:T(8,128)S(1)}, f32[136,128]{1,0:T(8,128)S(1)}, u32[]{:S(2)}, u32[]{:S(2)}) %collective-permute-start.7) | collective-permute-done | bytes 69664 | tf_op jit(solution)/shard_map/ppermute | solution.py:357
  26.4 1.7 %collective-permute-start.9 = (f32[128,128]{1,0:T(8,128)S(1)}, f32[128,128]{1,0:T(8,128)S(1)}, u32[]{:S(2)}, u32[]{:S(2)}) collective-permute-start(f32[128,128]{1,0:T(8,128)S(1)} %get-tuple-element.137), channel_id=1, source_target_pairs={{0,2},{1,3},{2,0},{3,1},{4,6},{5,7},{6,4},{7,5},{8,10},{9,11},{10,... | collective-permute-start | bytes 196616 | tf_op jit(solution)/shard_map/ppermute | solution.py:357
  31.5 1.5 %collective-permute-done.8.refs_1_ = f32[128,128]{1,0:T(8,128)S(1)} collective-permute-done((f32[128,128]{1,0:T(8,128)S(1)}, f32[128,128]{1,0:T(8,128)S(1)}, u32[]{:S(2)}, u32[]{:S(2)}) %collective-permute-start.8) | collective-permute-done | bytes 65568 | tf_op jit(solution)/shard_map/ppermute | solution.py:357
  33.7 1.8 %shard_map.109 = (f32[264,128]{1,0:T(8,128)S(1)}, f32[264,128]{1,0:T(8,128)S(1)}, bf16[512,512]{1,0:T(8,128)(2,1)S(1)}, bf16[4,2,128,128]{3,2,1,0:T(8,128)(2,1)S...) custom-call(s32[3]{0:T(128)S(1)} %pad_add_fusion.scalar_ref, bf16[512,1024]{1,0:T(8,128)(2,1)S(1)} %copy-done, ...), custom_call_target="tpu_custom_call" | custom-call | tf_op jit(solution)/shard_map/pallas_call | solution.py:51
  36.0 1.7 %shard_map.110 = (f32[264,128]{1,0:T(8,128)S(1)}, f32[264,128]{1,0:T(8,128)S(1)}, bf16[512,512]{1,0:T(8,128)(2,1)S(1)}, bf16[4,2,128,128]{3,2,1,0:T(8,128)(2,1)S...) custom-call(s32[3]{0:T(128)S(1)} %pad_add_fusion.scalar_ref, bf16[512,1024]{1,0:T(8,128)(2,1)S(1)} %copy-done, ...), custom_call_target="tpu_custom_call" | custom-call | tf_op jit(solution)/shard_map/pallas_call | solution.py:51
  39.9 1.4 %collective-permute-start.14 = (f32[136,128]{1,0:T(8,128)S(1)}, f32[136,128]{1,0:T(8,128)S(1)}, u32[]{:S(2)}, u32[]{:S(2)}) collective-permute-start(f32[136,128]{1,0:T(8,128)S(1)} %get-tuple-element.178), channel_id=1, source_target_pairs={{0,2},{1,3},{2,0},{3,1},{4,6},{5,7},{6,4},{7,5},{8,10},{9,11},{10,... | collective-permute-start | bytes 208904 | tf_op jit(solution)/shard_map/ppermute | solution.py:357
  41.2 2.5 %shard_map.113 = (f32[512,256]{1,0:T(8,128)S(1)}, f32[512,256]{1,0:T(8,128)S(1)}, bf16[512,1024]{1,0:T(8,128)(2,1)}, bf16[512,1024]{1,0:T(8,128)(2,1)}) custom-call(s32[3]{0:T(128)S(1)} %pad_add_fusion.scalar_ref, bf16[512,1024]{1,0:T(8,128)(2,1)S(1)} %copy-done, bf16[512,512]{1,0:T(8,128)(2,1)S(1)} %get-tuple-element.122.refs_1_.refs_0_, ...), custom_call_target="tpu_custom_call" | custom-call | tf_op jit(solution)/shard_map/pallas_call | solution.py:51
  47.0 2.4 %shard_map.116 = (f32[512,256]{1,0:T(8,128)S(1)}, f32[512,256]{1,0:T(8,128)S(1)}, bf16[512,1024]{1,0:T(8,128)(2,1)}, bf16[512,1024]{1,0:T(8,128)(2,1)}) custom-call(s32[3]{0:T(128)S(1)} %pad_add_fusion.scalar_ref, bf16[512,1024]{1,0:T(8,128)(2,1)S(1)} %copy-done, ...), custom_call_target="tpu_custom_call", output_to_operand_aliasing={{2}: (11, {}), {3}: (12, {})} | custom-call | tf_op jit(solution)/shard_map/pallas_call | solution.py:51
  50.0 1.6 %collective-permute-start.19 = (f32[136,128]{1,0:T(8,128)S(1)}, f32[136,128]{1,0:T(8,128)S(1)}, u32[]{:S(2)}, u32[]{:S(2)}) collective-permute-start(f32[136,128]{1,0:T(8,128)S(1)} %get-tuple-element.184.refs_2_), channel_id=1, source_target_pairs={{0,8},{1,9},{2,10},{3,11},{4,12},{5,13},{6,14},{7,15},{8,0},{9,1},... | collective-permute-start | bytes 208904 | tf_op jit(solution)/shard_map/ppermute | solution.py:357
  52.2 1.4 %collective-permute-start.18 = (f32[136,128]{1,0:T(8,128)S(1)}, f32[136,128]{1,0:T(8,128)S(1)}, u32[]{:S(2)}, u32[]{:S(2)}) collective-permute-start(f32[136,128]{1,0:T(8,128)S(1)} %get-tuple-element.185.refs_12_), channel_id=1, source_target_pairs={{0,8},{1,9},{2,10},{3,11},{4,12},{5,13},{6,14},{7,15},{8,0},{9,1},... | collective-permute-start | bytes 208904 | tf_op jit(solution)/shard_map/ppermute | solution.py:357
  53.6 2.4 %shard_map.119 = (f32[512,256]{1,0:T(8,128)S(1)}, f32[512,256]{1,0:T(8,128)S(1)}, bf16[512,1024]{1,0:T(8,128)(2,1)}, bf16[512,1024]{1,0:T(8,128)(2,1)}) custom-call(s32[3]{0:T(128)S(1)} %pad_add_fusion.scalar_ref, bf16[512,1024]{1,0:T(8,128)(2,1)S(1)} %copy-done, ...), custom_call_target="tpu_custom_call", output_to_operand_aliasing={{2}: (11, {}), {3}: (12, {})} | custom-call | tf_op jit(solution)/shard_map/pallas_call | solution.py:51
  60.5 2.4 %shard_map.122 = (f32[512,256]{1,0:T(8,128)S(1)}, f32[512,256]{1,0:T(8,128)S(1)}, bf16[512,1024]{1,0:T(8,128)(2,1)}, bf16[512,1024]{1,0:T(8,128)(2,1)}) custom-call(s32[3]{0:T(128)S(1)} %pad_add_fusion.scalar_ref, bf16[512,1024]{1,0:T(8,128)(2,1)S(1)} %copy-done, ...), custom_call_target="tpu_custom_call", output_to_operand_aliasing={{2}: (11, {}), {3}: (12, {})} | custom-call | tf_op jit(solution)/shard_map/pallas_call | solution.py:51
  64.9 1.9 %shard_map.125 = (bf16[512,1024]{1,0:T(8,128)(2,1)}, bf16[512,1024]{1,0:T(8,128)(2,1)}) custom-call(s32[3]{0:T(128)S(1)} %pad_add_fusion.scalar_ref, bf16[512,512]{1,0:T(8,128)(2,1)S(1)} %get-tuple-element.122.refs_1_.refs_0_, bf16[512,512]{1,0:T(8,128)(2,1)S(1)} %get-tuple-element.123.refs_2_.refs_1_, f32[4,128,128]{2,1,0:T(8,128)S(1)} %get-tuple-element.206.refs_2_, ...), custom_call_target="tpu_custom_call" | custom-call | tf_op jit(solution)/shard_map/pallas_call | solution.py:51
  66.8 1.9 %shard_map.126 = (bf16[512,1024]{1,0:T(8,128)(2,1)}, bf16[512,1024]{1,0:T(8,128)(2,1)}) custom-call(s32[3]{0:T(128)S(1)} %pad_add_fusion.scalar_ref, bf16[512,512]{1,0:T(8,128)(2,1)S(1)} %get-tuple-element.112.refs_1_.refs_0_, bf16[512,512]{1,0:T(8,128)(2,1)S(1)} %get-tuple-element.113.refs_2_.refs_1_, ...), custom_call_target="tpu_custom_call", output_to_operand_aliasing={{0}: (13, {}), {1}: (14, {})} | custom-call | tf_op jit(solution)/shard_map/pallas_call | solution.py:51
  (63 shorter events, 22.6 us)
Async XLA Ops:
  3.1 3.0 %collective-permute-start.1 = (f32[264,128]{1,0:T(8,128)S(1)}, f32[264,128]{1,0:T(8,128)S(1)}, u32[]{:S(2)}, u32[]{:S(2)}) collective-permute-start(f32[264,128]{1,0:T(8,128)S(1)} %get-tuple-element.117), channel_id=1, source_target_pairs={{0,1},{1,0},{2,3},{3,2},{4,5},{5,4},{6,7},{7,6},{8,9},{9,8},{10,11... | collective-permute-start | bytes 405512 | tf_op jit(solution)/shard_map/ppermute | solution.py:357
  5.9 3.7 %collective-permute-start = (f32[264,128]{1,0:T(8,128)S(1)}, f32[264,128]{1,0:T(8,128)S(1)}, u32[]{:S(2)}, u32[]{:S(2)}) collective-permute-start(f32[264,128]{1,0:T(8,128)S(1)} %get-tuple-element.116), channel_id=1, source_target_pairs={{0,1},{1,0},{2,3},{3,2},{4,5},{5,4},{6,7},{7,6},{8,9},{9,8},{10,11... | collective-permute-start | bytes 405512 | tf_op jit(solution)/shard_map/ppermute | solution.py:357
  6.6 5.4 %collective-permute-start.3 = (f32[136,128]{1,0:T(8,128)S(1)}, f32[136,128]{1,0:T(8,128)S(1)}, u32[]{:S(2)}, u32[]{:S(2)}) collective-permute-start(f32[136,128]{1,0:T(8,128)S(1)} %get-tuple-element.121), channel_id=1, source_target_pairs={{0,2},{1,3},{2,0},{3,1},{4,6},{5,7},{6,4},{7,5},{8,10},{9,11},{10,... | collective-permute-start | bytes 208904 | tf_op jit(solution)/shard_map/ppermute | solution.py:357
  10.2 4.4 %collective-permute-start.2 = (f32[136,128]{1,0:T(8,128)S(1)}, f32[136,128]{1,0:T(8,128)S(1)}, u32[]{:S(2)}, u32[]{:S(2)}) collective-permute-start(f32[136,128]{1,0:T(8,128)S(1)} %get-tuple-element.120), channel_id=1, source_target_pairs={{0,2},{1,3},{2,0},{3,1},{4,6},{5,7},{6,4},{7,5},{8,10},{9,11},{10,... | collective-permute-start | bytes 208904 | tf_op jit(solution)/shard_map/ppermute | solution.py:357
  12.6 5.5 %collective-permute-start.5 = (f32[136,128]{1,0:T(8,128)S(1)}, f32[136,128]{1,0:T(8,128)S(1)}, u32[]{:S(2)}, u32[]{:S(2)}) collective-permute-start(f32[136,128]{1,0:T(8,128)S(1)} %shard_map.98.refs_2_.refs_0_), channel_id=1, source_target_pairs={{0,4},{1,5},{2,6},{3,7},{4,0},{5,1},{6,2},{7,3},{8,12},{9,13},{10,... | collective-permute-start | bytes 208904 | tf_op jit(solution)/shard_map/ppermute | solution.py:357
  15.2 6.1 %collective-permute-start.4 = (f32[136,128]{1,0:T(8,128)S(1)}, f32[136,128]{1,0:T(8,128)S(1)}, u32[]{:S(2)}, u32[]{:S(2)}) collective-permute-start(f32[136,128]{1,0:T(8,128)S(1)} %shard_map.99.refs_7_.refs_0_), channel_id=1, source_target_pairs={{0,4},{1,5},{2,6},{3,7},{4,0},{5,1},{6,2},{7,3},{8,12},{9,13},{10,... | collective-permute-start | bytes 208904 | tf_op jit(solution)/shard_map/ppermute | solution.py:357
  18.7 7.2 %collective-permute-start.7 = (f32[136,128]{1,0:T(8,128)S(1)}, f32[136,128]{1,0:T(8,128)S(1)}, u32[]{:S(2)}, u32[]{:S(2)}) collective-permute-start(f32[136,128]{1,0:T(8,128)S(1)} %get-tuple-element.129.refs_2_), channel_id=1, source_target_pairs={{0,8},{1,9},{2,10},{3,11},{4,12},{5,13},{6,14},{7,15},{8,0},{9,1},... | collective-permute-start | bytes 208904 | tf_op jit(solution)/shard_map/ppermute | solution.py:357
  21.9 6.3 %collective-permute-start.6 = (f32[136,128]{1,0:T(8,128)S(1)}, f32[136,128]{1,0:T(8,128)S(1)}, u32[]{:S(2)}, u32[]{:S(2)}) collective-permute-start(f32[136,128]{1,0:T(8,128)S(1)} %get-tuple-element.130.refs_7_), channel_id=1, source_target_pairs={{0,8},{1,9},{2,10},{3,11},{4,12},{5,13},{6,14},{7,15},{8,0},{9,1},... | collective-permute-start | bytes 208904 | tf_op jit(solution)/shard_map/ppermute | solution.py:357
  26.4 4.4 %collective-permute-start.9 = (f32[128,128]{1,0:T(8,128)S(1)}, f32[128,128]{1,0:T(8,128)S(1)}, u32[]{:S(2)}, u32[]{:S(2)}) collective-permute-start(f32[128,128]{1,0:T(8,128)S(1)} %get-tuple-element.137), channel_id=1, source_target_pairs={{0,2},{1,3},{2,0},{3,1},{4,6},{5,7},{6,4},{7,5},{8,10},{9,11},{10,... | collective-permute-start | bytes 196616 | tf_op jit(solution)/shard_map/ppermute | solution.py:357
  28.7 4.3 %collective-permute-start.8 = (f32[128,128]{1,0:T(8,128)S(1)}, f32[128,128]{1,0:T(8,128)S(1)}, u32[]{:S(2)}, u32[]{:S(2)}) collective-permute-start(f32[128,128]{1,0:T(8,128)S(1)} %get-tuple-element.136), channel_id=1, source_target_pairs={{0,2},{1,3},{2,0},{3,1},{4,6},{5,7},{6,4},{7,5},{8,10},{9,11},{10,... | collective-permute-start | bytes 196616 | tf_op jit(solution)/shard_map/ppermute | solution.py:357
  31.4 2.3 %collective-permute-start.11 = (f32[256,128]{1,0:T(8,128)S(1)}, f32[256,128]{1,0:T(8,128)S(1)}, u32[]{:S(2)}, u32[]{:S(2)}) collective-permute-start(f32[256,128]{1,0:T(8,128)S(1)} %get-tuple-element.147), channel_id=1, source_target_pairs={{0,1},{1,0},{2,3},{3,2},{4,5},{5,4},{6,7},{7,6},{8,9},{9,8},{10,11... | collective-permute-start | bytes 393224 | tf_op jit(solution)/shard_map/ppermute | solution.py:357
  33.6 2.4 %collective-permute-start.10 = (f32[256,128]{1,0:T(8,128)S(1)}, f32[256,128]{1,0:T(8,128)S(1)}, u32[]{:S(2)}, u32[]{:S(2)}) collective-permute-start(f32[256,128]{1,0:T(8,128)S(1)} %get-tuple-element.141), channel_id=1, source_target_pairs={{0,1},{1,0},{2,3},{3,2},{4,5},{5,4},{6,7},{7,6},{8,9},{9,8},{10,11... | collective-permute-start | bytes 393224 | tf_op jit(solution)/shard_map/ppermute | solution.py:357
  35.5 2.4 %collective-permute-start.13 = (f32[264,128]{1,0:T(8,128)S(1)}, f32[264,128]{1,0:T(8,128)S(1)}, u32[]{:S(2)}, u32[]{:S(2)}) collective-permute-start(f32[264,128]{1,0:T(8,128)S(1)} %get-tuple-element.173), channel_id=1, source_target_pairs={{0,1},{1,0},{2,3},{3,2},{4,5},{5,4},{6,7},{7,6},{8,9},{9,8},{10,11... | collective-permute-start | bytes 405512 | tf_op jit(solution)/shard_map/ppermute | solution.py:357
  37.8 1.5 %collective-permute-start.12 = (f32[264,128]{1,0:T(8,128)S(1)}, f32[264,128]{1,0:T(8,128)S(1)}, u32[]{:S(2)}, u32[]{:S(2)}) collective-permute-start(f32[264,128]{1,0:T(8,128)S(1)} %get-tuple-element.172), channel_id=1, source_target_pairs={{0,1},{1,0},{2,3},{3,2},{4,5},{5,4},{6,7},{7,6},{8,9},{9,8},{10,11... | collective-permute-start | bytes 405512 | tf_op jit(solution)/shard_map/ppermute | solution.py:357
  38.5 5.2 %collective-permute-start.15 = (f32[136,128]{1,0:T(8,128)S(1)}, f32[136,128]{1,0:T(8,128)S(1)}, u32[]{:S(2)}, u32[]{:S(2)}) collective-permute-start(f32[136,128]{1,0:T(8,128)S(1)} %get-tuple-element.179), channel_id=1, source_target_pairs={{0,2},{1,3},{2,0},{3,1},{4,6},{5,7},{6,4},{7,5},{8,10},{9,11},{10,... | collective-permute-start | bytes 208904 | tf_op jit(solution)/shard_map/ppermute | solution.py:357
  39.9 5.4 %collective-permute-start.14 = (f32[136,128]{1,0:T(8,128)S(1)}, f32[136,128]{1,0:T(8,128)S(1)}, u32[]{:S(2)}, u32[]{:S(2)}) collective-permute-start(f32[136,128]{1,0:T(8,128)S(1)} %get-tuple-element.178), channel_id=1, source_target_pairs={{0,2},{1,3},{2,0},{3,1},{4,6},{5,7},{6,4},{7,5},{8,10},{9,11},{10,... | collective-permute-start | bytes 208904 | tf_op jit(solution)/shard_map/ppermute | solution.py:357
  44.3 5.1 %collective-permute-start.17 = (f32[136,128]{1,0:T(8,128)S(1)}, f32[136,128]{1,0:T(8,128)S(1)}, u32[]{:S(2)}, u32[]{:S(2)}) collective-permute-start(f32[136,128]{1,0:T(8,128)S(1)} %shard_map.114.refs_2_.refs_0_), channel_id=1, source_target_pairs={{0,4},{1,5},{2,6},{3,7},{4,0},{5,1},{6,2},{7,3},{8,12},{9,13},{10,... | collective-permute-start | bytes 208904 | tf_op jit(solution)/shard_map/ppermute | solution.py:357
  45.8 5.8 %collective-permute-start.16 = (f32[136,128]{1,0:T(8,128)S(1)}, f32[136,128]{1,0:T(8,128)S(1)}, u32[]{:S(2)}, u32[]{:S(2)}) collective-permute-start(f32[136,128]{1,0:T(8,128)S(1)} %shard_map.115.refs_12_.refs_0_), channel_id=1, source_target_pairs={{0,4},{1,5},{2,6},{3,7},{4,0},{5,1},{6,2},{7,3},{8,12},{9,13},{10,... | collective-permute-start | bytes 208904 | tf_op jit(solution)/shard_map/ppermute | solution.py:357
  50.0 7.2 %collective-permute-start.19 = (f32[136,128]{1,0:T(8,128)S(1)}, f32[136,128]{1,0:T(8,128)S(1)}, u32[]{:S(2)}, u32[]{:S(2)}) collective-permute-start(f32[136,128]{1,0:T(8,128)S(1)} %get-tuple-element.184.refs_2_), channel_id=1, source_target_pairs={{0,8},{1,9},{2,10},{3,11},{4,12},{5,13},{6,14},{7,15},{8,0},{9,1},... | collective-permute-start | bytes 208904 | tf_op jit(solution)/shard_map/ppermute | solution.py:357
  52.2 6.8 %collective-permute-start.18 = (f32[136,128]{1,0:T(8,128)S(1)}, f32[136,128]{1,0:T(8,128)S(1)}, u32[]{:S(2)}, u32[]{:S(2)}) collective-permute-start(f32[136,128]{1,0:T(8,128)S(1)} %get-tuple-element.185.refs_12_), channel_id=1, source_target_pairs={{0,8},{1,9},{2,10},{3,11},{4,12},{5,13},{6,14},{7,15},{8,0},{9,1},... | collective-permute-start | bytes 208904 | tf_op jit(solution)/shard_map/ppermute | solution.py:357
  57.8 5.2 %collective-permute-start.21 = (f32[128,128]{1,0:T(8,128)S(1)}, f32[128,128]{1,0:T(8,128)S(1)}, u32[]{:S(2)}, u32[]{:S(2)}) collective-permute-start(f32[128,128]{1,0:T(8,128)S(1)} %get-tuple-element.197), channel_id=1, source_target_pairs={{0,2},{1,3},{2,0},{3,1},{4,6},{5,7},{6,4},{7,5},{8,10},{9,11},{10,... | collective-permute-start | bytes 196616 | tf_op jit(solution)/shard_map/ppermute | solution.py:357
  59.5 4.3 %collective-permute-start.20 = (f32[128,128]{1,0:T(8,128)S(1)}, f32[128,128]{1,0:T(8,128)S(1)}, u32[]{:S(2)}, u32[]{:S(2)}) collective-permute-start(f32[128,128]{1,0:T(8,128)S(1)} %get-tuple-element.196), channel_id=1, source_target_pairs={{0,2},{1,3},{2,0},{3,1},{4,6},{5,7},{6,4},{7,5},{8,10},{9,11},{10,... | collective-permute-start | bytes 196616 | tf_op jit(solution)/shard_map/ppermute | solution.py:357
  63.5 1.4 %collective-permute-start.23 = (f32[256,128]{1,0:T(8,128)S(1)}, f32[256,128]{1,0:T(8,128)S(1)}, u32[]{:S(2)}, u32[]{:S(2)}) collective-permute-start(f32[256,128]{1,0:T(8,128)S(1)} %get-tuple-element.207), channel_id=1, source_target_pairs={{0,1},{1,0},{2,3},{3,2},{4,5},{5,4},{6,7},{7,6},{8,9},{9,8},{10,11... | collective-permute-start | bytes 393224 | tf_op jit(solution)/shard_map/ppermute | solution.py:357
  64.5 2.4 %collective-permute-start.22 = (f32[256,128]{1,0:T(8,128)S(1)}, f32[256,128]{1,0:T(8,128)S(1)}, u32[]{:S(2)}, u32[]{:S(2)}) collective-permute-start(f32[256,128]{1,0:T(8,128)S(1)} %get-tuple-element.201), channel_id=1, source_target_pairs={{0,1},{1,0},{2,3},{3,2},{4,5},{5,4},{6,7},{7,6},{8,9},{9,8},{10,11... | collective-permute-start | bytes 393224 | tf_op jit(solution)/shard_map/ppermute | solution.py:357
  (2 other events, 10.0 us)

commit v4 on v3

--- a/solution.py
+++ b/solution.py
@@ -33,6 +33,14 @@
 
 def block(b):
     return slice(b * BLOCK, (b + 1) * BLOCK)
+
+
+def group_of(place):
+    return ((place[0] & 1) << 1) | ((place[0] >> 1) & 1)
+
+
+def position(place, backward):
+    return ~place[0] if backward else place[0]
 
 
 SMEM = pl.BlockSpec(memory_space=pltpu.SMEM)
@@ -89,7 +97,7 @@
     for out, first in ((own_ref, 0), (send_ref, 2 * k)):
         for r in range(2 * k):
             group, j = (first + r) // k, (first + r) % k
-            head = (group ^ place[0]) * k + j
+            head = (group ^ group_of(place)) * k + j
             out[cut(r), :] = terms_ref[head]
             out[pl.ds(2 * k * DH + r, 1), :] = keep_ref[pl.ds(head, 1), :]
         rest = 8 - 2 * k
@@ -99,35 +107,33 @@
 def take_in(place, k, mine_ref, other_ref, state_ref):
     for r in range(GROUPS * k):
         source = mine_ref if r < 2 * k else other_ref
-        state_ref[((r // k) ^ place[0]) * k + r % k] = source[cut(r % (2 * k)), :]
-
-
-def k1_body(k, head0, place, *refs):
+        state_ref[((r // k) ^ group_of(place)) * k + r % k] = source[cut(r % (2 * k)), :]
+
+
+def k1_body(k, head0, chunks, place, *refs):
     heads = GROUPS * k
-    loads = []
     if head0 == 0:
-        (decay_hbm, start_hbm, key_hbm, value_hbm, own_ref, send_ref, loc_ref, key_ref, value_ref, rows_ref, cols_ref,
-         terms_ref, keep_ref, sems, decay_ref, start_ref) = refs
+        decay_hbm, start_hbm, key_hbm, value_hbm, own_ref, send_ref, loc_ref, rows_ref, cols_ref = refs[:9]
+        copied = refs[9 : 9 + 2 * chunks]
+        terms_ref, keep_ref, decay_ref, start_ref, sems = refs[9 + 2 * chunks :]
         loads = [
-            pltpu.make_async_copy(decay_hbm, decay_ref, sems.at[2 * heads]),
-            pltpu.make_async_copy(start_hbm, start_ref, sems.at[2 * heads + 1]),
+            pltpu.make_async_copy(decay_hbm, decay_ref, sems.at[0]),
+            pltpu.make_async_copy(start_hbm, start_ref, sems.at[1]),
         ]
-    else:
-        (rows_ref, key_hbm, value_hbm, own_ref, send_ref, loc_ref, key_ref, value_ref,
-         terms_ref, keep_ref, sems) = refs
-    for j in range(heads):
-        for i, (source, target) in enumerate(((key_hbm, key_ref), (value_hbm, value_ref))):
-            loads.append(
-                pltpu.make_async_copy(source.at[:, cut(head0 + j)], target.at[:, cut(j)], sems.at[2 * j + i])
-            )
-    for load in loads:
-        load.start()
-    if head0 == 0:
+        for n, target in enumerate(copied):
+            source, first = (key_hbm, value_hbm)[n % 2], n // 2 * heads * DH
+            loads.append(pltpu.make_async_copy(source.at[:, first : first + heads * DH], target, sems.at[2 + n]))
+        for load in loads:
+            load.start()
         loads[0].wait()
         loads[1].wait()
         prepare(decay_ref, start_ref, rows_ref, cols_ref)
-    for load in loads[-2 * heads :]:
-        load.wait()
+        loads[2].wait()
+        loads[3].wait()
+        key_ref, value_ref = copied[:2]
+    else:
+        rows_ref, key_ref, value_ref, own_ref, send_ref, loc_ref, terms_ref, keep_ref = refs
+        loads = []
     for j in range(heads):
         head = head0 + j
         leave = rows_ref[16 + head : 17 + head, :]
@@ -141,6 +147,8 @@
         terms_ref[j] = k1 * terms[0] + terms[1]
         keep_ref[j : j + 1, :] = k0 * k1
     send_out(place, k, terms_ref, keep_ref, own_ref, send_ref)
+    for load in loads[4:]:
+        load.wait()
 
 
 def make_bias(rows_ref, cols_ref, bias_ref, turned_ref):
@@ -224,15 +232,26 @@
     send_out(place, k, terms_ref, keep_ref, own_ref, send_ref)
 
 
-def k4_body(head0, base, count, has_alias, place, query_ref, key_ref, value_ref, mixgrad_ref, attended_ref, grid_ref,
+def columns(ref, first, count):
+    return ref.at[:, first * DH : (first + count) * DH]
+
+
+def k4_body(head0, base, count, place, query_ref, key_ref, value_ref, mixgrad_ref, attended_ref, grid_ref,
             turned_ref, weighted_ref, states_ref, enter_ref, *refs):
-    key_part_ref, value_part_ref, attended_hbm, query_grad_hbm, query_grad_ref, sems = refs[2 * has_alias :]
+    later = head0 > 0
+    key_part_ref, value_part_ref, query_grad_ref, attended_hbm, query_grad_hbm, sems = refs[3 * later :]
     inner0 = head0 - base
-    ours = slice(head0 * DH, (head0 + count) * DH)
-    attend = pltpu.make_async_copy(
-        attended_ref.at[:, inner0 * DH : (inner0 + count) * DH], attended_hbm.at[:, ours], sems.at[0]
-    )
-    attend.start()
+    copies = [
+        pltpu.make_async_copy(
+            columns(attended_ref, inner0, count), columns(attended_hbm, head0, count), sems.at[0]
+        )
+    ]
+    if later:
+        copies.append(
+            pltpu.make_async_copy(refs[0], columns(query_grad_hbm, head0 - count, count), sems.at[1])
+        )
+    for copy in copies:
+        copy.start()
     for j in range(count):
         head = head0 + j
         inner = head - base
@@ -247,19 +266,41 @@
             turned = (mm(value, mixgrad, NT) * turned_ref[j, b]).astype(BF16)
             key_part_ref[at, cut(j)] = mm(turned, query_ref[at, cut(head)])
             value_part_ref[at, cut(j)] = mm(weighted_ref[j, b], mixgrad)
-    grads = pltpu.make_async_copy(query_grad_ref, query_grad_hbm.at[:, ours], sems.at[1])
-    grads.start()
-    attend.wait()
-    grads.wait()
-
-
-def k5_body(k, head0, pieces, per, has_alias, place, key_ref, value_ref, back_ref, rows_ref, mine_ref, other_ref,
-            *refs):
+    for copy in copies:
+        copy.wait()
+
+
+def k5_body(k, head0, pieces, per, chunks, place, key_ref, value_ref, back_ref, rows_ref, mine_ref, other_ref, *refs):
+    heads = GROUPS * k
     key_parts, value_parts, leaves = refs[:pieces], refs[pieces : 2 * pieces], refs[2 * pieces : 3 * pieces]
-    key_grad_hbm, value_grad_hbm, key_grad_ref, value_grad_ref, state_ref, sems = refs[3 * pieces + 2 * has_alias :]
+    refs = refs[3 * pieces :]
+    first, last = head0 == 0, head0 == (chunks - 1) * heads
+    copies = []
+    if first:
+        done_ref, refs = refs[0], refs[2:]
+    earlier, refs = refs[: 2 * (chunks - 1) * last], refs[2 * (chunks - 1) * last :]
+    if last:
+        key_grad_hbm, value_grad_hbm, refs = refs[0], refs[1], refs[2:]
+    else:
+        key_grad_ref, value_grad_ref, refs = refs[0], refs[1], refs[2:]
+    if first:
+        query_grad_hbm, refs = refs[0], refs[1:]
+    state_ref, sems, refs = refs[0], refs[1], refs[2:]
+    if last:
+        key_grad_ref, value_grad_ref = refs
+
+    def ship(source, target):
+        copy = pltpu.make_async_copy(source, target, sems.at[len(copies)])
+        copy.start()
+        copies.append(copy)
+
+    if first:
+        ship(done_ref, columns(query_grad_hbm, chunks * heads - per, per))
+    for n in range(0, len(earlier), 2):
+        ship(earlier[n], columns(key_grad_hbm, n // 2 * heads, heads))
+        ship(earlier[n + 1], columns(value_grad_hbm, n // 2 * heads, heads))
     take_in(place, k, mine_ref, other_ref, state_ref)
-    copies = []
-    for j in range(GROUPS * k):
+    for j in range(heads):
         head = head0 + j
         p, i = j // per, j % per
         k0, k1 = keeps(rows_ref, head)
@@ -275,10 +316,9 @@
             value_grad_ref[at, cut(j)] = (
                 value_parts[p][at, cut(i)] + mm(key_ref[at, cut(j)], low) * leave
             ).astype(BF16)
-        for n, (source, target) in enumerate(((key_grad_ref, key_grad_hbm), (value_grad_ref, value_grad_hbm))):
-            copy = pltpu.make_async_copy(source.at[:, cut(j)], target.at[:, cut(head)], sems.at[2 * j + n])
-            copy.start()
-            copies.append(copy)
+        if last:
+            ship(columns(key_grad_ref, j, 1), columns(key_grad_hbm, head, 1))
+            ship(columns(value_grad_ref, j, 1), columns(value_grad_hbm, head, 1))
     for copy in copies:
         copy.wait()
 
@@ -305,7 +345,7 @@
 
 
 def c1_body(turn, k, place, own_ref, got_ref, keep_ref, send_ref):
-    later = (place[turn] & 1) == 1
+    later = (position(place, turn) & 1) == 1
     for out in (keep_ref, send_ref):
         out[k * DH :, :] = jnp.ones((8, DH), F32)
     for j in range(2 * k):
@@ -313,7 +353,7 @@
 
 
 def c2_body(turn, k, place, own_ref, got_ref, total_ref):
-    later = (place[turn] & 2) == 2
+    later = (position(place, turn) & 2) == 2
     total_ref[k * DH :, :] = jnp.ones((8, DH), F32)
     for j in range(k):
         put(total_ref, k, j, joined(later, got_ref, own_ref, k, j))
@@ -323,7 +363,7 @@
     total_ref, got_ref = refs[:2]
     prefix_ref = None if first else refs[2]
     new_total_ref, new_prefix_ref = refs[-2:]
-    later = (place[turn] & bit) == bit
+    later = (position(place, turn) & bit) == bit
     for out in (new_total_ref, new_prefix_ref):
         out[k * DH :, :] = jnp.ones((8, DH), F32)
     for j in range(k):
@@ -335,8 +375,8 @@
     got_ref = refs[0]
     prefix_ref = None if first else refs[1]
     own_ref, chip_ref, mine_ref, send_ref = refs[-4:]
-    later = (place[turn] & bit) == bit
-    upper = (place[turn] & 2) == 2
+    later = (position(place, turn) & bit) == bit
+    upper = (position(place, turn) & 2) == 2
     for j in range(k):
         at, one = cut(j), slice(k * DH + j, k * DH + j + 1)
         prefix, _ = before(later, got_ref, prefix_ref, k, j)
@@ -345,7 +385,7 @@
 
 
 def c4_body(turn, k, place, half_ref, got_half_ref, own_ref, got_ref, mine_ref, send_ref):
-    later = (place[turn] & 1) == 1
+    later = (position(place, turn) & 1) == 1
     for j in range(2 * k):
         at, one = cut(j), slice(2 * k * DH + j, 2 * k * DH + j + 1)
         chip = half_ref[cut(j), :] if j < k else got_half_ref[cut(j - k), :]
@@ -416,8 +456,7 @@
     tokens, width = query_rows.shape
     count = lax.axis_size("seq")
     seat = lax.axis_index("seq")
-    place = jnp.stack([((seat & 1) << 1) | ((seat >> 1) & 1), seat, count - 1 - seat])
-    call = Order(place)
+    call = Order(seat.reshape(1))
     heads = all_heads // CHUNKS
     k = heads // GROUPS
     per = heads // PIECES
@@ -432,25 +471,22 @@
     mask = ((2, BLOCK, BLOCK), F32)
     scratch_terms = (pltpu.VMEM((heads, DH, DH), F32), pltpu.VMEM((8, DH), F32))
 
-    own, send, loc, keys, values, scans = [], [], [], [], [], []
+    loc, scans = [], []
     for c in chunks:
-        outs = (message, message, states, chunk_bf16, chunk_bf16)
-        scratch = scratch_terms + (dma((2 * heads + 2,)),)
+        outs = (message, message, states)
+        scratch = scratch_terms
+        body = functools.partial(k1_body, k, c * heads, CHUNKS)
         if c == 0:
-            outs += (((32, tokens), F32), ((tokens, DH), F32))
-            scratch += (pltpu.VMEM(log_decay.shape, F32), pltpu.VMEM((1, tokens), jnp.int32))
-            inside, outside = (), (log_decay, run_start.reshape(1, tokens), key_rows, value_rows)
+            outs += (((32, tokens), F32), ((tokens, DH), F32)) + (chunk_bf16,) * (2 * CHUNKS)
+            scratch += (pltpu.VMEM(log_decay.shape, F32), pltpu.VMEM((1, tokens), jnp.int32), dma((2 * CHUNKS + 2,)))
+            outside = (log_decay, run_start.reshape(1, tokens), key_rows, value_rows)
+            out = call(body, (), outs, outside=outside, scratch=scratch)
+            rows, cols = out[3:5]
+            keys, values = out[5::2], out[6::2]
         else:
-            inside, outside = (rows,), (key_rows, value_rows)
-        out = call(functools.partial(k1_body, k, c * heads), inside, outs, outside=outside, scratch=scratch)
-        if c == 0:
-            rows, cols = out[5:]
-        own.append(out[0])
-        send.append(out[1])
+            out = call(body, (rows, keys[c], values[c]), outs, scratch=scratch)
         loc.append(out[2])
-        keys.append(out[3])
-        values.append(out[4])
-        scans.append(scan_devices(call, out[0], out[1], 1, k, count))
+        scans.append(scan_devices(call, out[0], out[1], False, k, count))
 
     forward = []
 
@@ -478,7 +514,7 @@
             scratch=scratch_terms + (pltpu.VMEM((heads, DH, DH), F32),),
         )
         middle.append(out)
-        scans.append(scan_devices(call, out[0], out[1], 2, k, count))
+        scans.append(scan_devices(call, out[0], out[1], True, k, count))
 
     backward = []
 
@@ -488,31 +524,38 @@
         f = forward[n]
         backward.append(
             call(
-                functools.partial(k4_body, n * per, c * heads, per, int(n > 0)),
-                (query_rows, keys[c], values[c], mixgrad, attended, f[1], f[2], f[3], states_low, f[5]),
-                (piece_f32, piece_f32, flat, flat),
-                outside=tuple(backward[-1][2:]) if backward else (),
-                aliases={0: 2, 1: 3} if backward else None,
-                scratch=(pltpu.VMEM((tokens, per * DH), BF16), dma((2,))),
+                functools.partial(k4_body, n * per, c * heads, per),
+                (query_rows, keys[c], values[c], mixgrad, attended, f[1], f[2], f[3], states_low, f[5])
+                + ((backward[-1][2],) if n else ()),
+                (piece_f32, piece_f32, ((tokens, per * DH), BF16), flat, flat),
+                outside=tuple(backward[-1][3:]) if n else (),
+                aliases={0: 3, 1: 4} if n else None,
+                scratch=(dma((2,)),),
             )
         )
 
     results = drive(scans, [functools.partial(k4, n) for n in fillers])
+    attended, query_grad = backward[-1][3:]
     grads = ()
     for c, (mine, other) in enumerate(results):
+        first, last = c == 0, c == CHUNKS - 1
         back = backward[c * PIECES : (c + 1) * PIECES]
         mid = forward[c * PIECES : (c + 1) * PIECES]
-        grads = call(
-            functools.partial(k5_body, k, c * heads, PIECES, per, int(c > 0)),
+        out = call(
+            functools.partial(k5_body, k, c * heads, PIECES, per, CHUNKS),
             (keys[c], values[c], middle[c][4], rows, mine, other)
-            + tuple(b[0] for b in back) + tuple(b[1] for b in back) + tuple(f[6] for f in mid),
-            (flat, flat),
-            outside=tuple(grads),
-            aliases={0: 0, 1: 1} if grads else None,
-            scratch=(pltpu.VMEM((tokens, heads * DH), BF16),) * 2
-            + (pltpu.VMEM((heads, DH, DH), F32), dma((2 * heads,))),
+            + tuple(b[0] for b in back) + tuple(b[1] for b in back) + tuple(f[6] for f in mid)
+            + ((backward[-1][2],) if first else ()) + (grads if last else ()),
+            ((flat,) * 2 if last else (chunk_bf16,) * 2) + ((flat,) if first else ()),
+            outside=(query_grad,) if first else (),
+            aliases={0: 2} if first else None,
+            scratch=(pltpu.VMEM((heads, DH, DH), F32), dma((2 * heads + 2 * CHUNKS,)))
+            + ((pltpu.VMEM((tokens, heads * DH), BF16),) * 2 if last else ()),
         )
-    return (*backward[-1][2:], *grads)
+        if first:
+            query_grad = out[2]
+        grads = grads + tuple(out[:2])
+    return attended, query_grad, out[0], out[1]
 
 
 def solution(mesh):

time: 68.9 us -> 57.3 us (0.83)
  Pallas kernels: 38.1 us -> 18.2 us
  waiting for transfers between devices: 5 us -> 10 us
  starting transfers between devices: 24.5 us -> 27.9 us
    pallas_call x34, Pallas kernels: 38.1 us -> 18.2 us  [run(): pl.pallas_call(kernel, in_specs=[SMEM] + [VMEM] * len(inside) + [HBM] * l...]
    ppermute x24, waiting for transfers between devices: 5 us -> 10 us  [exchange(): return lax.ppermute(x, 'seq', [(i, i ^ bit) for i in range(count)])]
    ppermute x24, starting transfers between devices: 24.5 us -> 27.9 us  [exchange(): return lax.ppermute(x, 'seq', [(i, i ^ bit) for i in range(count)])]
  transfers between devices with their start and end apart: 24 -> 24, of which waited for: 6 -> 10; matrix products, arithmetic and copies ran while one was open for 0% -> 0% of each run, Pallas kernels for 49% -> 26%
where the time goes in v4:
time: 57.3 us; the launch traced here: 57.1 us
  starting transfers between devices  27.9 us (49%)
  Pallas kernels  18.2 us (32%)
  waiting for transfers between devices  10 us (17%)
  between operations  0.93 us (2%)
    ppermute x24, starting transfers between devices, exchange(): return lax.ppermute(x, 'seq', [(i, i ^ bit) for i in range(count)])  27.9 us
    pallas_call x34, Pallas kernels, run(): pl.pallas_call(kernel, in_specs=[SMEM] + [VMEM] * len(inside) + [HBM] * l...  18.2 us
    ppermute x24, waiting for transfers between devices, exchange(): return lax.ppermute(x, 'seq', [(i, i ^ bit) for i in range(count)])  10 us
  transfers between devices with their start and end apart: 24, of which 10 were waited for; matrix products, arithmetic and copies ran while one was open for 0% of the time, Pallas kernels for 26%

profile of v4, /device:TPU:0, one launch (start us, length us, event | category | flops | bytes accessed | tf_op | source)
XLA Modules:
  0.0 57.1 jit_solution(10083134684104827508)
XLA Ops:
  0.6 1.7 %shard_map.93 = (f32[264,128]{1,0:T(8,128)S(1)}, f32[264,128]{1,0:T(8,128)S(1)}, f32[4,128,128]{2,1,0:T(8,128)S(1)}, f32[32,512]{1,0:T(8,128)S(1)}, f32[512,128]...) custom-call(s32[1]{0:T(128)} %bitcast.scalar_ref, ...), custom_call_target="tpu_custom_call" | custom-call | tf_op jit(solution)/shard_map/pallas_call | solution.py:59
  3.9 2.9 %collective-permute-start.3 = (f32[136,128]{1,0:T(8,128)S(1)}, f32[136,128]{1,0:T(8,128)S(1)}, u32[]{:S(2)}, u32[]{:S(2)}) collective-permute-start(f32[136,128]{1,0:T(8,128)S(1)} %get-tuple-element.126), channel_id=1, source_target_pairs={{0,2},{1,3},{2,0},{3,1},{4,6},{5,7},{6,4},{7,5},{8,10},{9,11},{10,... | collective-permute-start | bytes 208904 | tf_op jit(solution)/shard_map/ppermute | solution.py:397
  9.4 2.2 %collective-permute-start.5 = (f32[136,128]{1,0:T(8,128)S(1)}, f32[136,128]{1,0:T(8,128)S(1)}, u32[]{:S(2)}, u32[]{:S(2)}) collective-permute-start(f32[136,128]{1,0:T(8,128)S(1)} %shard_map.98.refs_2_.refs_0_), channel_id=1, source_target_pairs={{0,4},{1,5},{2,6},{3,7},{4,0},{5,1},{6,2},{7,3},{8,12},{9,13},{10,... | collective-permute-start | bytes 208904 | tf_op jit(solution)/shard_map/ppermute | solution.py:397
  11.6 1.3 %collective-permute-start.4 = (f32[136,128]{1,0:T(8,128)S(1)}, f32[136,128]{1,0:T(8,128)S(1)}, u32[]{:S(2)}, u32[]{:S(2)}) collective-permute-start(f32[136,128]{1,0:T(8,128)S(1)} %shard_map.99.refs_7_.refs_0_), channel_id=1, source_target_pairs={{0,4},{1,5},{2,6},{3,7},{4,0},{5,1},{6,2},{7,3},{8,12},{9,13},{10,... | collective-permute-start | bytes 208904 | tf_op jit(solution)/shard_map/ppermute | solution.py:397
  14.2 2.8 %collective-permute-start.7 = (f32[136,128]{1,0:T(8,128)S(1)}, f32[136,128]{1,0:T(8,128)S(1)}, u32[]{:S(2)}, u32[]{:S(2)}) collective-permute-start(f32[136,128]{1,0:T(8,128)S(1)} %get-tuple-element.134.refs_2_), channel_id=1, source_target_pairs={{0,8},{1,9},{2,10},{3,11},{4,12},{5,13},{6,14},{7,15},{8,0},{9,1},... | collective-permute-start | bytes 208904 | tf_op jit(solution)/shard_map/ppermute | solution.py:397
  17.0 1.6 %collective-permute-start.6 = (f32[136,128]{1,0:T(8,128)S(1)}, f32[136,128]{1,0:T(8,128)S(1)}, u32[]{:S(2)}, u32[]{:S(2)}) collective-permute-start(f32[136,128]{1,0:T(8,128)S(1)} %get-tuple-element.135.refs_7_), channel_id=1, source_target_pairs={{0,8},{1,9},{2,10},{3,11},{4,12},{5,13},{6,14},{7,15},{8,0},{9,1},... | collective-permute-start | bytes 208904 | tf_op jit(solution)/shard_map/ppermute | solution.py:397
  19.4 1.9 %collective-permute-done.7.refs_0_ = f32[136,128]{1,0:T(8,128)S(1)} collective-permute-done((f32[136,128]{1,0:T(8,128)S(1)}, f32[136,128]{1,0:T(8,128)S(1)}, u32[]{:S(2)}, u32[]{:S(2)}) %collective-permute-start.7) | collective-permute-done | bytes 69664 | tf_op jit(solution)/shard_map/ppermute | solution.py:397
  21.4 1.8 %collective-permute-start.9 = (f32[128,128]{1,0:T(8,128)S(1)}, f32[128,128]{1,0:T(8,128)S(1)}, u32[]{:S(2)}, u32[]{:S(2)}) collective-permute-start(f32[128,128]{1,0:T(8,128)S(1)} %get-tuple-element.142), channel_id=1, source_target_pairs={{0,2},{1,3},{2,0},{3,1},{4,6},{5,7},{6,4},{7,5},{8,10},{9,11},{10,... | collective-permute-start | bytes 196616 | tf_op jit(solution)/shard_map/ppermute | solution.py:397
  23.2 2.2 %collective-permute-start.8 = (f32[128,128]{1,0:T(8,128)S(1)}, f32[128,128]{1,0:T(8,128)S(1)}, u32[]{:S(2)}, u32[]{:S(2)}) collective-permute-start(f32[128,128]{1,0:T(8,128)S(1)} %get-tuple-element.141), channel_id=1, source_target_pairs={{0,2},{1,3},{2,0},{3,1},{4,6},{5,7},{6,4},{7,5},{8,10},{9,11},{10,... | collective-permute-start | bytes 196616 | tf_op jit(solution)/shard_map/ppermute | solution.py:397
  26.4 1.3 %collective-permute-done.8.refs_1_ = f32[128,128]{1,0:T(8,128)S(1)} collective-permute-done((f32[128,128]{1,0:T(8,128)S(1)}, f32[128,128]{1,0:T(8,128)S(1)}, u32[]{:S(2)}, u32[]{:S(2)}) %collective-permute-start.8) | collective-permute-done | bytes 65568 | tf_op jit(solution)/shard_map/ppermute | solution.py:397
  27.8 1.2 %shard_map.109 = (f32[264,128]{1,0:T(8,128)S(1)}, f32[264,128]{1,0:T(8,128)S(1)}, bf16[512,512]{1,0:T(8,128)(2,1)S(1)}, bf16[4,2,128,128]{3,2,1,0:T(8,128)(2,1)S...) custom-call(s32[1]{0:T(128)} %bitcast.scalar_ref, bf16[512,1024]{1,0:T(8,128)(2,1)S(1)} %copy-done, ...), custom_call_target="tpu_custom_call" | custom-call | tf_op jit(solution)/shard_map/pallas_call | solution.py:59
  31.0 2.1 %collective-permute-start.15 = (f32[136,128]{1,0:T(8,128)S(1)}, f32[136,128]{1,0:T(8,128)S(1)}, u32[]{:S(2)}, u32[]{:S(2)}) collective-permute-start(f32[136,128]{1,0:T(8,128)S(1)} %get-tuple-element.185), channel_id=1, source_target_pairs={{0,2},{1,3},{2,0},{3,1},{4,6},{5,7},{6,4},{7,5},{8,10},{9,11},{10,... | collective-permute-start | bytes 208904 | tf_op jit(solution)/shard_map/ppermute | solution.py:397
  33.1 1.3 %collective-permute-start.14 = (f32[136,128]{1,0:T(8,128)S(1)}, f32[136,128]{1,0:T(8,128)S(1)}, u32[]{:S(2)}, u32[]{:S(2)}) collective-permute-start(f32[136,128]{1,0:T(8,128)S(1)} %get-tuple-element.184), channel_id=1, source_target_pairs={{0,2},{1,3},{2,0},{3,1},{4,6},{5,7},{6,4},{7,5},{8,10},{9,11},{10,... | collective-permute-start | bytes 208904 | tf_op jit(solution)/shard_map/ppermute | solution.py:397
  34.4 1.7 %shard_map.113 = (f32[512,256]{1,0:T(8,128)S(1)}, f32[512,256]{1,0:T(8,128)S(1)}, bf16[512,256]{1,0:T(8,128)(2,1)S(1)}, bf16[512,1024]{1,0:T(8,128)(2,1)}, bf16[512,1024]{1,0:T(8,128)(2,1)}) custom-call(s32[1]{0:T(128)} %bitcast.scalar_ref, bf16[512,1024]{1,0:T(8,128)(2,1)S(1)} %copy-done, bf16[512,512]{1,0:T(8,128)(2,1)S(1)} %get-tuple-element.127.refs_1_.refs_0_, ...), custom_call_target="tpu_custom_call" | custom-call | tf_op jit(solution)/shard_map/pallas_call | solution.py:59
  38.3 1.9 %shard_map.116 = (f32[512,256]{1,0:T(8,128)S(1)}, f32[512,256]{1,0:T(8,128)S(1)}, bf16[512,256]{1,0:T(8,128)(2,1)S(1)}, bf16[512,1024]{1,0:T(8,128)(2,1)}, bf16[512,1024]{1,0:T(8,128)(2,1)}) custom-call(s32[1]{0:T(128)} %bitcast.scalar_ref, bf16[512,1024]{1,0:T(8,128)(2,1)S(1)} %copy-done, ...), custom_call_target="tpu_custom_call", output_to_operand_aliasing={{3}: (12, {}), {4}: (13, {})} | custom-call | tf_op jit(solution)/shard_map/pallas_call | solution.py:59
  40.9 1.7 %collective-permute-start.19 = (f32[136,128]{1,0:T(8,128)S(1)}, f32[136,128]{1,0:T(8,128)S(1)}, u32[]{:S(2)}, u32[]{:S(2)}) collective-permute-start(f32[136,128]{1,0:T(8,128)S(1)} %get-tuple-element.191.refs_2_), channel_id=1, source_target_pairs={{0,8},{1,9},{2,10},{3,11},{4,12},{5,13},{6,14},{7,15},{8,0},{9,1},... | collective-permute-start | bytes 208904 | tf_op jit(solution)/shard_map/ppermute | solution.py:397
  42.6 1.4 %collective-permute-start.18 = (f32[136,128]{1,0:T(8,128)S(1)}, f32[136,128]{1,0:T(8,128)S(1)}, u32[]{:S(2)}, u32[]{:S(2)}) collective-permute-start(f32[136,128]{1,0:T(8,128)S(1)} %get-tuple-element.192.refs_13_), channel_id=1, source_target_pairs={{0,8},{1,9},{2,10},{3,11},{4,12},{5,13},{6,14},{7,15},{8,0},{9,1},... | collective-permute-start | bytes 208904 | tf_op jit(solution)/shard_map/ppermute | solution.py:397
  44.0 1.7 %shard_map.119 = (f32[512,256]{1,0:T(8,128)S(1)}, f32[512,256]{1,0:T(8,128)S(1)}, bf16[512,256]{1,0:T(8,128)(2,1)S(1)}, bf16[512,1024]{1,0:T(8,128)(2,1)}, bf16[512,1024]{1,0:T(8,128)(2,1)}) custom-call(s32[1]{0:T(128)} %bitcast.scalar_ref, bf16[512,1024]{1,0:T(8,128)(2,1)S(1)} %copy-done, ...), custom_call_target="tpu_custom_call", output_to_operand_aliasing={{3}: (12, {}), {4}: (13, {})} | custom-call | tf_op jit(solution)/shard_map/pallas_call | solution.py:59
  45.7 2.2 %collective-permute-done.19.refs_0_ = f32[136,128]{1,0:T(8,128)S(1)} collective-permute-done((f32[136,128]{1,0:T(8,128)S(1)}, f32[136,128]{1,0:T(8,128)S(1)}, u32[]{:S(2)}, u32[]{:S(2)}) %collective-permute-start.19) | collective-permute-done | bytes 69664 | tf_op jit(solution)/shard_map/ppermute | solution.py:397
  48.0 1.5 %collective-permute-start.20 = (f32[128,128]{1,0:T(8,128)S(1)}, f32[128,128]{1,0:T(8,128)S(1)}, u32[]{:S(2)}, u32[]{:S(2)}) collective-permute-start(f32[128,128]{1,0:T(8,128)S(1)} %get-tuple-element.203), channel_id=1, source_target_pairs={{0,2},{1,3},{2,0},{3,1},{4,6},{5,7},{6,4},{7,5},{8,10},{9,11},{10,... | collective-permute-start | bytes 196616 | tf_op jit(solution)/shard_map/ppermute | solution.py:397
  49.5 1.5 %collective-permute-start.22 = (f32[128,128]{1,0:T(8,128)S(1)}, f32[128,128]{1,0:T(8,128)S(1)}, u32[]{:S(2)}, u32[]{:S(2)}) collective-permute-start(f32[128,128]{1,0:T(8,128)S(1)} %get-tuple-element.213), channel_id=1, source_target_pairs={{0,2},{1,3},{2,0},{3,1},{4,6},{5,7},{6,4},{7,5},{8,10},{9,11},{10,... | collective-permute-start | bytes 196616 | tf_op jit(solution)/shard_map/ppermute | solution.py:397
  51.0 1.9 %shard_map.122 = (f32[512,256]{1,0:T(8,128)S(1)}, f32[512,256]{1,0:T(8,128)S(1)}, bf16[512,256]{1,0:T(8,128)(2,1)S(1)}, bf16[512,1024]{1,0:T(8,128)(2,1)}, bf16[512,1024]{1,0:T(8,128)(2,1)}) custom-call(s32[1]{0:T(128)} %bitcast.scalar_ref, bf16[512,1024]{1,0:T(8,128)(2,1)S(1)} %copy-done, ...), custom_call_target="tpu_custom_call", output_to_operand_aliasing={{3}: (12, {}), {4}: (13, {})} | custom-call | tf_op jit(solution)/shard_map/pallas_call | solution.py:59
  54.4 1.3 %shard_map.125 = (bf16[512,512]{1,0:T(8,128)(2,1)S(1)}, bf16[512,512]{1,0:T(8,128)(2,1)S(1)}, bf16[512,1024]{1,0:T(8,128)(2,1)}) custom-call(s32[1]{0:T(128)} %bitcast.scalar_ref, bf16[512,512]{1,0:T(8,128)(2,1)S(1)} %get-tuple-element.127.refs_1_.refs_0_, bf16[512,512]{1,0:T(8,128)(2,1)S(1)} %get-tuple-element.128.refs_2_.refs_1_, ...), custom_call_target="tpu_custom_call", output_to_operand_aliasing={{2}: (14, {})} | custom-call | tf_op jit(solution)/shard_map/pallas_call | solution.py:59
  55.6 1.4 %shard_map.126 = (bf16[512,1024]{1,0:T(8,128)(2,1)}, bf16[512,1024]{1,0:T(8,128)(2,1)}) custom-call(s32[1]{0:T(128)} %bitcast.scalar_ref, bf16[512,512]{1,0:T(8,128)(2,1)S(1)} %get-tuple-element.115.refs_1_.refs_0_, bf16[512,512]{1,0:T(8,128)(2,1)S(1)} %get-tuple-element.116.refs_2_.refs_1_, f32[4,128,128]{2,1,0:T(8,128)S(1)} %get-tuple-element.216.refs_2_, ...), custom_call_target="tpu_custom_call" | custom-call | tf_op jit(solution)/shard_map/pallas_call | solution.py:59
  (62 shorter events, 13.7 us)
Async XLA Ops:
  2.3 1.5 %collective-permute-start.1 = (f32[264,128]{1,0:T(8,128)S(1)}, f32[264,128]{1,0:T(8,128)S(1)}, u32[]{:S(2)}, u32[]{:S(2)}) collective-permute-start(f32[264,128]{1,0:T(8,128)S(1)} %get-tuple-element.122), channel_id=1, source_target_pairs={{0,1},{1,0},{2,3},{3,2},{4,5},{5,4},{6,7},{7,6},{8,9},{9,8},{10,11... | collective-permute-start | bytes 405512 | tf_op jit(solution)/shard_map/ppermute | solution.py:397
  3.2 3.6 %collective-permute-start = (f32[264,128]{1,0:T(8,128)S(1)}, f32[264,128]{1,0:T(8,128)S(1)}, u32[]{:S(2)}, u32[]{:S(2)}) collective-permute-start(f32[264,128]{1,0:T(8,128)S(1)} %get-tuple-element.121), channel_id=1, source_target_pairs={{0,1},{1,0},{2,3},{3,2},{4,5},{5,4},{6,7},{7,6},{8,9},{9,8},{10,11... | collective-permute-start | bytes 405512 | tf_op jit(solution)/shard_map/ppermute | solution.py:397
  3.9 5.5 %collective-permute-start.3 = (f32[136,128]{1,0:T(8,128)S(1)}, f32[136,128]{1,0:T(8,128)S(1)}, u32[]{:S(2)}, u32[]{:S(2)}) collective-permute-start(f32[136,128]{1,0:T(8,128)S(1)} %get-tuple-element.126), channel_id=1, source_target_pairs={{0,2},{1,3},{2,0},{3,1},{4,6},{5,7},{6,4},{7,5},{8,10},{9,11},{10,... | collective-permute-start | bytes 208904 | tf_op jit(solution)/shard_map/ppermute | solution.py:397
  6.8 4.7 %collective-permute-start.2 = (f32[136,128]{1,0:T(8,128)S(1)}, f32[136,128]{1,0:T(8,128)S(1)}, u32[]{:S(2)}, u32[]{:S(2)}) collective-permute-start(f32[136,128]{1,0:T(8,128)S(1)} %get-tuple-element.125), channel_id=1, source_target_pairs={{0,2},{1,3},{2,0},{3,1},{4,6},{5,7},{6,4},{7,5},{8,10},{9,11},{10,... | collective-permute-start | bytes 208904 | tf_op jit(solution)/shard_map/ppermute | solution.py:397
  9.4 4.8 %collective-permute-start.5 = (f32[136,128]{1,0:T(8,128)S(1)}, f32[136,128]{1,0:T(8,128)S(1)}, u32[]{:S(2)}, u32[]{:S(2)}) collective-permute-start(f32[136,128]{1,0:T(8,128)S(1)} %shard_map.98.refs_2_.refs_0_), channel_id=1, source_target_pairs={{0,4},{1,5},{2,6},{3,7},{4,0},{5,1},{6,2},{7,3},{8,12},{9,13},{10,... | collective-permute-start | bytes 208904 | tf_op jit(solution)/shard_map/ppermute | solution.py:397
  11.6 5.4 %collective-permute-start.4 = (f32[136,128]{1,0:T(8,128)S(1)}, f32[136,128]{1,0:T(8,128)S(1)}, u32[]{:S(2)}, u32[]{:S(2)}) collective-permute-start(f32[136,128]{1,0:T(8,128)S(1)} %shard_map.99.refs_7_.refs_0_), channel_id=1, source_target_pairs={{0,4},{1,5},{2,6},{3,7},{4,0},{5,1},{6,2},{7,3},{8,12},{9,13},{10,... | collective-permute-start | bytes 208904 | tf_op jit(solution)/shard_map/ppermute | solution.py:397
  14.2 7.1 %collective-permute-start.7 = (f32[136,128]{1,0:T(8,128)S(1)}, f32[136,128]{1,0:T(8,128)S(1)}, u32[]{:S(2)}, u32[]{:S(2)}) collective-permute-start(f32[136,128]{1,0:T(8,128)S(1)} %get-tuple-element.134.refs_2_), channel_id=1, source_target_pairs={{0,8},{1,9},{2,10},{3,11},{4,12},{5,13},{6,14},{7,15},{8,0},{9,1},... | collective-permute-start | bytes 208904 | tf_op jit(solution)/shard_map/ppermute | solution.py:397
  17.0 6.2 %collective-permute-start.6 = (f32[136,128]{1,0:T(8,128)S(1)}, f32[136,128]{1,0:T(8,128)S(1)}, u32[]{:S(2)}, u32[]{:S(2)}) collective-permute-start(f32[136,128]{1,0:T(8,128)S(1)} %get-tuple-element.135.refs_7_), channel_id=1, source_target_pairs={{0,8},{1,9},{2,10},{3,11},{4,12},{5,13},{6,14},{7,15},{8,0},{9,1},... | collective-permute-start | bytes 208904 | tf_op jit(solution)/shard_map/ppermute | solution.py:397
  21.4 4.9 %collective-permute-start.9 = (f32[128,128]{1,0:T(8,128)S(1)}, f32[128,128]{1,0:T(8,128)S(1)}, u32[]{:S(2)}, u32[]{:S(2)}) collective-permute-start(f32[128,128]{1,0:T(8,128)S(1)} %get-tuple-element.142), channel_id=1, source_target_pairs={{0,2},{1,3},{2,0},{3,1},{4,6},{5,7},{6,4},{7,5},{8,10},{9,11},{10,... | collective-permute-start | bytes 196616 | tf_op jit(solution)/shard_map/ppermute | solution.py:397
  23.2 4.4 %collective-permute-start.8 = (f32[128,128]{1,0:T(8,128)S(1)}, f32[128,128]{1,0:T(8,128)S(1)}, u32[]{:S(2)}, u32[]{:S(2)}) collective-permute-start(f32[128,128]{1,0:T(8,128)S(1)} %get-tuple-element.141), channel_id=1, source_target_pairs={{0,2},{1,3},{2,0},{3,1},{4,6},{5,7},{6,4},{7,5},{8,10},{9,11},{10,... | collective-permute-start | bytes 196616 | tf_op jit(solution)/shard_map/ppermute | solution.py:397
  26.3 1.5 %collective-permute-start.11 = (f32[256,128]{1,0:T(8,128)S(1)}, f32[256,128]{1,0:T(8,128)S(1)}, u32[]{:S(2)}, u32[]{:S(2)}) collective-permute-start(f32[256,128]{1,0:T(8,128)S(1)} %get-tuple-element.152), channel_id=1, source_target_pairs={{0,1},{1,0},{2,3},{3,2},{4,5},{5,4},{6,7},{7,6},{8,9},{9,8},{10,11... | collective-permute-start | bytes 393224 | tf_op jit(solution)/shard_map/ppermute | solution.py:397
  27.7 1.9 %collective-permute-start.10 = (f32[256,128]{1,0:T(8,128)S(1)}, f32[256,128]{1,0:T(8,128)S(1)}, u32[]{:S(2)}, u32[]{:S(2)}) collective-permute-start(f32[256,128]{1,0:T(8,128)S(1)} %get-tuple-element.146), channel_id=1, source_target_pairs={{0,1},{1,0},{2,3},{3,2},{4,5},{5,4},{6,7},{7,6},{8,9},{9,8},{10,11... | collective-permute-start | bytes 393224 | tf_op jit(solution)/shard_map/ppermute | solution.py:397
  29.1 1.9 %collective-permute-start.13 = (f32[264,128]{1,0:T(8,128)S(1)}, f32[264,128]{1,0:T(8,128)S(1)}, u32[]{:S(2)}, u32[]{:S(2)}) collective-permute-start(f32[264,128]{1,0:T(8,128)S(1)} %get-tuple-element.178), channel_id=1, source_target_pairs={{0,1},{1,0},{2,3},{3,2},{4,5},{5,4},{6,7},{7,6},{8,9},{9,8},{10,11... | collective-permute-start | bytes 405512 | tf_op jit(solution)/shard_map/ppermute | solution.py:397
  30.8 2.2 %collective-permute-start.12 = (f32[264,128]{1,0:T(8,128)S(1)}, f32[264,128]{1,0:T(8,128)S(1)}, u32[]{:S(2)}, u32[]{:S(2)}) collective-permute-start(f32[264,128]{1,0:T(8,128)S(1)} %get-tuple-element.177), channel_id=1, source_target_pairs={{0,1},{1,0},{2,3},{3,2},{4,5},{5,4},{6,7},{7,6},{8,9},{9,8},{10,11... | collective-permute-start | bytes 405512 | tf_op jit(solution)/shard_map/ppermute | solution.py:397
  31.0 5.1 %collective-permute-start.15 = (f32[136,128]{1,0:T(8,128)S(1)}, f32[136,128]{1,0:T(8,128)S(1)}, u32[]{:S(2)}, u32[]{:S(2)}) collective-permute-start(f32[136,128]{1,0:T(8,128)S(1)} %get-tuple-element.185), channel_id=1, source_target_pairs={{0,2},{1,3},{2,0},{3,1},{4,6},{5,7},{6,4},{7,5},{8,10},{9,11},{10,... | collective-permute-start | bytes 208904 | tf_op jit(solution)/shard_map/ppermute | solution.py:397
  33.1 4.4 %collective-permute-start.14 = (f32[136,128]{1,0:T(8,128)S(1)}, f32[136,128]{1,0:T(8,128)S(1)}, u32[]{:S(2)}, u32[]{:S(2)}) collective-permute-start(f32[136,128]{1,0:T(8,128)S(1)} %get-tuple-element.184), channel_id=1, source_target_pairs={{0,2},{1,3},{2,0},{3,1},{4,6},{5,7},{6,4},{7,5},{8,10},{9,11},{10,... | collective-permute-start | bytes 208904 | tf_op jit(solution)/shard_map/ppermute | solution.py:397
  36.1 4.8 %collective-permute-start.17 = (f32[136,128]{1,0:T(8,128)S(1)}, f32[136,128]{1,0:T(8,128)S(1)}, u32[]{:S(2)}, u32[]{:S(2)}) collective-permute-start(f32[136,128]{1,0:T(8,128)S(1)} %shard_map.114.refs_2_.refs_0_), channel_id=1, source_target_pairs={{0,4},{1,5},{2,6},{3,7},{4,0},{5,1},{6,2},{7,3},{8,12},{9,13},{10,... | collective-permute-start | bytes 208904 | tf_op jit(solution)/shard_map/ppermute | solution.py:397
  37.5 5.1 %collective-permute-start.16 = (f32[136,128]{1,0:T(8,128)S(1)}, f32[136,128]{1,0:T(8,128)S(1)}, u32[]{:S(2)}, u32[]{:S(2)}) collective-permute-start(f32[136,128]{1,0:T(8,128)S(1)} %shard_map.115.refs_13_.refs_0_), channel_id=1, source_target_pairs={{0,4},{1,5},{2,6},{3,7},{4,0},{5,1},{6,2},{7,3},{8,12},{9,13},{10,... | collective-permute-start | bytes 208904 | tf_op jit(solution)/shard_map/ppermute | solution.py:397
  40.9 7.0 %collective-permute-start.19 = (f32[136,128]{1,0:T(8,128)S(1)}, f32[136,128]{1,0:T(8,128)S(1)}, u32[]{:S(2)}, u32[]{:S(2)}) collective-permute-start(f32[136,128]{1,0:T(8,128)S(1)} %get-tuple-element.191.refs_2_), channel_id=1, source_target_pairs={{0,8},{1,9},{2,10},{3,11},{4,12},{5,13},{6,14},{7,15},{8,0},{9,1},... | collective-permute-start | bytes 208904 | tf_op jit(solution)/shard_map/ppermute | solution.py:397
  42.6 6.9 %collective-permute-start.18 = (f32[136,128]{1,0:T(8,128)S(1)}, f32[136,128]{1,0:T(8,128)S(1)}, u32[]{:S(2)}, u32[]{:S(2)}) collective-permute-start(f32[136,128]{1,0:T(8,128)S(1)} %get-tuple-element.192.refs_13_), channel_id=1, source_target_pairs={{0,8},{1,9},{2,10},{3,11},{4,12},{5,13},{6,14},{7,15},{8,0},{9,1},... | collective-permute-start | bytes 208904 | tf_op jit(solution)/shard_map/ppermute | solution.py:397
  48.0 4.9 %collective-permute-start.20 = (f32[128,128]{1,0:T(8,128)S(1)}, f32[128,128]{1,0:T(8,128)S(1)}, u32[]{:S(2)}, u32[]{:S(2)}) collective-permute-start(f32[128,128]{1,0:T(8,128)S(1)} %get-tuple-element.203), channel_id=1, source_target_pairs={{0,2},{1,3},{2,0},{3,1},{4,6},{5,7},{6,4},{7,5},{8,10},{9,11},{10,... | collective-permute-start | bytes 196616 | tf_op jit(solution)/shard_map/ppermute | solution.py:397
  49.5 4.3 %collective-permute-start.22 = (f32[128,128]{1,0:T(8,128)S(1)}, f32[128,128]{1,0:T(8,128)S(1)}, u32[]{:S(2)}, u32[]{:S(2)}) collective-permute-start(f32[128,128]{1,0:T(8,128)S(1)} %get-tuple-element.213), channel_id=1, source_target_pairs={{0,2},{1,3},{2,0},{3,1},{4,6},{5,7},{6,4},{7,5},{8,10},{9,11},{10,... | collective-permute-start | bytes 196616 | tf_op jit(solution)/shard_map/ppermute | solution.py:397
  52.9 1.4 %collective-permute-start.21 = (f32[256,128]{1,0:T(8,128)S(1)}, f32[256,128]{1,0:T(8,128)S(1)}, u32[]{:S(2)}, u32[]{:S(2)}) collective-permute-start(f32[256,128]{1,0:T(8,128)S(1)} %get-tuple-element.206), channel_id=1, source_target_pairs={{0,1},{1,0},{2,3},{3,2},{4,5},{5,4},{6,7},{7,6},{8,9},{9,8},{10,11... | collective-permute-start | bytes 393224 | tf_op jit(solution)/shard_map/ppermute | solution.py:397
  53.9 1.7 %collective-permute-start.23 = (f32[256,128]{1,0:T(8,128)S(1)}, f32[256,128]{1,0:T(8,128)S(1)}, u32[]{:S(2)}, u32[]{:S(2)}) collective-permute-start(f32[256,128]{1,0:T(8,128)S(1)} %get-tuple-element.217), channel_id=1, source_target_pairs={{0,1},{1,0},{2,3},{3,2},{4,5},{5,4},{6,7},{7,6},{8,9},{9,8},{10,11... | collective-permute-start | bytes 393224 | tf_op jit(solution)/shard_map/ppermute | solution.py:397
  (2 other events, 6.7 us)

commit v5 on v4

--- a/solution.py
+++ b/solution.py
@@ -14,6 +14,8 @@
 FAR = -1e30
 GROUPS = 4
 CHUNKS = 2
+K3_TURNS = ((0, 0), (0, 1), (1, 1))
+K5_TURNS = ((0, 0), (0, 1), (1, 0), (1, 1))
 PIECES = 2
 F32 = jnp.float32
 BF16 = jnp.bfloat16
@@ -49,7 +51,7 @@
 HBM = pl.BlockSpec(memory_space=pltpu.HBM)
 
 
-def run(body, scalar, inside, outs, outside=(), after=(), aliases=None, scratch=(), megabytes=8):
+def run(body, scalar, inside, outs, outside=(), after=(), aliases=None, renewed=None, scratch=(), megabytes=8):
     taken = len(inside) + len(outside)
 
     def kernel(scalar_ref, *refs):
@@ -61,7 +63,8 @@
         in_specs=[SMEM] + [VMEM] * len(inside) + [HBM] * len(outside) + [ANY] * len(after),
         out_specs=[HBM if isinstance(o, jax.ShapeDtypeStruct) else VMEM for o in outs],
         out_shape=shapes,
-        input_output_aliases={1 + len(inside) + i: o for i, o in (aliases or {}).items()},
+        input_output_aliases={1 + len(inside) + i: o for i, o in (aliases or {}).items()}
+        | {1 + i: o for i, o in (renewed or {}).items()},
         scratch_shapes=list(scratch),
         compiler_params=pltpu.CompilerParams(vmem_limit_bytes=megabytes << 20),
     )(scalar, *[pltpu.with_memory_space_constraint(a, pltpu.VMEM) for a in inside],
@@ -104,10 +107,17 @@
         out[2 * k * DH + 2 * k :, :] = jnp.ones((rest, DH), F32)
 
 
-def take_in(place, k, mine_ref, other_ref, state_ref):
-    for r in range(GROUPS * k):
-        source = mine_ref if r < 2 * k else other_ref
-        state_ref[((r // k) ^ group_of(place)) * k + r % k] = source[cut(r % (2 * k)), :]
+def turned_half(place, k, i):
+    return ((i // k) ^ ((place[0] >> 1) & 1)) * k + i % k
+
+
+def at_rows(i):
+    return pl.ds(pl.multiple_of(i * DH, DH), DH)
+
+
+def each_half(place, other, work):
+    for p in range(2):
+        pl.when(((place[0] & 1) ^ other) == p)(functools.partial(work, p))
 
 
 def k1_body(k, head0, chunks, place, *refs):
@@ -201,35 +211,39 @@
             leave_ref[at, cut(j)] = jnp.broadcast_to(cols_ref[at, 16 + head : 17 + head], (BLOCK, DH))
 
 
-def k3_body(k, head0, pieces, per, place, query_ref, grad_ref, loc_ref, rows_ref, mine_ref, other_ref, *refs):
-    withins, scaleds, enters = refs[:pieces], refs[pieces : 2 * pieces], refs[2 * pieces : 3 * pieces]
-    own_ref, send_ref, mixgrad_ref, states_ref, back_ref, attended_ref = refs[3 * pieces : 3 * pieces + 6]
-    terms_ref, keep_ref, state_ref = refs[3 * pieces + 6 :]
-    take_in(place, k, mine_ref, other_ref, state_ref)
-    for j in range(GROUPS * k):
-        head = head0 + j
-        p, i = j // per, j % per
-        k0, k1 = keeps(rows_ref, head)
-        incoming = state_ref[j]
-        states = (incoming, k0 * incoming + loc_ref[j])
-        backs = []
-        for b in range(2):
-            at = block(b)
-            low = states[b].astype(BF16)
-            states_ref[j, b] = low
-            mixture = withins[p][at, cut(i)] + mm(query_ref[at, cut(head)], low) * enters[p][at, cut(i)]
-            wide = grad_ref[at, cut(head)].astype(F32)
-            inverse = lax.rsqrt(jnp.mean(mixture * mixture, axis=1, keepdims=True) + EPS)
-            along = jnp.mean(wide * mixture, axis=1, keepdims=True) * inverse
-            normed = mixture * inverse
-            attended_ref[at, cut(j)] = normed.astype(BF16)
-            mixgrad = (inverse * (wide - normed * along)).astype(BF16)
-            mixgrad_ref[at, cut(j)] = mixgrad
-            backs.append(mm(scaleds[p][i, b], mixgrad))
-        back_ref[j] = backs[1]
-        terms_ref[j] = k0 * backs[1] + backs[0]
-        keep_ref[j : j + 1, :] = k0 * k1
-    send_out(place, k, terms_ref, keep_ref, own_ref, send_ref)
+def k3_body(k, head0, other, place, query_ref, grad_ref, loc_ref, rows_ref, state_ref, *refs):
+    per = 2 * k
+    withins, scaleds, enters, refs = refs[:2], refs[2:4], refs[4:6], refs[6:]
+    message_ref, mixgrad_ref, states_ref, back_ref, attended_ref = refs[-5:]
+    message_ref[per * DH :, :] = jnp.ones((8, DH), F32)
+
+    def work(p):
+        for i in range(per):
+            j = p * per + i
+            head = head0 + j
+            stand = turned_half(place, k, i)
+            k0, k1 = keeps(rows_ref, head)
+            incoming = state_ref[at_rows(stand), :]
+            states = (incoming, k0 * incoming + loc_ref[j])
+            backs = []
+            for b in range(2):
+                at = block(b)
+                low = states[b].astype(BF16)
+                states_ref[j, b] = low
+                mixture = withins[p][at, cut(i)] + mm(query_ref[at, cut(head)], low) * enters[p][at, cut(i)]
+                wide = grad_ref[at, cut(head)].astype(F32)
+                inverse = lax.rsqrt(jnp.mean(mixture * mixture, axis=1, keepdims=True) + EPS)
+                along = jnp.mean(wide * mixture, axis=1, keepdims=True) * inverse
+                normed = mixture * inverse
+                attended_ref[at, cut(j)] = normed.astype(BF16)
+                mixgrad = (inverse * (wide - normed * along)).astype(BF16)
+                mixgrad_ref[at, cut(j)] = mixgrad
+                backs.append(mm(scaleds[p][i, b], mixgrad))
+            back_ref[j] = backs[1]
+            message_ref[at_rows(stand), :] = k0 * backs[1] + backs[0]
+            message_ref[pl.ds(per * DH + stand, 1), :] = k0 * k1
+
+    each_half(place, other, work)
 
 
 def columns(ref, first, count):
@@ -270,55 +284,55 @@
         copy.wait()
 
 
-def k5_body(k, head0, pieces, per, chunks, place, key_ref, value_ref, back_ref, rows_ref, mine_ref, other_ref, *refs):
-    heads = GROUPS * k
-    key_parts, value_parts, leaves = refs[:pieces], refs[pieces : 2 * pieces], refs[2 * pieces : 3 * pieces]
-    refs = refs[3 * pieces :]
-    first, last = head0 == 0, head0 == (chunks - 1) * heads
+def k5_body(k, head0, other, kept, query_at, place, key_ref, value_ref, back_ref, rows_ref, state_ref, *refs):
+    per = 2 * k
+    key_parts, value_parts, leaves, refs = refs[:2], refs[2:4], refs[4:6], refs[6:]
+    left, refs = refs[: 2 * len(kept)], refs[2 * len(kept) :]
+    if query_at is not None:
+        query_ref, _, key_grad_ref, value_grad_ref, query_hbm, sems = refs
+    elif kept:
+        key_hbm, value_hbm, key_grad_ref, value_grad_ref, sems = refs
+    else:
+        key_grad_ref, value_grad_ref = refs
+
+    def ship(source, target, sem):
+        copy = pltpu.make_async_copy(source, target, sems.at[sem])
+        copy.start()
+        return copy
+
     copies = []
-    if first:
-        done_ref, refs = refs[0], refs[2:]
-    earlier, refs = refs[: 2 * (chunks - 1) * last], refs[2 * (chunks - 1) * last :]
-    if last:
-        key_grad_hbm, value_grad_hbm, refs = refs[0], refs[1], refs[2:]
-    else:
-        key_grad_ref, value_grad_ref, refs = refs[0], refs[1], refs[2:]
-    if first:
-        query_grad_hbm, refs = refs[0], refs[1:]
-    state_ref, sems, refs = refs[0], refs[1], refs[2:]
-    if last:
-        key_grad_ref, value_grad_ref = refs
-
-    def ship(source, target):
-        copy = pltpu.make_async_copy(source, target, sems.at[len(copies)])
-        copy.start()
-        copies.append(copy)
-
-    if first:
-        ship(done_ref, columns(query_grad_hbm, chunks * heads - per, per))
-    for n in range(0, len(earlier), 2):
-        ship(earlier[n], columns(key_grad_hbm, n // 2 * heads, heads))
-        ship(earlier[n + 1], columns(value_grad_hbm, n // 2 * heads, heads))
-    take_in(place, k, mine_ref, other_ref, state_ref)
-    for j in range(heads):
-        head = head0 + j
-        p, i = j // per, j % per
-        k0, k1 = keeps(rows_ref, head)
-        outgoing = state_ref[j]
-        afters = (k1 * outgoing + back_ref[j], outgoing)
-        for b in range(2):
-            at = block(b)
-            low = afters[b].astype(BF16)
-            leave = leaves[p][at, cut(i)]
-            key_grad_ref[at, cut(j)] = (
-                key_parts[p][at, cut(i)] + mm(value_ref[at, cut(j)], low, NT) * leave
-            ).astype(BF16)
-            value_grad_ref[at, cut(j)] = (
-                value_parts[p][at, cut(i)] + mm(key_ref[at, cut(j)], low) * leave
-            ).astype(BF16)
-        if last:
-            ship(columns(key_grad_ref, j, 1), columns(key_grad_hbm, head, 1))
-            ship(columns(value_grad_ref, j, 1), columns(value_grad_hbm, head, 1))
+    if query_at is not None:
+        copies.append(ship(query_ref, columns(query_hbm, query_at, per), 0))
+    for n, (base, half) in enumerate(kept):
+        start = pl.multiple_of((base + ((place[0] & 1) ^ half) * per) * DH, DH)
+        copies.append(ship(left[2 * n], key_hbm.at[:, pl.ds(start, per * DH)], 2 * n))
+        copies.append(ship(left[2 * n + 1], value_hbm.at[:, pl.ds(start, per * DH)], 2 * n + 1))
+
+    def work(p):
+        ours = []
+        for i in range(per):
+            j = p * per + i
+            k0, k1 = keeps(rows_ref, head0 + j)
+            outgoing = state_ref[at_rows(turned_half(place, k, i)), :]
+            afters = (k1 * outgoing + back_ref[j], outgoing)
+            for b in range(2):
+                at = block(b)
+                low = afters[b].astype(BF16)
+                leave = leaves[p][at, cut(i)]
+                key_grad_ref[at, cut(i)] = (
+                    key_parts[p][at, cut(i)] + mm(value_ref[at, cut(j)], low, NT) * leave
+                ).astype(BF16)
+                value_grad_ref[at, cut(i)] = (
+                    value_parts[p][at, cut(i)] + mm(key_ref[at, cut(j)], low) * leave
+                ).astype(BF16)
+            if kept:
+                sem = 2 * len(kept) + 2 * i
+                ours.append(ship(columns(key_grad_ref, i, 1), columns(key_hbm, head0 + j, 1), sem))
+                ours.append(ship(columns(value_grad_ref, i, 1), columns(value_hbm, head0 + j, 1), sem + 1))
+        for copy in ours:
+            copy.wait()
+
+    each_half(place, other, work)
     for copy in copies:
         copy.wait()
 
@@ -402,7 +416,7 @@
         self.place, self.last = place, ()
 
     def __call__(self, body, inside, outs, **options):
-        taken = [id(a) for a in options.get("outside", ())]
+        taken = [id(a) for a in (*options.get("outside", ()), *inside)]
         after = tuple(a for a in self.last if id(a) not in taken)
         out = run(body, self.place, inside, outs, after=after, **options)
         self.last = (out[0],)
@@ -413,6 +427,7 @@
     half = ((k * DH + 8, DH), F32)
     got = exchange(send, 1, count)
     yield
+    own = own()
     chip, chip_send = call(functools.partial(c1_body, turn, k), (own, got), (half, half))
     chip_got = exchange(chip_send, 2, count)
     yield
@@ -436,19 +451,27 @@
     yield state, exchange(state_send, 1, count)
 
 
-def drive(scans, fillers):
+def drive(scans, fillers, rounds, late=None):
     fillers = list(fillers)
-    step = 0
-    while True:
-        results = [next(scan) for scan in scans]
-        if results[0] is not None:
-            break
+    for step in range(rounds):
+        for c, scan in enumerate(scans):
+            if step == 1 and late:
+                late(c)
+            next(scan)
         if step and fillers:
             fillers.pop(0)()
-        step += 1
     for filler in fillers:
         filler()
-    return results
+
+
+def by_halves(scans, half, turns):
+    ready = {}
+    for c, other in turns:
+        for n in range(c + 1 + (len(ready) > 0 and c + 1 < len(scans))):
+            if n not in ready:
+                ready[n] = next(scans[n])
+        half(c, other, ready[c][other])
+    return ready
 
 
 def local(query_rows, key_rows, value_rows, log_decay, run_start, out_grad):
@@ -467,6 +490,7 @@
     flat = jax.ShapeDtypeStruct((tokens, width), BF16)
     chunk_bf16 = ((tokens, heads * DH), BF16)
     piece_f32 = ((tokens, per * DH), F32)
+    half_bf16 = ((tokens, per * DH), BF16)
     square = (per, 2, BLOCK, BLOCK)
     mask = ((2, BLOCK, BLOCK), F32)
     scratch_terms = (pltpu.VMEM((heads, DH, DH), F32), pltpu.VMEM((8, DH), F32))
@@ -486,7 +510,7 @@
         else:
             out = call(body, (rows, keys[c], values[c]), outs, scratch=scratch)
         loc.append(out[2])
-        scans.append(scan_devices(call, out[0], out[1], False, k, count))
+        scans.append(scan_devices(call, lambda own=out[0]: own, out[1], False, k, count))
 
     forward = []
 
@@ -502,25 +526,32 @@
         forward.append(call(functools.partial(k2_body, n == 0, n * per, c * heads, per), inputs, outs))
 
     fillers = range(CHUNKS * PIECES)
-    results = drive(scans, [functools.partial(k2, n) for n in fillers])
-    middle, scans = [], []
-    for c, (mine, other) in enumerate(results):
+    rounds = count.bit_length()
+    drive(scans, [functools.partial(k2, n) for n in fillers], rounds)
+    middle, newest = {}, {}
+
+    def k3(c, other, state):
         mid = forward[c * PIECES : (c + 1) * PIECES]
+        inside = (query_rows, out_grad, loc[c], rows, state)
+        inside += tuple(f[i] for i in (0, 4, 5) for f in mid)
+        renewed = {len(inside) + i: 1 + i for i in range(4)} if c in newest else None
         out = call(
-            functools.partial(k3_body, k, c * heads, PIECES, per),
-            (query_rows, out_grad, loc[c], rows, mine, other)
-            + tuple(f[0] for f in mid) + tuple(f[4] for f in mid) + tuple(f[5] for f in mid),
-            (message, message, chunk_bf16, ((heads, 2, DH, DH), BF16), states, chunk_bf16),
-            scratch=scratch_terms + (pltpu.VMEM((heads, DH, DH), F32),),
+            functools.partial(k3_body, k, c * heads, other),
+            inside + tuple(newest.get(c, ())),
+            (message, chunk_bf16, ((heads, 2, DH, DH), BF16), states, chunk_bf16),
+            renewed=renewed,
         )
-        middle.append(out)
-        scans.append(scan_devices(call, out[0], out[1], True, k, count))
+        middle[c, other], newest[c] = out[0], out[1:]
+
+    ready = by_halves(scans, k3, K3_TURNS)
+    late = {c for c in chunks if (c, 0) not in K3_TURNS}
+    scans = [scan_devices(call, lambda c=c: middle[c, 0], middle[c, 1], True, k, count) for c in chunks]
 
     backward = []
 
     def k4(n):
         c = n // PIECES
-        _, _, mixgrad, states_low, _, attended = middle[c]
+        mixgrad, states_low, _, attended = newest[c]
         f = forward[n]
         backward.append(
             call(
@@ -534,28 +565,34 @@
             )
         )
 
-    results = drive(scans, [functools.partial(k4, n) for n in fillers])
+    drive(scans, [functools.partial(k4, n) for n in fillers], rounds, lambda c: k3(c, 0, ready[c][0]) if c in late else None)
     attended, query_grad = backward[-1][3:]
-    grads = ()
-    for c, (mine, other) in enumerate(results):
-        first, last = c == 0, c == CHUNKS - 1
-        back = backward[c * PIECES : (c + 1) * PIECES]
-        mid = forward[c * PIECES : (c + 1) * PIECES]
-        out = call(
-            functools.partial(k5_body, k, c * heads, PIECES, per, CHUNKS),
-            (keys[c], values[c], middle[c][4], rows, mine, other)
-            + tuple(b[0] for b in back) + tuple(b[1] for b in back) + tuple(f[6] for f in mid)
-            + ((backward[-1][2],) if first else ()) + (grads if last else ()),
-            ((flat,) * 2 if last else (chunk_bf16,) * 2) + ((flat,) if first else ()),
-            outside=(query_grad,) if first else (),
-            aliases={0: 2} if first else None,
-            scratch=(pltpu.VMEM((heads, DH, DH), F32), dma((2 * heads + 2 * CHUNKS,)))
-            + ((pltpu.VMEM((tokens, heads * DH), BF16),) * 2 if last else ()),
-        )
-        if first:
-            query_grad = out[2]
-        grads = grads + tuple(out[:2])
-    return attended, query_grad, out[0], out[1]
+    final = []
+
+    def k5(c, other, state):
+        last = c == CHUNKS - 1 and other == 1
+        mid = [forward[n] for n in range(c * PIECES, (c + 1) * PIECES)]
+        back = [backward[n] for n in range(c * PIECES, (c + 1) * PIECES)]
+        inside = (keys[c], values[c], newest[c][2], rows, state)
+        inside += tuple(b[0] for b in back) + tuple(b[1] for b in back) + tuple(f[6] for f in mid)
+        kept, query_at, options = (), None, {}
+        outs = (half_bf16, half_bf16)
+        if not final:
+            inside += (backward[-1][2],)
+            query_at = CHUNKS * heads - per
+            outs += (flat,)
+            options = {"outside": (query_grad,), "aliases": {0: 2}, "scratch": (dma((1,)),)}
+        elif last:
+            kept = tuple(f[1:] for f in final)
+            inside += tuple(a for f in final for a in f[0][:2])
+            outs = (flat, flat)
+            half = pltpu.VMEM((tokens, per * DH), BF16)
+            options = {"scratch": (half, half, dma((2 * len(kept) + 2 * per,)))}
+        body = functools.partial(k5_body, k, c * heads, other, kept, query_at)
+        final.append((call(body, inside, outs, **options), c * heads, other))
+
+    by_halves(scans, k5, K5_TURNS)
+    return attended, final[0][0][2], *final[-1][0]
 
 
 def solution(mesh):

time: 57.3 us -> 56.2 us (0.981)
  starting transfers between devices: 27.9 us -> 26.6 us
  waiting for transfers between devices: 10 us -> 9 us
  Pallas kernels: 18.2 us -> 19 us
    ppermute x24, starting transfers between devices: 27.9 us -> 26.6 us  [exchange(): return lax.ppermute(x, 'seq', [(i, i ^ bit) for i in range(count)])]
    ppermute x24, waiting for transfers between devices: 10 us -> 9 us  [exchange(): return lax.ppermute(x, 'seq', [(i, i ^ bit) for i in range(count)])]
    pallas_call x34 -> x38, Pallas kernels: 18.2 us -> 19 us  [run(): pl.pallas_call(kernel, in_specs=[SMEM] + [VMEM] * len(inside) + [HBM] * l...]
  transfers between devices with their start and end apart: 24 -> 24, of which waited for: 10 -> 11; matrix products, arithmetic and copies ran while one was open for 0% -> 0% of each run, Pallas kernels for 26% -> 28%
where the time goes in v5:
time: 56.2 us; the launch traced here: 56 us
  starting transfers between devices  26.6 us (47%)
  Pallas kernels  19 us (34%)
  waiting for transfers between devices  9 us (16%)
  between operations  1.1 us (2%)
    ppermute x24, starting transfers between devices, exchange(): return lax.ppermute(x, 'seq', [(i, i ^ bit) for i in range(count)])  26.6 us
    pallas_call x38, Pallas kernels, run(): pl.pallas_call(kernel, in_specs=[SMEM] + [VMEM] * len(inside) + [HBM] * l...  19 us
    ppermute x24, waiting for transfers between devices, exchange(): return lax.ppermute(x, 'seq', [(i, i ^ bit) for i in range(count)])  9 us
  transfers between devices with their start and end apart: 24, of which 11 were waited for; matrix products, arithmetic and copies ran while one was open for 0% of the time, Pallas kernels for 28%

profile of v5, /device:TPU:0, one launch (start us, length us, event | category | flops | bytes accessed | tf_op | source)
XLA Modules:
  0.0 56.0 jit_solution(11474224005217948496)
XLA Ops:
  0.6 1.7 %shard_map.93 = (f32[264,128]{1,0:T(8,128)S(1)}, f32[264,128]{1,0:T(8,128)S(1)}, f32[4,128,128]{2,1,0:T(8,128)S(1)}, f32[32,512]{1,0:T(8,128)S(1)}, f32[512,128]...) custom-call(s32[1]{0:T(128)} %bitcast.scalar_ref, ...), custom_call_target="tpu_custom_call" | custom-call | tf_op jit(solution)/shard_map/pallas_call | solution.py:61
  3.9 2.9 %collective-permute-start.3 = (f32[136,128]{1,0:T(8,128)S(1)}, f32[136,128]{1,0:T(8,128)S(1)}, u32[]{:S(2)}, u32[]{:S(2)}) collective-permute-start(f32[136,128]{1,0:T(8,128)S(1)} %get-tuple-element.138), channel_id=1, source_target_pairs={{0,2},{1,3},{2,0},{3,1},{4,6},{5,7},{6,4},{7,5},{8,10},{9,11},{10,... | collective-permute-start | bytes 208904 | tf_op jit(solution)/shard_map/ppermute | solution.py:411
  7.4 0.9 %shard_map.97 = (f32[512,256]{1,0:T(8,128)S(1)}, f32[2,2,256,256]{3,2,1,0:T(8,128)S(1)}, f32[2,2,256,256]{3,2,1,0:T(8,128)S(1)}, bf16[2,2,256,256]{3,2,1,0:T(8,1...) custom-call(s32[1]{0:T(128)} %bitcast.scalar_ref, ...), custom_call_target="tpu_custom_call" | custom-call | tf_op jit(solution)/shard_map/pallas_call | solution.py:61
  8.3 1.1 %collective-permute-done.3.refs_1_.refs_3_ = f32[136,128]{1,0:T(8,128)S(1)} collective-permute-done((f32[136,128]{1,0:T(8,128)S(1)}, f32[136,128]{1,0:T(8,128)S(1)}, u32[]{:S(2)}, u32[]{:S(2)}) %collective-permute-start.3) | collective-permute-done | bytes 69664 | tf_op jit(solution)/shard_map/ppermute | solution.py:411
  9.4 2.2 %collective-permute-start.5 = (f32[136,128]{1,0:T(8,128)S(1)}, f32[136,128]{1,0:T(8,128)S(1)}, u32[]{:S(2)}, u32[]{:S(2)}) collective-permute-start(f32[136,128]{1,0:T(8,128)S(1)} %shard_map.98.refs_2_.refs_0_), channel_id=1, source_target_pairs={{0,4},{1,5},{2,6},{3,7},{4,0},{5,1},{6,2},{7,3},{8,12},{9,13},{10,... | collective-permute-start | bytes 208904 | tf_op jit(solution)/shard_map/ppermute | solution.py:411
  11.6 1.3 %collective-permute-start.4 = (f32[136,128]{1,0:T(8,128)S(1)}, f32[136,128]{1,0:T(8,128)S(1)}, u32[]{:S(2)}, u32[]{:S(2)}) collective-permute-start(f32[136,128]{1,0:T(8,128)S(1)} %shard_map.99.refs_7_.refs_0_), channel_id=1, source_target_pairs={{0,4},{1,5},{2,6},{3,7},{4,0},{5,1},{6,2},{7,3},{8,12},{9,13},{10,... | collective-permute-start | bytes 208904 | tf_op jit(solution)/shard_map/ppermute | solution.py:411
  14.2 2.8 %collective-permute-start.7 = (f32[136,128]{1,0:T(8,128)S(1)}, f32[136,128]{1,0:T(8,128)S(1)}, u32[]{:S(2)}, u32[]{:S(2)}) collective-permute-start(f32[136,128]{1,0:T(8,128)S(1)} %get-tuple-element.146.refs_2_), channel_id=1, source_target_pairs={{0,8},{1,9},{2,10},{3,11},{4,12},{5,13},{6,14},{7,15},{8,0},{9,1},... | collective-permute-start | bytes 208904 | tf_op jit(solution)/shard_map/ppermute | solution.py:411
  17.0 1.6 %collective-permute-start.6 = (f32[136,128]{1,0:T(8,128)S(1)}, f32[136,128]{1,0:T(8,128)S(1)}, u32[]{:S(2)}, u32[]{:S(2)}) collective-permute-start(f32[136,128]{1,0:T(8,128)S(1)} %get-tuple-element.147.refs_7_), channel_id=1, source_target_pairs={{0,8},{1,9},{2,10},{3,11},{4,12},{5,13},{6,14},{7,15},{8,0},{9,1},... | collective-permute-start | bytes 208904 | tf_op jit(solution)/shard_map/ppermute | solution.py:411
  19.4 1.9 %collective-permute-done.7.refs_0_ = f32[136,128]{1,0:T(8,128)S(1)} collective-permute-done((f32[136,128]{1,0:T(8,128)S(1)}, f32[136,128]{1,0:T(8,128)S(1)}, u32[]{:S(2)}, u32[]{:S(2)}) %collective-permute-start.7) | collective-permute-done | bytes 69664 | tf_op jit(solution)/shard_map/ppermute | solution.py:411
  21.4 1.8 %collective-permute-start.9 = (f32[128,128]{1,0:T(8,128)S(1)}, f32[128,128]{1,0:T(8,128)S(1)}, u32[]{:S(2)}, u32[]{:S(2)}) collective-permute-start(f32[128,128]{1,0:T(8,128)S(1)} %get-tuple-element.155), channel_id=1, source_target_pairs={{0,2},{1,3},{2,0},{3,1},{4,6},{5,7},{6,4},{7,5},{8,10},{9,11},{10,... | collective-permute-start | bytes 196616 | tf_op jit(solution)/shard_map/ppermute | solution.py:411
  23.2 2.2 %collective-permute-start.8 = (f32[128,128]{1,0:T(8,128)S(1)}, f32[128,128]{1,0:T(8,128)S(1)}, u32[]{:S(2)}, u32[]{:S(2)}) collective-permute-start(f32[128,128]{1,0:T(8,128)S(1)} %get-tuple-element.153), channel_id=1, source_target_pairs={{0,2},{1,3},{2,0},{3,1},{4,6},{5,7},{6,4},{7,5},{8,10},{9,11},{10,... | collective-permute-start | bytes 196616 | tf_op jit(solution)/shard_map/ppermute | solution.py:411
  30.1 2.1 %collective-permute-start.15 = (f32[136,128]{1,0:T(8,128)S(1)}, f32[136,128]{1,0:T(8,128)S(1)}, u32[]{:S(2)}, u32[]{:S(2)}) collective-permute-start(f32[136,128]{1,0:T(8,128)S(1)} %get-tuple-element.205), channel_id=1, source_target_pairs={{0,2},{1,3},{2,0},{3,1},{4,6},{5,7},{6,4},{7,5},{8,10},{9,11},{10,... | collective-permute-start | bytes 208904 | tf_op jit(solution)/shard_map/ppermute | solution.py:411
  32.2 0.9 %shard_map.113 = (f32[264,128]{1,0:T(8,128)S(1)}, bf16[512,512]{1,0:T(8,128)(2,1)S(1)}, bf16[4,2,128,128]{3,2,1,0:T(8,128)(2,1)S(1)}, f32[4,128,128]{2,1,0:T(8,128)S(1)}, bf16[512,512]{1,0:T(8,128)(2,1)S(1)}) custom-call(s32[1]{0:T(128)} %bitcast.scalar_ref, ...), custom_call_target="tpu_custom_call", output_to_operand_aliasing={{1}: (12, {}), {2}: (13, {}), {3}: (14, {}), {4}: (15, {})} | custom-call | tf_op jit(solution)/shard_map/pallas_call | solution.py:61
  33.4 1.7 %shard_map.115 = (f32[512,256]{1,0:T(8,128)S(1)}, f32[512,256]{1,0:T(8,128)S(1)}, bf16[512,256]{1,0:T(8,128)(2,1)S(1)}, bf16[512,1024]{1,0:T(8,128)(2,1)}, bf16[512,1024]{1,0:T(8,128)(2,1)}) custom-call(s32[1]{0:T(128)} %bitcast.scalar_ref, bf16[512,1024]{1,0:T(8,128)(2,1)S(1)} %copy-done, bf16[512,512]{1,0:T(8,128)(2,1)S(1)} %get-tuple-element.139.refs_1_.refs_0_, ...), custom_call_target="tpu_custom_call" | custom-call | tf_op jit(solution)/shard_map/pallas_call | solution.py:61
  35.8 1.8 %collective-permute-done.14.refs_1_.refs_3_ = f32[136,128]{1,0:T(8,128)S(1)} collective-permute-done((f32[136,128]{1,0:T(8,128)S(1)}, f32[136,128]{1,0:T(8,128)S(1)}, u32[]{:S(2)}, u32[]{:S(2)}) %collective-permute-start.14) | collective-permute-done | bytes 69664 | tf_op jit(solution)/shard_map/ppermute | solution.py:411
  38.2 1.9 %shard_map.118 = (f32[512,256]{1,0:T(8,128)S(1)}, f32[512,256]{1,0:T(8,128)S(1)}, bf16[512,256]{1,0:T(8,128)(2,1)S(1)}, bf16[512,1024]{1,0:T(8,128)(2,1)}, bf16[512,1024]{1,0:T(8,128)(2,1)}) custom-call(s32[1]{0:T(128)} %bitcast.scalar_ref, bf16[512,1024]{1,0:T(8,128)(2,1)S(1)} %copy-done, ...), custom_call_target="tpu_custom_call", output_to_operand_aliasing={{3}: (12, {}), {4}: (13, {})} | custom-call | tf_op jit(solution)/shard_map/pallas_call | solution.py:61
  40.1 2.1 %collective-permute-start.19 = (f32[136,128]{1,0:T(8,128)S(1)}, f32[136,128]{1,0:T(8,128)S(1)}, u32[]{:S(2)}, u32[]{:S(2)}) collective-permute-start(f32[136,128]{1,0:T(8,128)S(1)} %get-tuple-element.211.refs_2_), channel_id=1, source_target_pairs={{0,8},{1,9},{2,10},{3,11},{4,12},{5,13},{6,14},{7,15},{8,0},{9,1},... | collective-permute-start | bytes 208904 | tf_op jit(solution)/shard_map/ppermute | solution.py:411
  42.2 0.9 %collective-permute-start.18 = (f32[136,128]{1,0:T(8,128)S(1)}, f32[136,128]{1,0:T(8,128)S(1)}, u32[]{:S(2)}, u32[]{:S(2)}) collective-permute-start(f32[136,128]{1,0:T(8,128)S(1)} %get-tuple-element.212.refs_13_), channel_id=1, source_target_pairs={{0,8},{1,9},{2,10},{3,11},{4,12},{5,13},{6,14},{7,15},{8,0},{9,1},... | collective-permute-start | bytes 208904 | tf_op jit(solution)/shard_map/ppermute | solution.py:411
  43.2 1.7 %shard_map.121 = (f32[512,256]{1,0:T(8,128)S(1)}, f32[512,256]{1,0:T(8,128)S(1)}, bf16[512,256]{1,0:T(8,128)(2,1)S(1)}, bf16[512,1024]{1,0:T(8,128)(2,1)}, bf16[512,1024]{1,0:T(8,128)(2,1)}) custom-call(s32[1]{0:T(128)} %bitcast.scalar_ref, bf16[512,1024]{1,0:T(8,128)(2,1)S(1)} %copy-done, ...), custom_call_target="tpu_custom_call", output_to_operand_aliasing={{3}: (12, {}), {4}: (13, {})} | custom-call | tf_op jit(solution)/shard_map/pallas_call | solution.py:61
  44.9 2.2 %collective-permute-done.19.refs_0_ = f32[136,128]{1,0:T(8,128)S(1)} collective-permute-done((f32[136,128]{1,0:T(8,128)S(1)}, f32[136,128]{1,0:T(8,128)S(1)}, u32[]{:S(2)}, u32[]{:S(2)}) %collective-permute-start.19) | collective-permute-done | bytes 69664 | tf_op jit(solution)/shard_map/ppermute | solution.py:411
  47.2 1.3 %collective-permute-start.20 = (f32[128,128]{1,0:T(8,128)S(1)}, f32[128,128]{1,0:T(8,128)S(1)}, u32[]{:S(2)}, u32[]{:S(2)}) collective-permute-start(f32[128,128]{1,0:T(8,128)S(1)} %get-tuple-element.223), channel_id=1, source_target_pairs={{0,2},{1,3},{2,0},{3,1},{4,6},{5,7},{6,4},{7,5},{8,10},{9,11},{10,... | collective-permute-start | bytes 196616 | tf_op jit(solution)/shard_map/ppermute | solution.py:411
  48.6 1.3 %collective-permute-start.21 = (f32[128,128]{1,0:T(8,128)S(1)}, f32[128,128]{1,0:T(8,128)S(1)}, u32[]{:S(2)}, u32[]{:S(2)}) collective-permute-start(f32[128,128]{1,0:T(8,128)S(1)} %get-tuple-element.234), channel_id=1, source_target_pairs={{0,2},{1,3},{2,0},{3,1},{4,6},{5,7},{6,4},{7,5},{8,10},{9,11},{10,... | collective-permute-start | bytes 196616 | tf_op jit(solution)/shard_map/ppermute | solution.py:411
  50.0 1.9 %shard_map.124 = (f32[512,256]{1,0:T(8,128)S(1)}, f32[512,256]{1,0:T(8,128)S(1)}, bf16[512,256]{1,0:T(8,128)(2,1)S(1)}, bf16[512,1024]{1,0:T(8,128)(2,1)}, bf16[512,1024]{1,0:T(8,128)(2,1)}) custom-call(s32[1]{0:T(128)} %bitcast.scalar_ref, bf16[512,1024]{1,0:T(8,128)(2,1)S(1)} %copy-done, ...), custom_call_target="tpu_custom_call", output_to_operand_aliasing={{3}: (12, {}), {4}: (13, {})} | custom-call | tf_op jit(solution)/shard_map/pallas_call | solution.py:61
  54.4 1.4 %shard_map.130 = (bf16[512,1024]{1,0:T(8,128)(2,1)}, bf16[512,1024]{1,0:T(8,128)(2,1)}) custom-call(s32[1]{0:T(128)} %bitcast.scalar_ref, bf16[512,512]{1,0:T(8,128)(2,1)S(1)} %get-tuple-element.127.refs_1_.refs_0_, bf16[512,512]{1,0:T(8,128)(2,1)S(1)} %get-tuple-element.128.refs_2_.refs_1_, f32[4,128,128]{2,1,0:T(8,128)S(1)} %get-tuple-element.233.refs_2_, ...), custom_call_target="tpu_custom_call" | custom-call | tf_op jit(solution)/shard_map/pallas_call | solution.py:61
  (66 shorter events, 13.2 us)
Async XLA Ops:
  2.3 1.5 %collective-permute-start.1 = (f32[264,128]{1,0:T(8,128)S(1)}, f32[264,128]{1,0:T(8,128)S(1)}, u32[]{:S(2)}, u32[]{:S(2)}) collective-permute-start(f32[264,128]{1,0:T(8,128)S(1)} %get-tuple-element.134), channel_id=1, source_target_pairs={{0,1},{1,0},{2,3},{3,2},{4,5},{5,4},{6,7},{7,6},{8,9},{9,8},{10,11... | collective-permute-start | bytes 405512 | tf_op jit(solution)/shard_map/ppermute | solution.py:411
  3.2 3.6 %collective-permute-start = (f32[264,128]{1,0:T(8,128)S(1)}, f32[264,128]{1,0:T(8,128)S(1)}, u32[]{:S(2)}, u32[]{:S(2)}) collective-permute-start(f32[264,128]{1,0:T(8,128)S(1)} %get-tuple-element.133), channel_id=1, source_target_pairs={{0,1},{1,0},{2,3},{3,2},{4,5},{5,4},{6,7},{7,6},{8,9},{9,8},{10,11... | collective-permute-start | bytes 405512 | tf_op jit(solution)/shard_map/ppermute | solution.py:411
  3.9 5.5 %collective-permute-start.3 = (f32[136,128]{1,0:T(8,128)S(1)}, f32[136,128]{1,0:T(8,128)S(1)}, u32[]{:S(2)}, u32[]{:S(2)}) collective-permute-start(f32[136,128]{1,0:T(8,128)S(1)} %get-tuple-element.138), channel_id=1, source_target_pairs={{0,2},{1,3},{2,0},{3,1},{4,6},{5,7},{6,4},{7,5},{8,10},{9,11},{10,... | collective-permute-start | bytes 208904 | tf_op jit(solution)/shard_map/ppermute | solution.py:411
  6.8 4.7 %collective-permute-start.2 = (f32[136,128]{1,0:T(8,128)S(1)}, f32[136,128]{1,0:T(8,128)S(1)}, u32[]{:S(2)}, u32[]{:S(2)}) collective-permute-start(f32[136,128]{1,0:T(8,128)S(1)} %get-tuple-element.137), channel_id=1, source_target_pairs={{0,2},{1,3},{2,0},{3,1},{4,6},{5,7},{6,4},{7,5},{8,10},{9,11},{10,... | collective-permute-start | bytes 208904 | tf_op jit(solution)/shard_map/ppermute | solution.py:411
  9.4 4.8 %collective-permute-start.5 = (f32[136,128]{1,0:T(8,128)S(1)}, f32[136,128]{1,0:T(8,128)S(1)}, u32[]{:S(2)}, u32[]{:S(2)}) collective-permute-start(f32[136,128]{1,0:T(8,128)S(1)} %shard_map.98.refs_2_.refs_0_), channel_id=1, source_target_pairs={{0,4},{1,5},{2,6},{3,7},{4,0},{5,1},{6,2},{7,3},{8,12},{9,13},{10,... | collective-permute-start | bytes 208904 | tf_op jit(solution)/shard_map/ppermute | solution.py:411
  11.6 5.4 %collective-permute-start.4 = (f32[136,128]{1,0:T(8,128)S(1)}, f32[136,128]{1,0:T(8,128)S(1)}, u32[]{:S(2)}, u32[]{:S(2)}) collective-permute-start(f32[136,128]{1,0:T(8,128)S(1)} %shard_map.99.refs_7_.refs_0_), channel_id=1, source_target_pairs={{0,4},{1,5},{2,6},{3,7},{4,0},{5,1},{6,2},{7,3},{8,12},{9,13},{10,... | collective-permute-start | bytes 208904 | tf_op jit(solution)/shard_map/ppermute | solution.py:411
  14.2 7.1 %collective-permute-start.7 = (f32[136,128]{1,0:T(8,128)S(1)}, f32[136,128]{1,0:T(8,128)S(1)}, u32[]{:S(2)}, u32[]{:S(2)}) collective-permute-start(f32[136,128]{1,0:T(8,128)S(1)} %get-tuple-element.146.refs_2_), channel_id=1, source_target_pairs={{0,8},{1,9},{2,10},{3,11},{4,12},{5,13},{6,14},{7,15},{8,0},{9,1},... | collective-permute-start | bytes 208904 | tf_op jit(solution)/shard_map/ppermute | solution.py:411
  17.0 6.2 %collective-permute-start.6 = (f32[136,128]{1,0:T(8,128)S(1)}, f32[136,128]{1,0:T(8,128)S(1)}, u32[]{:S(2)}, u32[]{:S(2)}) collective-permute-start(f32[136,128]{1,0:T(8,128)S(1)} %get-tuple-element.147.refs_7_), channel_id=1, source_target_pairs={{0,8},{1,9},{2,10},{3,11},{4,12},{5,13},{6,14},{7,15},{8,0},{9,1},... | collective-permute-start | bytes 208904 | tf_op jit(solution)/shard_map/ppermute | solution.py:411
  21.4 4.9 %collective-permute-start.9 = (f32[128,128]{1,0:T(8,128)S(1)}, f32[128,128]{1,0:T(8,128)S(1)}, u32[]{:S(2)}, u32[]{:S(2)}) collective-permute-start(f32[128,128]{1,0:T(8,128)S(1)} %get-tuple-element.155), channel_id=1, source_target_pairs={{0,2},{1,3},{2,0},{3,1},{4,6},{5,7},{6,4},{7,5},{8,10},{9,11},{10,... | collective-permute-start | bytes 196616 | tf_op jit(solution)/shard_map/ppermute | solution.py:411
  23.2 4.4 %collective-permute-start.8 = (f32[128,128]{1,0:T(8,128)S(1)}, f32[128,128]{1,0:T(8,128)S(1)}, u32[]{:S(2)}, u32[]{:S(2)}) collective-permute-start(f32[128,128]{1,0:T(8,128)S(1)} %get-tuple-element.153), channel_id=1, source_target_pairs={{0,2},{1,3},{2,0},{3,1},{4,6},{5,7},{6,4},{7,5},{8,10},{9,11},{10,... | collective-permute-start | bytes 196616 | tf_op jit(solution)/shard_map/ppermute | solution.py:411
  26.3 1.5 %collective-permute-start.11 = (f32[256,128]{1,0:T(8,128)S(1)}, f32[256,128]{1,0:T(8,128)S(1)}, u32[]{:S(2)}, u32[]{:S(2)}) collective-permute-start(f32[256,128]{1,0:T(8,128)S(1)} %get-tuple-element.169), channel_id=1, source_target_pairs={{0,1},{1,0},{2,3},{3,2},{4,5},{5,4},{6,7},{7,6},{8,9},{9,8},{10,11... | collective-permute-start | bytes 393224 | tf_op jit(solution)/shard_map/ppermute | solution.py:411
  27.7 1.4 %collective-permute-start.10 = (f32[256,128]{1,0:T(8,128)S(1)}, f32[256,128]{1,0:T(8,128)S(1)}, u32[]{:S(2)}, u32[]{:S(2)}) collective-permute-start(f32[256,128]{1,0:T(8,128)S(1)} %get-tuple-element.168), channel_id=1, source_target_pairs={{0,1},{1,0},{2,3},{3,2},{4,5},{5,4},{6,7},{7,6},{8,9},{9,8},{10,11... | collective-permute-start | bytes 393224 | tf_op jit(solution)/shard_map/ppermute | solution.py:411
  28.6 1.5 %collective-permute-start.12 = (f32[264,128]{1,0:T(8,128)S(1)}, f32[264,128]{1,0:T(8,128)S(1)}, u32[]{:S(2)}, u32[]{:S(2)}) collective-permute-start(f32[264,128]{1,0:T(8,128)S(1)} %get-tuple-element.174.refs_11_), channel_id=1, source_target_pairs={{0,1},{1,0},{2,3},{3,2},{4,5},{5,4},{6,7},{7,6},{8,9},{9,8},{10,11... | collective-permute-start | bytes 405512 | tf_op jit(solution)/shard_map/ppermute | solution.py:411
  29.8 3.3 %collective-permute-start.13 = (f32[264,128]{1,0:T(8,128)S(1)}, f32[264,128]{1,0:T(8,128)S(1)}, u32[]{:S(2)}, u32[]{:S(2)}) collective-permute-start(f32[264,128]{1,0:T(8,128)S(1)} %get-tuple-element.179.refs_2_), channel_id=1, source_target_pairs={{0,1},{1,0},{2,3},{3,2},{4,5},{5,4},{6,7},{7,6},{8,9},{9,8},{10,11... | collective-permute-start | bytes 405512 | tf_op jit(solution)/shard_map/ppermute | solution.py:411
  30.1 5.0 %collective-permute-start.15 = (f32[136,128]{1,0:T(8,128)S(1)}, f32[136,128]{1,0:T(8,128)S(1)}, u32[]{:S(2)}, u32[]{:S(2)}) collective-permute-start(f32[136,128]{1,0:T(8,128)S(1)} %get-tuple-element.205), channel_id=1, source_target_pairs={{0,2},{1,3},{2,0},{3,1},{4,6},{5,7},{6,4},{7,5},{8,10},{9,11},{10,... | collective-permute-start | bytes 208904 | tf_op jit(solution)/shard_map/ppermute | solution.py:411
  33.2 4.4 %collective-permute-start.14 = (f32[136,128]{1,0:T(8,128)S(1)}, f32[136,128]{1,0:T(8,128)S(1)}, u32[]{:S(2)}, u32[]{:S(2)}) collective-permute-start(f32[136,128]{1,0:T(8,128)S(1)} %get-tuple-element.204), channel_id=1, source_target_pairs={{0,2},{1,3},{2,0},{3,1},{4,6},{5,7},{6,4},{7,5},{8,10},{9,11},{10,... | collective-permute-start | bytes 208904 | tf_op jit(solution)/shard_map/ppermute | solution.py:411
  35.1 4.9 %collective-permute-start.17 = (f32[136,128]{1,0:T(8,128)S(1)}, f32[136,128]{1,0:T(8,128)S(1)}, u32[]{:S(2)}, u32[]{:S(2)}) collective-permute-start(f32[136,128]{1,0:T(8,128)S(1)} %shard_map.116.refs_2_.refs_0_), channel_id=1, source_target_pairs={{0,4},{1,5},{2,6},{3,7},{4,0},{5,1},{6,2},{7,3},{8,12},{9,13},{10,... | collective-permute-start | bytes 208904 | tf_op jit(solution)/shard_map/ppermute | solution.py:411
  37.5 4.7 %collective-permute-start.16 = (f32[136,128]{1,0:T(8,128)S(1)}, f32[136,128]{1,0:T(8,128)S(1)}, u32[]{:S(2)}, u32[]{:S(2)}) collective-permute-start(f32[136,128]{1,0:T(8,128)S(1)} %shard_map.117.refs_13_.refs_0_), channel_id=1, source_target_pairs={{0,4},{1,5},{2,6},{3,7},{4,0},{5,1},{6,2},{7,3},{8,12},{9,13},{10,... | collective-permute-start | bytes 208904 | tf_op jit(solution)/shard_map/ppermute | solution.py:411
  40.1 7.0 %collective-permute-start.19 = (f32[136,128]{1,0:T(8,128)S(1)}, f32[136,128]{1,0:T(8,128)S(1)}, u32[]{:S(2)}, u32[]{:S(2)}) collective-permute-start(f32[136,128]{1,0:T(8,128)S(1)} %get-tuple-element.211.refs_2_), channel_id=1, source_target_pairs={{0,8},{1,9},{2,10},{3,11},{4,12},{5,13},{6,14},{7,15},{8,0},{9,1},... | collective-permute-start | bytes 208904 | tf_op jit(solution)/shard_map/ppermute | solution.py:411
  42.2 6.4 %collective-permute-start.18 = (f32[136,128]{1,0:T(8,128)S(1)}, f32[136,128]{1,0:T(8,128)S(1)}, u32[]{:S(2)}, u32[]{:S(2)}) collective-permute-start(f32[136,128]{1,0:T(8,128)S(1)} %get-tuple-element.212.refs_13_), channel_id=1, source_target_pairs={{0,8},{1,9},{2,10},{3,11},{4,12},{5,13},{6,14},{7,15},{8,0},{9,1},... | collective-permute-start | bytes 208904 | tf_op jit(solution)/shard_map/ppermute | solution.py:411
  47.2 4.7 %collective-permute-start.20 = (f32[128,128]{1,0:T(8,128)S(1)}, f32[128,128]{1,0:T(8,128)S(1)}, u32[]{:S(2)}, u32[]{:S(2)}) collective-permute-start(f32[128,128]{1,0:T(8,128)S(1)} %get-tuple-element.223), channel_id=1, source_target_pairs={{0,2},{1,3},{2,0},{3,1},{4,6},{5,7},{6,4},{7,5},{8,10},{9,11},{10,... | collective-permute-start | bytes 196616 | tf_op jit(solution)/shard_map/ppermute | solution.py:411
  48.6 4.3 %collective-permute-start.21 = (f32[128,128]{1,0:T(8,128)S(1)}, f32[128,128]{1,0:T(8,128)S(1)}, u32[]{:S(2)}, u32[]{:S(2)}) collective-permute-start(f32[128,128]{1,0:T(8,128)S(1)} %get-tuple-element.234), channel_id=1, source_target_pairs={{0,2},{1,3},{2,0},{3,1},{4,6},{5,7},{6,4},{7,5},{8,10},{9,11},{10,... | collective-permute-start | bytes 196616 | tf_op jit(solution)/shard_map/ppermute | solution.py:411
  51.9 1.4 %collective-permute-start.23 = (f32[256,128]{1,0:T(8,128)S(1)}, f32[256,128]{1,0:T(8,128)S(1)}, u32[]{:S(2)}, u32[]{:S(2)}) collective-permute-start(f32[256,128]{1,0:T(8,128)S(1)} %get-tuple-element.242), channel_id=1, source_target_pairs={{0,1},{1,0},{2,3},{3,2},{4,5},{5,4},{6,7},{7,6},{8,9},{9,8},{10,11... | collective-permute-start | bytes 393224 | tf_op jit(solution)/shard_map/ppermute | solution.py:411
  53.0 1.4 %collective-permute-start.22 = (f32[256,128]{1,0:T(8,128)S(1)}, f32[256,128]{1,0:T(8,128)S(1)}, u32[]{:S(2)}, u32[]{:S(2)}) collective-permute-start(f32[256,128]{1,0:T(8,128)S(1)} %get-tuple-element.236), channel_id=1, source_target_pairs={{0,1},{1,0},{2,3},{3,2},{4,5},{5,4},{6,7},{7,6},{8,9},{9,8},{10,11... | collective-permute-start | bytes 393224 | tf_op jit(solution)/shard_map/ppermute | solution.py:411
  (2 other events, 6.3 us)

commit v6 on v5

--- a/solution.py
+++ b/solution.py
@@ -458,7 +458,8 @@
             if step == 1 and late:
                 late(c)
             next(scan)
-        if step and fillers:
+        pieces = int(step > 0) if late else (step > 1) + (step == rounds - 2)
+        for _ in range(min(pieces, len(fillers))):
             fillers.pop(0)()
     for filler in fillers:
         filler()

time: 56.2 us -> 56.2 us (level)
  transfers between devices with their start and end apart: 24 -> 24, of which waited for: 11 -> 10; matrix products, arithmetic and copies ran while one was open for 0% -> 0% of each run, Pallas kernels for 28% -> 28%
where the time goes in v6:
time: 56.2 us; the launch traced here: 56 us
  starting transfers between devices  26.6 us (47%)
  Pallas kernels  19 us (34%)
  waiting for transfers between devices  9.05 us (16%)
  between operations  1.1 us (2%)
    ppermute x24, starting transfers between devices, exchange(): return lax.ppermute(x, 'seq', [(i, i ^ bit) for i in range(count)])  26.6 us
    pallas_call x38, Pallas kernels, run(): pl.pallas_call(kernel, in_specs=[SMEM] + [VMEM] * len(inside) + [HBM] * l...  19 us
    ppermute x24, waiting for transfers between devices, exchange(): return lax.ppermute(x, 'seq', [(i, i ^ bit) for i in range(count)])  9.05 us
  transfers between devices with their start and end apart: 24, of which 10 were waited for; matrix products, arithmetic and copies ran while one was open for 0% of the time, Pallas kernels for 28%

profile of v6, /device:TPU:0, one launch (start us, length us, event | category | flops | bytes accessed | tf_op | source)
XLA Modules:
  0.0 56.0 jit_solution(18302431755214232233)
XLA Ops:
  0.6 1.7 %shard_map.93 = (f32[264,128]{1,0:T(8,128)S(1)}, f32[264,128]{1,0:T(8,128)S(1)}, f32[4,128,128]{2,1,0:T(8,128)S(1)}, f32[32,512]{1,0:T(8,128)S(1)}, f32[512,128]...) custom-call(s32[1]{0:T(128)} %bitcast.scalar_ref, ...), custom_call_target="tpu_custom_call" | custom-call | tf_op jit(solution)/shard_map/pallas_call | solution.py:61
  3.9 2.9 %collective-permute-start.3 = (f32[136,128]{1,0:T(8,128)S(1)}, f32[136,128]{1,0:T(8,128)S(1)}, u32[]{:S(2)}, u32[]{:S(2)}) collective-permute-start(f32[136,128]{1,0:T(8,128)S(1)} %get-tuple-element.138), channel_id=1, source_target_pairs={{0,2},{1,3},{2,0},{3,1},{4,6},{5,7},{6,4},{7,5},{8,10},{9,11},{10,... | collective-permute-start | bytes 208904 | tf_op jit(solution)/shard_map/ppermute | solution.py:411
  7.4 2.0 %collective-permute-done.3.refs_1_.refs_3_ = f32[136,128]{1,0:T(8,128)S(1)} collective-permute-done((f32[136,128]{1,0:T(8,128)S(1)}, f32[136,128]{1,0:T(8,128)S(1)}, u32[]{:S(2)}, u32[]{:S(2)}) %collective-permute-start.3) | collective-permute-done | bytes 69664 | tf_op jit(solution)/shard_map/ppermute | solution.py:411
  9.4 2.2 %collective-permute-start.5 = (f32[136,128]{1,0:T(8,128)S(1)}, f32[136,128]{1,0:T(8,128)S(1)}, u32[]{:S(2)}, u32[]{:S(2)}) collective-permute-start(f32[136,128]{1,0:T(8,128)S(1)} %shard_map.97.refs_2_.refs_0_), channel_id=1, source_target_pairs={{0,4},{1,5},{2,6},{3,7},{4,0},{5,1},{6,2},{7,3},{8,12},{9,13},{10,... | collective-permute-start | bytes 208904 | tf_op jit(solution)/shard_map/ppermute | solution.py:411
  11.6 1.3 %collective-permute-start.4 = (f32[136,128]{1,0:T(8,128)S(1)}, f32[136,128]{1,0:T(8,128)S(1)}, u32[]{:S(2)}, u32[]{:S(2)}) collective-permute-start(f32[136,128]{1,0:T(8,128)S(1)} %shard_map.98.refs_5_.refs_0_), channel_id=1, source_target_pairs={{0,4},{1,5},{2,6},{3,7},{4,0},{5,1},{6,2},{7,3},{8,12},{9,13},{10,... | collective-permute-start | bytes 208904 | tf_op jit(solution)/shard_map/ppermute | solution.py:411
  12.9 0.9 %shard_map.99 = (f32[512,256]{1,0:T(8,128)S(1)}, f32[2,2,256,256]{3,2,1,0:T(8,128)S(1)}, f32[2,2,256,256]{3,2,1,0:T(8,128)S(1)}, bf16[2,2,256,256]{3,2,1,0:T(8,1...) custom-call(s32[1]{0:T(128)} %bitcast.scalar_ref, ...), custom_call_target="tpu_custom_call" | custom-call | tf_op jit(solution)/shard_map/pallas_call | solution.py:61
  14.2 2.8 %collective-permute-start.7 = (f32[136,128]{1,0:T(8,128)S(1)}, f32[136,128]{1,0:T(8,128)S(1)}, u32[]{:S(2)}, u32[]{:S(2)}) collective-permute-start(f32[136,128]{1,0:T(8,128)S(1)} %get-tuple-element.143.refs_2_), channel_id=1, source_target_pairs={{0,8},{1,9},{2,10},{3,11},{4,12},{5,13},{6,14},{7,15},{8,0},{9,1},... | collective-permute-start | bytes 208904 | tf_op jit(solution)/shard_map/ppermute | solution.py:411
  17.0 1.6 %collective-permute-start.6 = (f32[136,128]{1,0:T(8,128)S(1)}, f32[136,128]{1,0:T(8,128)S(1)}, u32[]{:S(2)}, u32[]{:S(2)}) collective-permute-start(f32[136,128]{1,0:T(8,128)S(1)} %get-tuple-element.144.refs_7_), channel_id=1, source_target_pairs={{0,8},{1,9},{2,10},{3,11},{4,12},{5,13},{6,14},{7,15},{8,0},{9,1},... | collective-permute-start | bytes 208904 | tf_op jit(solution)/shard_map/ppermute | solution.py:411
  20.3 1.1 %collective-permute-done.7.refs_0_ = f32[136,128]{1,0:T(8,128)S(1)} collective-permute-done((f32[136,128]{1,0:T(8,128)S(1)}, f32[136,128]{1,0:T(8,128)S(1)}, u32[]{:S(2)}, u32[]{:S(2)}) %collective-permute-start.7) | collective-permute-done | bytes 69664 | tf_op jit(solution)/shard_map/ppermute | solution.py:411
  21.4 1.9 %collective-permute-start.9 = (f32[128,128]{1,0:T(8,128)S(1)}, f32[128,128]{1,0:T(8,128)S(1)}, u32[]{:S(2)}, u32[]{:S(2)}) collective-permute-start(f32[128,128]{1,0:T(8,128)S(1)} %get-tuple-element.155), channel_id=1, source_target_pairs={{0,2},{1,3},{2,0},{3,1},{4,6},{5,7},{6,4},{7,5},{8,10},{9,11},{10,... | collective-permute-start | bytes 196616 | tf_op jit(solution)/shard_map/ppermute | solution.py:411
  23.4 2.1 %collective-permute-start.8 = (f32[128,128]{1,0:T(8,128)S(1)}, f32[128,128]{1,0:T(8,128)S(1)}, u32[]{:S(2)}, u32[]{:S(2)}) collective-permute-start(f32[128,128]{1,0:T(8,128)S(1)} %get-tuple-element.153), channel_id=1, source_target_pairs={{0,2},{1,3},{2,0},{3,1},{4,6},{5,7},{6,4},{7,5},{8,10},{9,11},{10,... | collective-permute-start | bytes 196616 | tf_op jit(solution)/shard_map/ppermute | solution.py:411
  30.1 2.1 %collective-permute-start.15 = (f32[136,128]{1,0:T(8,128)S(1)}, f32[136,128]{1,0:T(8,128)S(1)}, u32[]{:S(2)}, u32[]{:S(2)}) collective-permute-start(f32[136,128]{1,0:T(8,128)S(1)} %get-tuple-element.205), channel_id=1, source_target_pairs={{0,2},{1,3},{2,0},{3,1},{4,6},{5,7},{6,4},{7,5},{8,10},{9,11},{10,... | collective-permute-start | bytes 208904 | tf_op jit(solution)/shard_map/ppermute | solution.py:411
  32.2 0.9 %shard_map.113 = (f32[264,128]{1,0:T(8,128)S(1)}, bf16[512,512]{1,0:T(8,128)(2,1)S(1)}, bf16[4,2,128,128]{3,2,1,0:T(8,128)(2,1)S(1)}, f32[4,128,128]{2,1,0:T(8,128)S(1)}, bf16[512,512]{1,0:T(8,128)(2,1)S(1)}) custom-call(s32[1]{0:T(128)} %bitcast.scalar_ref, ...), custom_call_target="tpu_custom_call", output_to_operand_aliasing={{1}: (12, {}), {2}: (13, {}), {3}: (14, {}), {4}: (15, {})} | custom-call | tf_op jit(solution)/shard_map/pallas_call | solution.py:61
  33.4 1.7 %shard_map.115 = (f32[512,256]{1,0:T(8,128)S(1)}, f32[512,256]{1,0:T(8,128)S(1)}, bf16[512,256]{1,0:T(8,128)(2,1)S(1)}, bf16[512,1024]{1,0:T(8,128)(2,1)}, bf16[512,1024]{1,0:T(8,128)(2,1)}) custom-call(s32[1]{0:T(128)} %bitcast.scalar_ref, bf16[512,1024]{1,0:T(8,128)(2,1)S(1)} %copy-done, bf16[512,512]{1,0:T(8,128)(2,1)S(1)} %get-tuple-element.139.refs_1_.refs_0_, ...), custom_call_target="tpu_custom_call" | custom-call | tf_op jit(solution)/shard_map/pallas_call | solution.py:61
  35.8 1.8 %collective-permute-done.14.refs_1_.refs_3_ = f32[136,128]{1,0:T(8,128)S(1)} collective-permute-done((f32[136,128]{1,0:T(8,128)S(1)}, f32[136,128]{1,0:T(8,128)S(1)}, u32[]{:S(2)}, u32[]{:S(2)}) %collective-permute-start.14) | collective-permute-done | bytes 69664 | tf_op jit(solution)/shard_map/ppermute | solution.py:411
  38.1 1.9 %shard_map.118 = (f32[512,256]{1,0:T(8,128)S(1)}, f32[512,256]{1,0:T(8,128)S(1)}, bf16[512,256]{1,0:T(8,128)(2,1)S(1)}, bf16[512,1024]{1,0:T(8,128)(2,1)}, bf16[512,1024]{1,0:T(8,128)(2,1)}) custom-call(s32[1]{0:T(128)} %bitcast.scalar_ref, bf16[512,1024]{1,0:T(8,128)(2,1)S(1)} %copy-done, ...), custom_call_target="tpu_custom_call", output_to_operand_aliasing={{3}: (12, {}), {4}: (13, {})} | custom-call | tf_op jit(solution)/shard_map/pallas_call | solution.py:61
  40.1 2.1 %collective-permute-start.19 = (f32[136,128]{1,0:T(8,128)S(1)}, f32[136,128]{1,0:T(8,128)S(1)}, u32[]{:S(2)}, u32[]{:S(2)}) collective-permute-start(f32[136,128]{1,0:T(8,128)S(1)} %get-tuple-element.211.refs_2_), channel_id=1, source_target_pairs={{0,8},{1,9},{2,10},{3,11},{4,12},{5,13},{6,14},{7,15},{8,0},{9,1},... | collective-permute-start | bytes 208904 | tf_op jit(solution)/shard_map/ppermute | solution.py:411
  42.2 0.9 %collective-permute-start.18 = (f32[136,128]{1,0:T(8,128)S(1)}, f32[136,128]{1,0:T(8,128)S(1)}, u32[]{:S(2)}, u32[]{:S(2)}) collective-permute-start(f32[136,128]{1,0:T(8,128)S(1)} %get-tuple-element.212.refs_13_), channel_id=1, source_target_pairs={{0,8},{1,9},{2,10},{3,11},{4,12},{5,13},{6,14},{7,15},{8,0},{9,1},... | collective-permute-start | bytes 208904 | tf_op jit(solution)/shard_map/ppermute | solution.py:411
  43.2 1.7 %shard_map.121 = (f32[512,256]{1,0:T(8,128)S(1)}, f32[512,256]{1,0:T(8,128)S(1)}, bf16[512,256]{1,0:T(8,128)(2,1)S(1)}, bf16[512,1024]{1,0:T(8,128)(2,1)}, bf16[512,1024]{1,0:T(8,128)(2,1)}) custom-call(s32[1]{0:T(128)} %bitcast.scalar_ref, bf16[512,1024]{1,0:T(8,128)(2,1)S(1)} %copy-done, ...), custom_call_target="tpu_custom_call", output_to_operand_aliasing={{3}: (12, {}), {4}: (13, {})} | custom-call | tf_op jit(solution)/shard_map/pallas_call | solution.py:61
  44.9 2.2 %collective-permute-done.19.refs_0_ = f32[136,128]{1,0:T(8,128)S(1)} collective-permute-done((f32[136,128]{1,0:T(8,128)S(1)}, f32[136,128]{1,0:T(8,128)S(1)}, u32[]{:S(2)}, u32[]{:S(2)}) %collective-permute-start.19) | collective-permute-done | bytes 69664 | tf_op jit(solution)/shard_map/ppermute | solution.py:411
  47.1 1.3 %collective-permute-start.20 = (f32[128,128]{1,0:T(8,128)S(1)}, f32[128,128]{1,0:T(8,128)S(1)}, u32[]{:S(2)}, u32[]{:S(2)}) collective-permute-start(f32[128,128]{1,0:T(8,128)S(1)} %get-tuple-element.223), channel_id=1, source_target_pairs={{0,2},{1,3},{2,0},{3,1},{4,6},{5,7},{6,4},{7,5},{8,10},{9,11},{10,... | collective-permute-start | bytes 196616 | tf_op jit(solution)/shard_map/ppermute | solution.py:411
  48.6 1.3 %collective-permute-start.21 = (f32[128,128]{1,0:T(8,128)S(1)}, f32[128,128]{1,0:T(8,128)S(1)}, u32[]{:S(2)}, u32[]{:S(2)}) collective-permute-start(f32[128,128]{1,0:T(8,128)S(1)} %get-tuple-element.234), channel_id=1, source_target_pairs={{0,2},{1,3},{2,0},{3,1},{4,6},{5,7},{6,4},{7,5},{8,10},{9,11},{10,... | collective-permute-start | bytes 196616 | tf_op jit(solution)/shard_map/ppermute | solution.py:411
  50.0 1.9 %shard_map.124 = (f32[512,256]{1,0:T(8,128)S(1)}, f32[512,256]{1,0:T(8,128)S(1)}, bf16[512,256]{1,0:T(8,128)(2,1)S(1)}, bf16[512,1024]{1,0:T(8,128)(2,1)}, bf16[512,1024]{1,0:T(8,128)(2,1)}) custom-call(s32[1]{0:T(128)} %bitcast.scalar_ref, bf16[512,1024]{1,0:T(8,128)(2,1)S(1)} %copy-done, ...), custom_call_target="tpu_custom_call", output_to_operand_aliasing={{3}: (12, {}), {4}: (13, {})} | custom-call | tf_op jit(solution)/shard_map/pallas_call | solution.py:61
  54.4 1.4 %shard_map.130 = (bf16[512,1024]{1,0:T(8,128)(2,1)}, bf16[512,1024]{1,0:T(8,128)(2,1)}) custom-call(s32[1]{0:T(128)} %bitcast.scalar_ref, bf16[512,512]{1,0:T(8,128)(2,1)S(1)} %get-tuple-element.127.refs_1_.refs_0_, bf16[512,512]{1,0:T(8,128)(2,1)S(1)} %get-tuple-element.128.refs_2_.refs_1_, f32[4,128,128]{2,1,0:T(8,128)S(1)} %get-tuple-element.233.refs_2_, ...), custom_call_target="tpu_custom_call" | custom-call | tf_op jit(solution)/shard_map/pallas_call | solution.py:61
  (66 shorter events, 13.1 us)
Async XLA Ops:
  2.3 1.5 %collective-permute-start.1 = (f32[264,128]{1,0:T(8,128)S(1)}, f32[264,128]{1,0:T(8,128)S(1)}, u32[]{:S(2)}, u32[]{:S(2)}) collective-permute-start(f32[264,128]{1,0:T(8,128)S(1)} %get-tuple-element.134), channel_id=1, source_target_pairs={{0,1},{1,0},{2,3},{3,2},{4,5},{5,4},{6,7},{7,6},{8,9},{9,8},{10,11... | collective-permute-start | bytes 405512 | tf_op jit(solution)/shard_map/ppermute | solution.py:411
  3.2 3.6 %collective-permute-start = (f32[264,128]{1,0:T(8,128)S(1)}, f32[264,128]{1,0:T(8,128)S(1)}, u32[]{:S(2)}, u32[]{:S(2)}) collective-permute-start(f32[264,128]{1,0:T(8,128)S(1)} %get-tuple-element.133), channel_id=1, source_target_pairs={{0,1},{1,0},{2,3},{3,2},{4,5},{5,4},{6,7},{7,6},{8,9},{9,8},{10,11... | collective-permute-start | bytes 405512 | tf_op jit(solution)/shard_map/ppermute | solution.py:411
  3.9 5.5 %collective-permute-start.3 = (f32[136,128]{1,0:T(8,128)S(1)}, f32[136,128]{1,0:T(8,128)S(1)}, u32[]{:S(2)}, u32[]{:S(2)}) collective-permute-start(f32[136,128]{1,0:T(8,128)S(1)} %get-tuple-element.138), channel_id=1, source_target_pairs={{0,2},{1,3},{2,0},{3,1},{4,6},{5,7},{6,4},{7,5},{8,10},{9,11},{10,... | collective-permute-start | bytes 208904 | tf_op jit(solution)/shard_map/ppermute | solution.py:411
  6.8 4.7 %collective-permute-start.2 = (f32[136,128]{1,0:T(8,128)S(1)}, f32[136,128]{1,0:T(8,128)S(1)}, u32[]{:S(2)}, u32[]{:S(2)}) collective-permute-start(f32[136,128]{1,0:T(8,128)S(1)} %get-tuple-element.137), channel_id=1, source_target_pairs={{0,2},{1,3},{2,0},{3,1},{4,6},{5,7},{6,4},{7,5},{8,10},{9,11},{10,... | collective-permute-start | bytes 208904 | tf_op jit(solution)/shard_map/ppermute | solution.py:411
  9.4 4.8 %collective-permute-start.5 = (f32[136,128]{1,0:T(8,128)S(1)}, f32[136,128]{1,0:T(8,128)S(1)}, u32[]{:S(2)}, u32[]{:S(2)}) collective-permute-start(f32[136,128]{1,0:T(8,128)S(1)} %shard_map.97.refs_2_.refs_0_), channel_id=1, source_target_pairs={{0,4},{1,5},{2,6},{3,7},{4,0},{5,1},{6,2},{7,3},{8,12},{9,13},{10,... | collective-permute-start | bytes 208904 | tf_op jit(solution)/shard_map/ppermute | solution.py:411
  11.6 5.4 %collective-permute-start.4 = (f32[136,128]{1,0:T(8,128)S(1)}, f32[136,128]{1,0:T(8,128)S(1)}, u32[]{:S(2)}, u32[]{:S(2)}) collective-permute-start(f32[136,128]{1,0:T(8,128)S(1)} %shard_map.98.refs_5_.refs_0_), channel_id=1, source_target_pairs={{0,4},{1,5},{2,6},{3,7},{4,0},{5,1},{6,2},{7,3},{8,12},{9,13},{10,... | collective-permute-start | bytes 208904 | tf_op jit(solution)/shard_map/ppermute | solution.py:411
  14.2 7.2 %collective-permute-start.7 = (f32[136,128]{1,0:T(8,128)S(1)}, f32[136,128]{1,0:T(8,128)S(1)}, u32[]{:S(2)}, u32[]{:S(2)}) collective-permute-start(f32[136,128]{1,0:T(8,128)S(1)} %get-tuple-element.143.refs_2_), channel_id=1, source_target_pairs={{0,8},{1,9},{2,10},{3,11},{4,12},{5,13},{6,14},{7,15},{8,0},{9,1},... | collective-permute-start | bytes 208904 | tf_op jit(solution)/shard_map/ppermute | solution.py:411
  17.0 6.3 %collective-permute-start.6 = (f32[136,128]{1,0:T(8,128)S(1)}, f32[136,128]{1,0:T(8,128)S(1)}, u32[]{:S(2)}, u32[]{:S(2)}) collective-permute-start(f32[136,128]{1,0:T(8,128)S(1)} %get-tuple-element.144.refs_7_), channel_id=1, source_target_pairs={{0,8},{1,9},{2,10},{3,11},{4,12},{5,13},{6,14},{7,15},{8,0},{9,1},... | collective-permute-start | bytes 208904 | tf_op jit(solution)/shard_map/ppermute | solution.py:411
  21.4 4.8 %collective-permute-start.9 = (f32[128,128]{1,0:T(8,128)S(1)}, f32[128,128]{1,0:T(8,128)S(1)}, u32[]{:S(2)}, u32[]{:S(2)}) collective-permute-start(f32[128,128]{1,0:T(8,128)S(1)} %get-tuple-element.155), channel_id=1, source_target_pairs={{0,2},{1,3},{2,0},{3,1},{4,6},{5,7},{6,4},{7,5},{8,10},{9,11},{10,... | collective-permute-start | bytes 196616 | tf_op jit(solution)/shard_map/ppermute | solution.py:411
  23.4 4.3 %collective-permute-start.8 = (f32[128,128]{1,0:T(8,128)S(1)}, f32[128,128]{1,0:T(8,128)S(1)}, u32[]{:S(2)}, u32[]{:S(2)}) collective-permute-start(f32[128,128]{1,0:T(8,128)S(1)} %get-tuple-element.153), channel_id=1, source_target_pairs={{0,2},{1,3},{2,0},{3,1},{4,6},{5,7},{6,4},{7,5},{8,10},{9,11},{10,... | collective-permute-start | bytes 196616 | tf_op jit(solution)/shard_map/ppermute | solution.py:411
  26.3 1.5 %collective-permute-start.11 = (f32[256,128]{1,0:T(8,128)S(1)}, f32[256,128]{1,0:T(8,128)S(1)}, u32[]{:S(2)}, u32[]{:S(2)}) collective-permute-start(f32[256,128]{1,0:T(8,128)S(1)} %get-tuple-element.169), channel_id=1, source_target_pairs={{0,1},{1,0},{2,3},{3,2},{4,5},{5,4},{6,7},{7,6},{8,9},{9,8},{10,11... | collective-permute-start | bytes 393224 | tf_op jit(solution)/shard_map/ppermute | solution.py:411
  27.7 1.4 %collective-permute-start.10 = (f32[256,128]{1,0:T(8,128)S(1)}, f32[256,128]{1,0:T(8,128)S(1)}, u32[]{:S(2)}, u32[]{:S(2)}) collective-permute-start(f32[256,128]{1,0:T(8,128)S(1)} %get-tuple-element.168), channel_id=1, source_target_pairs={{0,1},{1,0},{2,3},{3,2},{4,5},{5,4},{6,7},{7,6},{8,9},{9,8},{10,11... | collective-permute-start | bytes 393224 | tf_op jit(solution)/shard_map/ppermute | solution.py:411
  28.5 1.5 %collective-permute-start.12 = (f32[264,128]{1,0:T(8,128)S(1)}, f32[264,128]{1,0:T(8,128)S(1)}, u32[]{:S(2)}, u32[]{:S(2)}) collective-permute-start(f32[264,128]{1,0:T(8,128)S(1)} %get-tuple-element.174.refs_11_), channel_id=1, source_target_pairs={{0,1},{1,0},{2,3},{3,2},{4,5},{5,4},{6,7},{7,6},{8,9},{9,8},{10,11... | collective-permute-start | bytes 405512 | tf_op jit(solution)/shard_map/ppermute | solution.py:411
  29.9 3.3 %collective-permute-start.13 = (f32[264,128]{1,0:T(8,128)S(1)}, f32[264,128]{1,0:T(8,128)S(1)}, u32[]{:S(2)}, u32[]{:S(2)}) collective-permute-start(f32[264,128]{1,0:T(8,128)S(1)} %get-tuple-element.179.refs_2_), channel_id=1, source_target_pairs={{0,1},{1,0},{2,3},{3,2},{4,5},{5,4},{6,7},{7,6},{8,9},{9,8},{10,11... | collective-permute-start | bytes 405512 | tf_op jit(solution)/shard_map/ppermute | solution.py:411
  30.1 5.0 %collective-permute-start.15 = (f32[136,128]{1,0:T(8,128)S(1)}, f32[136,128]{1,0:T(8,128)S(1)}, u32[]{:S(2)}, u32[]{:S(2)}) collective-permute-start(f32[136,128]{1,0:T(8,128)S(1)} %get-tuple-element.205), channel_id=1, source_target_pairs={{0,2},{1,3},{2,0},{3,1},{4,6},{5,7},{6,4},{7,5},{8,10},{9,11},{10,... | collective-permute-start | bytes 208904 | tf_op jit(solution)/shard_map/ppermute | solution.py:411
  33.1 4.4 %collective-permute-start.14 = (f32[136,128]{1,0:T(8,128)S(1)}, f32[136,128]{1,0:T(8,128)S(1)}, u32[]{:S(2)}, u32[]{:S(2)}) collective-permute-start(f32[136,128]{1,0:T(8,128)S(1)} %get-tuple-element.204), channel_id=1, source_target_pairs={{0,2},{1,3},{2,0},{3,1},{4,6},{5,7},{6,4},{7,5},{8,10},{9,11},{10,... | collective-permute-start | bytes 208904 | tf_op jit(solution)/shard_map/ppermute | solution.py:411
  35.2 4.9 %collective-permute-start.17 = (f32[136,128]{1,0:T(8,128)S(1)}, f32[136,128]{1,0:T(8,128)S(1)}, u32[]{:S(2)}, u32[]{:S(2)}) collective-permute-start(f32[136,128]{1,0:T(8,128)S(1)} %shard_map.116.refs_2_.refs_0_), channel_id=1, source_target_pairs={{0,4},{1,5},{2,6},{3,7},{4,0},{5,1},{6,2},{7,3},{8,12},{9,13},{10,... | collective-permute-start | bytes 208904 | tf_op jit(solution)/shard_map/ppermute | solution.py:411
  37.5 4.7 %collective-permute-start.16 = (f32[136,128]{1,0:T(8,128)S(1)}, f32[136,128]{1,0:T(8,128)S(1)}, u32[]{:S(2)}, u32[]{:S(2)}) collective-permute-start(f32[136,128]{1,0:T(8,128)S(1)} %shard_map.117.refs_13_.refs_0_), channel_id=1, source_target_pairs={{0,4},{1,5},{2,6},{3,7},{4,0},{5,1},{6,2},{7,3},{8,12},{9,13},{10,... | collective-permute-start | bytes 208904 | tf_op jit(solution)/shard_map/ppermute | solution.py:411
  40.1 7.0 %collective-permute-start.19 = (f32[136,128]{1,0:T(8,128)S(1)}, f32[136,128]{1,0:T(8,128)S(1)}, u32[]{:S(2)}, u32[]{:S(2)}) collective-permute-start(f32[136,128]{1,0:T(8,128)S(1)} %get-tuple-element.211.refs_2_), channel_id=1, source_target_pairs={{0,8},{1,9},{2,10},{3,11},{4,12},{5,13},{6,14},{7,15},{8,0},{9,1},... | collective-permute-start | bytes 208904 | tf_op jit(solution)/shard_map/ppermute | solution.py:411
  42.2 6.4 %collective-permute-start.18 = (f32[136,128]{1,0:T(8,128)S(1)}, f32[136,128]{1,0:T(8,128)S(1)}, u32[]{:S(2)}, u32[]{:S(2)}) collective-permute-start(f32[136,128]{1,0:T(8,128)S(1)} %get-tuple-element.212.refs_13_), channel_id=1, source_target_pairs={{0,8},{1,9},{2,10},{3,11},{4,12},{5,13},{6,14},{7,15},{8,0},{9,1},... | collective-permute-start | bytes 208904 | tf_op jit(solution)/shard_map/ppermute | solution.py:411
  47.1 4.7 %collective-permute-start.20 = (f32[128,128]{1,0:T(8,128)S(1)}, f32[128,128]{1,0:T(8,128)S(1)}, u32[]{:S(2)}, u32[]{:S(2)}) collective-permute-start(f32[128,128]{1,0:T(8,128)S(1)} %get-tuple-element.223), channel_id=1, source_target_pairs={{0,2},{1,3},{2,0},{3,1},{4,6},{5,7},{6,4},{7,5},{8,10},{9,11},{10,... | collective-permute-start | bytes 196616 | tf_op jit(solution)/shard_map/ppermute | solution.py:411
  48.6 4.3 %collective-permute-start.21 = (f32[128,128]{1,0:T(8,128)S(1)}, f32[128,128]{1,0:T(8,128)S(1)}, u32[]{:S(2)}, u32[]{:S(2)}) collective-permute-start(f32[128,128]{1,0:T(8,128)S(1)} %get-tuple-element.234), channel_id=1, source_target_pairs={{0,2},{1,3},{2,0},{3,1},{4,6},{5,7},{6,4},{7,5},{8,10},{9,11},{10,... | collective-permute-start | bytes 196616 | tf_op jit(solution)/shard_map/ppermute | solution.py:411
  51.9 1.4 %collective-permute-start.23 = (f32[256,128]{1,0:T(8,128)S(1)}, f32[256,128]{1,0:T(8,128)S(1)}, u32[]{:S(2)}, u32[]{:S(2)}) collective-permute-start(f32[256,128]{1,0:T(8,128)S(1)} %get-tuple-element.242), channel_id=1, source_target_pairs={{0,1},{1,0},{2,3},{3,2},{4,5},{5,4},{6,7},{7,6},{8,9},{9,8},{10,11... | collective-permute-start | bytes 393224 | tf_op jit(solution)/shard_map/ppermute | solution.py:411
  53.0 1.4 %collective-permute-start.22 = (f32[256,128]{1,0:T(8,128)S(1)}, f32[256,128]{1,0:T(8,128)S(1)}, u32[]{:S(2)}, u32[]{:S(2)}) collective-permute-start(f32[256,128]{1,0:T(8,128)S(1)} %get-tuple-element.236), channel_id=1, source_target_pairs={{0,1},{1,0},{2,3},{3,2},{4,5},{5,4},{6,7},{7,6},{8,9},{9,8},{10,11... | collective-permute-start | bytes 393224 | tf_op jit(solution)/shard_map/ppermute | solution.py:411
  (2 other events, 11.2 us)

commit v7 on v6

--- a/solution.py
+++ b/solution.py
@@ -15,7 +15,7 @@
 GROUPS = 4
 CHUNKS = 2
 K3_TURNS = ((0, 0), (0, 1), (1, 1))
-K5_TURNS = ((0, 0), (0, 1), (1, 0), (1, 1))
+K5_TURNS = ((0, 0), (1, 0), (0, 1), (1, 1))
 PIECES = 2
 F32 = jnp.float32
 BF16 = jnp.bfloat16

time: 56.2 us -> 56.2 us (level)
  no operation moved by 1% of the time
where the time goes in v7:
time: 56.2 us; the launch traced here: 56 us
  starting transfers between devices  26.6 us (47%)
  Pallas kernels  19 us (34%)
  waiting for transfers between devices  9.04 us (16%)
  between operations  1.11 us (2%)
    ppermute x24, starting transfers between devices, exchange(): return lax.ppermute(x, 'seq', [(i, i ^ bit) for i in range(count)])  26.6 us
    pallas_call x38, Pallas kernels, run(): pl.pallas_call(kernel, in_specs=[SMEM] + [VMEM] * len(inside) + [HBM] * l...  19 us
    ppermute x24, waiting for transfers between devices, exchange(): return lax.ppermute(x, 'seq', [(i, i ^ bit) for i in range(count)])  9.04 us
  transfers between devices with their start and end apart: 24, of which 10 were waited for; matrix products, arithmetic and copies ran while one was open for 0% of the time, Pallas kernels for 28%

profile of v7, /device:TPU:0, one launch (start us, length us, event | category | flops | bytes accessed | tf_op | source)
XLA Modules:
  0.0 56.0 jit_solution(14738618763552127588)
XLA Ops:
  0.6 1.7 %shard_map.93 = (f32[264,128]{1,0:T(8,128)S(1)}, f32[264,128]{1,0:T(8,128)S(1)}, f32[4,128,128]{2,1,0:T(8,128)S(1)}, f32[32,512]{1,0:T(8,128)S(1)}, f32[512,128]...) custom-call(s32[1]{0:T(128)} %bitcast.scalar_ref, ...), custom_call_target="tpu_custom_call" | custom-call | tf_op jit(solution)/shard_map/pallas_call | solution.py:61
  3.9 2.9 %collective-permute-start.3 = (f32[136,128]{1,0:T(8,128)S(1)}, f32[136,128]{1,0:T(8,128)S(1)}, u32[]{:S(2)}, u32[]{:S(2)}) collective-permute-start(f32[136,128]{1,0:T(8,128)S(1)} %get-tuple-element.138), channel_id=1, source_target_pairs={{0,2},{1,3},{2,0},{3,1},{4,6},{5,7},{6,4},{7,5},{8,10},{9,11},{10,... | collective-permute-start | bytes 208904 | tf_op jit(solution)/shard_map/ppermute | solution.py:411
  7.4 2.0 %collective-permute-done.3.refs_1_.refs_3_ = f32[136,128]{1,0:T(8,128)S(1)} collective-permute-done((f32[136,128]{1,0:T(8,128)S(1)}, f32[136,128]{1,0:T(8,128)S(1)}, u32[]{:S(2)}, u32[]{:S(2)}) %collective-permute-start.3) | collective-permute-done | bytes 69664 | tf_op jit(solution)/shard_map/ppermute | solution.py:411
  9.4 2.2 %collective-permute-start.5 = (f32[136,128]{1,0:T(8,128)S(1)}, f32[136,128]{1,0:T(8,128)S(1)}, u32[]{:S(2)}, u32[]{:S(2)}) collective-permute-start(f32[136,128]{1,0:T(8,128)S(1)} %shard_map.97.refs_2_.refs_0_), channel_id=1, source_target_pairs={{0,4},{1,5},{2,6},{3,7},{4,0},{5,1},{6,2},{7,3},{8,12},{9,13},{10,... | collective-permute-start | bytes 208904 | tf_op jit(solution)/shard_map/ppermute | solution.py:411
  11.6 1.3 %collective-permute-start.4 = (f32[136,128]{1,0:T(8,128)S(1)}, f32[136,128]{1,0:T(8,128)S(1)}, u32[]{:S(2)}, u32[]{:S(2)}) collective-permute-start(f32[136,128]{1,0:T(8,128)S(1)} %shard_map.98.refs_5_.refs_0_), channel_id=1, source_target_pairs={{0,4},{1,5},{2,6},{3,7},{4,0},{5,1},{6,2},{7,3},{8,12},{9,13},{10,... | collective-permute-start | bytes 208904 | tf_op jit(solution)/shard_map/ppermute | solution.py:411
  12.9 0.9 %shard_map.99 = (f32[512,256]{1,0:T(8,128)S(1)}, f32[2,2,256,256]{3,2,1,0:T(8,128)S(1)}, f32[2,2,256,256]{3,2,1,0:T(8,128)S(1)}, bf16[2,2,256,256]{3,2,1,0:T(8,1...) custom-call(s32[1]{0:T(128)} %bitcast.scalar_ref, ...), custom_call_target="tpu_custom_call" | custom-call | tf_op jit(solution)/shard_map/pallas_call | solution.py:61
  14.2 2.8 %collective-permute-start.7 = (f32[136,128]{1,0:T(8,128)S(1)}, f32[136,128]{1,0:T(8,128)S(1)}, u32[]{:S(2)}, u32[]{:S(2)}) collective-permute-start(f32[136,128]{1,0:T(8,128)S(1)} %get-tuple-element.143.refs_2_), channel_id=1, source_target_pairs={{0,8},{1,9},{2,10},{3,11},{4,12},{5,13},{6,14},{7,15},{8,0},{9,1},... | collective-permute-start | bytes 208904 | tf_op jit(solution)/shard_map/ppermute | solution.py:411
  17.0 1.6 %collective-permute-start.6 = (f32[136,128]{1,0:T(8,128)S(1)}, f32[136,128]{1,0:T(8,128)S(1)}, u32[]{:S(2)}, u32[]{:S(2)}) collective-permute-start(f32[136,128]{1,0:T(8,128)S(1)} %get-tuple-element.144.refs_7_), channel_id=1, source_target_pairs={{0,8},{1,9},{2,10},{3,11},{4,12},{5,13},{6,14},{7,15},{8,0},{9,1},... | collective-permute-start | bytes 208904 | tf_op jit(solution)/shard_map/ppermute | solution.py:411
  20.3 1.1 %collective-permute-done.7.refs_0_ = f32[136,128]{1,0:T(8,128)S(1)} collective-permute-done((f32[136,128]{1,0:T(8,128)S(1)}, f32[136,128]{1,0:T(8,128)S(1)}, u32[]{:S(2)}, u32[]{:S(2)}) %collective-permute-start.7) | collective-permute-done | bytes 69664 | tf_op jit(solution)/shard_map/ppermute | solution.py:411
  21.4 1.9 %collective-permute-start.9 = (f32[128,128]{1,0:T(8,128)S(1)}, f32[128,128]{1,0:T(8,128)S(1)}, u32[]{:S(2)}, u32[]{:S(2)}) collective-permute-start(f32[128,128]{1,0:T(8,128)S(1)} %get-tuple-element.155), channel_id=1, source_target_pairs={{0,2},{1,3},{2,0},{3,1},{4,6},{5,7},{6,4},{7,5},{8,10},{9,11},{10,... | collective-permute-start | bytes 196616 | tf_op jit(solution)/shard_map/ppermute | solution.py:411
  23.4 2.1 %collective-permute-start.8 = (f32[128,128]{1,0:T(8,128)S(1)}, f32[128,128]{1,0:T(8,128)S(1)}, u32[]{:S(2)}, u32[]{:S(2)}) collective-permute-start(f32[128,128]{1,0:T(8,128)S(1)} %get-tuple-element.153), channel_id=1, source_target_pairs={{0,2},{1,3},{2,0},{3,1},{4,6},{5,7},{6,4},{7,5},{8,10},{9,11},{10,... | collective-permute-start | bytes 196616 | tf_op jit(solution)/shard_map/ppermute | solution.py:411
  30.1 2.1 %collective-permute-start.15 = (f32[136,128]{1,0:T(8,128)S(1)}, f32[136,128]{1,0:T(8,128)S(1)}, u32[]{:S(2)}, u32[]{:S(2)}) collective-permute-start(f32[136,128]{1,0:T(8,128)S(1)} %get-tuple-element.205), channel_id=1, source_target_pairs={{0,2},{1,3},{2,0},{3,1},{4,6},{5,7},{6,4},{7,5},{8,10},{9,11},{10,... | collective-permute-start | bytes 208904 | tf_op jit(solution)/shard_map/ppermute | solution.py:411
  32.2 0.9 %shard_map.113 = (f32[264,128]{1,0:T(8,128)S(1)}, bf16[512,512]{1,0:T(8,128)(2,1)S(1)}, bf16[4,2,128,128]{3,2,1,0:T(8,128)(2,1)S(1)}, f32[4,128,128]{2,1,0:T(8,128)S(1)}, bf16[512,512]{1,0:T(8,128)(2,1)S(1)}) custom-call(s32[1]{0:T(128)} %bitcast.scalar_ref, ...), custom_call_target="tpu_custom_call", output_to_operand_aliasing={{1}: (12, {}), {2}: (13, {}), {3}: (14, {}), {4}: (15, {})} | custom-call | tf_op jit(solution)/shard_map/pallas_call | solution.py:61
  33.4 1.7 %shard_map.115 = (f32[512,256]{1,0:T(8,128)S(1)}, f32[512,256]{1,0:T(8,128)S(1)}, bf16[512,256]{1,0:T(8,128)(2,1)S(1)}, bf16[512,1024]{1,0:T(8,128)(2,1)}, bf16[512,1024]{1,0:T(8,128)(2,1)}) custom-call(s32[1]{0:T(128)} %bitcast.scalar_ref, bf16[512,1024]{1,0:T(8,128)(2,1)S(1)} %copy-done, bf16[512,512]{1,0:T(8,128)(2,1)S(1)} %get-tuple-element.139.refs_1_.refs_0_, ...), custom_call_target="tpu_custom_call" | custom-call | tf_op jit(solution)/shard_map/pallas_call | solution.py:61
  35.8 1.8 %collective-permute-done.14.refs_1_.refs_3_ = f32[136,128]{1,0:T(8,128)S(1)} collective-permute-done((f32[136,128]{1,0:T(8,128)S(1)}, f32[136,128]{1,0:T(8,128)S(1)}, u32[]{:S(2)}, u32[]{:S(2)}) %collective-permute-start.14) | collective-permute-done | bytes 69664 | tf_op jit(solution)/shard_map/ppermute | solution.py:411
  38.1 1.9 %shard_map.118 = (f32[512,256]{1,0:T(8,128)S(1)}, f32[512,256]{1,0:T(8,128)S(1)}, bf16[512,256]{1,0:T(8,128)(2,1)S(1)}, bf16[512,1024]{1,0:T(8,128)(2,1)}, bf16[512,1024]{1,0:T(8,128)(2,1)}) custom-call(s32[1]{0:T(128)} %bitcast.scalar_ref, bf16[512,1024]{1,0:T(8,128)(2,1)S(1)} %copy-done, ...), custom_call_target="tpu_custom_call", output_to_operand_aliasing={{3}: (12, {}), {4}: (13, {})} | custom-call | tf_op jit(solution)/shard_map/pallas_call | solution.py:61
  40.1 2.1 %collective-permute-start.19 = (f32[136,128]{1,0:T(8,128)S(1)}, f32[136,128]{1,0:T(8,128)S(1)}, u32[]{:S(2)}, u32[]{:S(2)}) collective-permute-start(f32[136,128]{1,0:T(8,128)S(1)} %get-tuple-element.211.refs_2_), channel_id=1, source_target_pairs={{0,8},{1,9},{2,10},{3,11},{4,12},{5,13},{6,14},{7,15},{8,0},{9,1},... | collective-permute-start | bytes 208904 | tf_op jit(solution)/shard_map/ppermute | solution.py:411
  42.2 0.9 %collective-permute-start.18 = (f32[136,128]{1,0:T(8,128)S(1)}, f32[136,128]{1,0:T(8,128)S(1)}, u32[]{:S(2)}, u32[]{:S(2)}) collective-permute-start(f32[136,128]{1,0:T(8,128)S(1)} %get-tuple-element.212.refs_13_), channel_id=1, source_target_pairs={{0,8},{1,9},{2,10},{3,11},{4,12},{5,13},{6,14},{7,15},{8,0},{9,1},... | collective-permute-start | bytes 208904 | tf_op jit(solution)/shard_map/ppermute | solution.py:411
  43.2 1.7 %shard_map.121 = (f32[512,256]{1,0:T(8,128)S(1)}, f32[512,256]{1,0:T(8,128)S(1)}, bf16[512,256]{1,0:T(8,128)(2,1)S(1)}, bf16[512,1024]{1,0:T(8,128)(2,1)}, bf16[512,1024]{1,0:T(8,128)(2,1)}) custom-call(s32[1]{0:T(128)} %bitcast.scalar_ref, bf16[512,1024]{1,0:T(8,128)(2,1)S(1)} %copy-done, ...), custom_call_target="tpu_custom_call", output_to_operand_aliasing={{3}: (12, {}), {4}: (13, {})} | custom-call | tf_op jit(solution)/shard_map/pallas_call | solution.py:61
  44.9 2.2 %collective-permute-done.19.refs_0_ = f32[136,128]{1,0:T(8,128)S(1)} collective-permute-done((f32[136,128]{1,0:T(8,128)S(1)}, f32[136,128]{1,0:T(8,128)S(1)}, u32[]{:S(2)}, u32[]{:S(2)}) %collective-permute-start.19) | collective-permute-done | bytes 69664 | tf_op jit(solution)/shard_map/ppermute | solution.py:411
  47.1 1.3 %collective-permute-start.20 = (f32[128,128]{1,0:T(8,128)S(1)}, f32[128,128]{1,0:T(8,128)S(1)}, u32[]{:S(2)}, u32[]{:S(2)}) collective-permute-start(f32[128,128]{1,0:T(8,128)S(1)} %get-tuple-element.223), channel_id=1, source_target_pairs={{0,2},{1,3},{2,0},{3,1},{4,6},{5,7},{6,4},{7,5},{8,10},{9,11},{10,... | collective-permute-start | bytes 196616 | tf_op jit(solution)/shard_map/ppermute | solution.py:411
  48.6 1.3 %collective-permute-start.21 = (f32[128,128]{1,0:T(8,128)S(1)}, f32[128,128]{1,0:T(8,128)S(1)}, u32[]{:S(2)}, u32[]{:S(2)}) collective-permute-start(f32[128,128]{1,0:T(8,128)S(1)} %get-tuple-element.234), channel_id=1, source_target_pairs={{0,2},{1,3},{2,0},{3,1},{4,6},{5,7},{6,4},{7,5},{8,10},{9,11},{10,... | collective-permute-start | bytes 196616 | tf_op jit(solution)/shard_map/ppermute | solution.py:411
  50.0 1.9 %shard_map.124 = (f32[512,256]{1,0:T(8,128)S(1)}, f32[512,256]{1,0:T(8,128)S(1)}, bf16[512,256]{1,0:T(8,128)(2,1)S(1)}, bf16[512,1024]{1,0:T(8,128)(2,1)}, bf16[512,1024]{1,0:T(8,128)(2,1)}) custom-call(s32[1]{0:T(128)} %bitcast.scalar_ref, bf16[512,1024]{1,0:T(8,128)(2,1)S(1)} %copy-done, ...), custom_call_target="tpu_custom_call", output_to_operand_aliasing={{3}: (12, {}), {4}: (13, {})} | custom-call | tf_op jit(solution)/shard_map/pallas_call | solution.py:61
  54.4 1.4 %shard_map.130 = (bf16[512,1024]{1,0:T(8,128)(2,1)}, bf16[512,1024]{1,0:T(8,128)(2,1)}) custom-call(s32[1]{0:T(128)} %bitcast.scalar_ref, bf16[512,512]{1,0:T(8,128)(2,1)S(1)} %get-tuple-element.127.refs_1_.refs_0_, bf16[512,512]{1,0:T(8,128)(2,1)S(1)} %get-tuple-element.128.refs_2_.refs_1_, f32[4,128,128]{2,1,0:T(8,128)S(1)} %get-tuple-element.233.refs_2_, ...), custom_call_target="tpu_custom_call" | custom-call | tf_op jit(solution)/shard_map/pallas_call | solution.py:61
  (66 shorter events, 13.1 us)
Async XLA Ops:
  2.3 1.5 %collective-permute-start.1 = (f32[264,128]{1,0:T(8,128)S(1)}, f32[264,128]{1,0:T(8,128)S(1)}, u32[]{:S(2)}, u32[]{:S(2)}) collective-permute-start(f32[264,128]{1,0:T(8,128)S(1)} %get-tuple-element.134), channel_id=1, source_target_pairs={{0,1},{1,0},{2,3},{3,2},{4,5},{5,4},{6,7},{7,6},{8,9},{9,8},{10,11... | collective-permute-start | bytes 405512 | tf_op jit(solution)/shard_map/ppermute | solution.py:411
  3.2 3.6 %collective-permute-start = (f32[264,128]{1,0:T(8,128)S(1)}, f32[264,128]{1,0:T(8,128)S(1)}, u32[]{:S(2)}, u32[]{:S(2)}) collective-permute-start(f32[264,128]{1,0:T(8,128)S(1)} %get-tuple-element.133), channel_id=1, source_target_pairs={{0,1},{1,0},{2,3},{3,2},{4,5},{5,4},{6,7},{7,6},{8,9},{9,8},{10,11... | collective-permute-start | bytes 405512 | tf_op jit(solution)/shard_map/ppermute | solution.py:411
  3.9 5.5 %collective-permute-start.3 = (f32[136,128]{1,0:T(8,128)S(1)}, f32[136,128]{1,0:T(8,128)S(1)}, u32[]{:S(2)}, u32[]{:S(2)}) collective-permute-start(f32[136,128]{1,0:T(8,128)S(1)} %get-tuple-element.138), channel_id=1, source_target_pairs={{0,2},{1,3},{2,0},{3,1},{4,6},{5,7},{6,4},{7,5},{8,10},{9,11},{10,... | collective-permute-start | bytes 208904 | tf_op jit(solution)/shard_map/ppermute | solution.py:411
  6.8 4.7 %collective-permute-start.2 = (f32[136,128]{1,0:T(8,128)S(1)}, f32[136,128]{1,0:T(8,128)S(1)}, u32[]{:S(2)}, u32[]{:S(2)}) collective-permute-start(f32[136,128]{1,0:T(8,128)S(1)} %get-tuple-element.137), channel_id=1, source_target_pairs={{0,2},{1,3},{2,0},{3,1},{4,6},{5,7},{6,4},{7,5},{8,10},{9,11},{10,... | collective-permute-start | bytes 208904 | tf_op jit(solution)/shard_map/ppermute | solution.py:411
  9.4 4.8 %collective-permute-start.5 = (f32[136,128]{1,0:T(8,128)S(1)}, f32[136,128]{1,0:T(8,128)S(1)}, u32[]{:S(2)}, u32[]{:S(2)}) collective-permute-start(f32[136,128]{1,0:T(8,128)S(1)} %shard_map.97.refs_2_.refs_0_), channel_id=1, source_target_pairs={{0,4},{1,5},{2,6},{3,7},{4,0},{5,1},{6,2},{7,3},{8,12},{9,13},{10,... | collective-permute-start | bytes 208904 | tf_op jit(solution)/shard_map/ppermute | solution.py:411
  11.6 5.4 %collective-permute-start.4 = (f32[136,128]{1,0:T(8,128)S(1)}, f32[136,128]{1,0:T(8,128)S(1)}, u32[]{:S(2)}, u32[]{:S(2)}) collective-permute-start(f32[136,128]{1,0:T(8,128)S(1)} %shard_map.98.refs_5_.refs_0_), channel_id=1, source_target_pairs={{0,4},{1,5},{2,6},{3,7},{4,0},{5,1},{6,2},{7,3},{8,12},{9,13},{10,... | collective-permute-start | bytes 208904 | tf_op jit(solution)/shard_map/ppermute | solution.py:411
  14.2 7.2 %collective-permute-start.7 = (f32[136,128]{1,0:T(8,128)S(1)}, f32[136,128]{1,0:T(8,128)S(1)}, u32[]{:S(2)}, u32[]{:S(2)}) collective-permute-start(f32[136,128]{1,0:T(8,128)S(1)} %get-tuple-element.143.refs_2_), channel_id=1, source_target_pairs={{0,8},{1,9},{2,10},{3,11},{4,12},{5,13},{6,14},{7,15},{8,0},{9,1},... | collective-permute-start | bytes 208904 | tf_op jit(solution)/shard_map/ppermute | solution.py:411
  17.0 6.3 %collective-permute-start.6 = (f32[136,128]{1,0:T(8,128)S(1)}, f32[136,128]{1,0:T(8,128)S(1)}, u32[]{:S(2)}, u32[]{:S(2)}) collective-permute-start(f32[136,128]{1,0:T(8,128)S(1)} %get-tuple-element.144.refs_7_), channel_id=1, source_target_pairs={{0,8},{1,9},{2,10},{3,11},{4,12},{5,13},{6,14},{7,15},{8,0},{9,1},... | collective-permute-start | bytes 208904 | tf_op jit(solution)/shard_map/ppermute | solution.py:411
  21.4 4.8 %collective-permute-start.9 = (f32[128,128]{1,0:T(8,128)S(1)}, f32[128,128]{1,0:T(8,128)S(1)}, u32[]{:S(2)}, u32[]{:S(2)}) collective-permute-start(f32[128,128]{1,0:T(8,128)S(1)} %get-tuple-element.155), channel_id=1, source_target_pairs={{0,2},{1,3},{2,0},{3,1},{4,6},{5,7},{6,4},{7,5},{8,10},{9,11},{10,... | collective-permute-start | bytes 196616 | tf_op jit(solution)/shard_map/ppermute | solution.py:411
  23.4 4.3 %collective-permute-start.8 = (f32[128,128]{1,0:T(8,128)S(1)}, f32[128,128]{1,0:T(8,128)S(1)}, u32[]{:S(2)}, u32[]{:S(2)}) collective-permute-start(f32[128,128]{1,0:T(8,128)S(1)} %get-tuple-element.153), channel_id=1, source_target_pairs={{0,2},{1,3},{2,0},{3,1},{4,6},{5,7},{6,4},{7,5},{8,10},{9,11},{10,... | collective-permute-start | bytes 196616 | tf_op jit(solution)/shard_map/ppermute | solution.py:411
  26.3 1.5 %collective-permute-start.11 = (f32[256,128]{1,0:T(8,128)S(1)}, f32[256,128]{1,0:T(8,128)S(1)}, u32[]{:S(2)}, u32[]{:S(2)}) collective-permute-start(f32[256,128]{1,0:T(8,128)S(1)} %get-tuple-element.169), channel_id=1, source_target_pairs={{0,1},{1,0},{2,3},{3,2},{4,5},{5,4},{6,7},{7,6},{8,9},{9,8},{10,11... | collective-permute-start | bytes 393224 | tf_op jit(solution)/shard_map/ppermute | solution.py:411
  27.7 1.4 %collective-permute-start.10 = (f32[256,128]{1,0:T(8,128)S(1)}, f32[256,128]{1,0:T(8,128)S(1)}, u32[]{:S(2)}, u32[]{:S(2)}) collective-permute-start(f32[256,128]{1,0:T(8,128)S(1)} %get-tuple-element.168), channel_id=1, source_target_pairs={{0,1},{1,0},{2,3},{3,2},{4,5},{5,4},{6,7},{7,6},{8,9},{9,8},{10,11... | collective-permute-start | bytes 393224 | tf_op jit(solution)/shard_map/ppermute | solution.py:411
  28.5 1.5 %collective-permute-start.12 = (f32[264,128]{1,0:T(8,128)S(1)}, f32[264,128]{1,0:T(8,128)S(1)}, u32[]{:S(2)}, u32[]{:S(2)}) collective-permute-start(f32[264,128]{1,0:T(8,128)S(1)} %get-tuple-element.174.refs_11_), channel_id=1, source_target_pairs={{0,1},{1,0},{2,3},{3,2},{4,5},{5,4},{6,7},{7,6},{8,9},{9,8},{10,11... | collective-permute-start | bytes 405512 | tf_op jit(solution)/shard_map/ppermute | solution.py:411
  29.9 3.3 %collective-permute-start.13 = (f32[264,128]{1,0:T(8,128)S(1)}, f32[264,128]{1,0:T(8,128)S(1)}, u32[]{:S(2)}, u32[]{:S(2)}) collective-permute-start(f32[264,128]{1,0:T(8,128)S(1)} %get-tuple-element.179.refs_2_), channel_id=1, source_target_pairs={{0,1},{1,0},{2,3},{3,2},{4,5},{5,4},{6,7},{7,6},{8,9},{9,8},{10,11... | collective-permute-start | bytes 405512 | tf_op jit(solution)/shard_map/ppermute | solution.py:411
  30.1 5.0 %collective-permute-start.15 = (f32[136,128]{1,0:T(8,128)S(1)}, f32[136,128]{1,0:T(8,128)S(1)}, u32[]{:S(2)}, u32[]{:S(2)}) collective-permute-start(f32[136,128]{1,0:T(8,128)S(1)} %get-tuple-element.205), channel_id=1, source_target_pairs={{0,2},{1,3},{2,0},{3,1},{4,6},{5,7},{6,4},{7,5},{8,10},{9,11},{10,... | collective-permute-start | bytes 208904 | tf_op jit(solution)/shard_map/ppermute | solution.py:411
  33.1 4.4 %collective-permute-start.14 = (f32[136,128]{1,0:T(8,128)S(1)}, f32[136,128]{1,0:T(8,128)S(1)}, u32[]{:S(2)}, u32[]{:S(2)}) collective-permute-start(f32[136,128]{1,0:T(8,128)S(1)} %get-tuple-element.204), channel_id=1, source_target_pairs={{0,2},{1,3},{2,0},{3,1},{4,6},{5,7},{6,4},{7,5},{8,10},{9,11},{10,... | collective-permute-start | bytes 208904 | tf_op jit(solution)/shard_map/ppermute | solution.py:411
  35.2 4.9 %collective-permute-start.17 = (f32[136,128]{1,0:T(8,128)S(1)}, f32[136,128]{1,0:T(8,128)S(1)}, u32[]{:S(2)}, u32[]{:S(2)}) collective-permute-start(f32[136,128]{1,0:T(8,128)S(1)} %shard_map.116.refs_2_.refs_0_), channel_id=1, source_target_pairs={{0,4},{1,5},{2,6},{3,7},{4,0},{5,1},{6,2},{7,3},{8,12},{9,13},{10,... | collective-permute-start | bytes 208904 | tf_op jit(solution)/shard_map/ppermute | solution.py:411
  37.5 4.7 %collective-permute-start.16 = (f32[136,128]{1,0:T(8,128)S(1)}, f32[136,128]{1,0:T(8,128)S(1)}, u32[]{:S(2)}, u32[]{:S(2)}) collective-permute-start(f32[136,128]{1,0:T(8,128)S(1)} %shard_map.117.refs_13_.refs_0_), channel_id=1, source_target_pairs={{0,4},{1,5},{2,6},{3,7},{4,0},{5,1},{6,2},{7,3},{8,12},{9,13},{10,... | collective-permute-start | bytes 208904 | tf_op jit(solution)/shard_map/ppermute | solution.py:411
  40.1 7.0 %collective-permute-start.19 = (f32[136,128]{1,0:T(8,128)S(1)}, f32[136,128]{1,0:T(8,128)S(1)}, u32[]{:S(2)}, u32[]{:S(2)}) collective-permute-start(f32[136,128]{1,0:T(8,128)S(1)} %get-tuple-element.211.refs_2_), channel_id=1, source_target_pairs={{0,8},{1,9},{2,10},{3,11},{4,12},{5,13},{6,14},{7,15},{8,0},{9,1},... | collective-permute-start | bytes 208904 | tf_op jit(solution)/shard_map/ppermute | solution.py:411
  42.2 6.4 %collective-permute-start.18 = (f32[136,128]{1,0:T(8,128)S(1)}, f32[136,128]{1,0:T(8,128)S(1)}, u32[]{:S(2)}, u32[]{:S(2)}) collective-permute-start(f32[136,128]{1,0:T(8,128)S(1)} %get-tuple-element.212.refs_13_), channel_id=1, source_target_pairs={{0,8},{1,9},{2,10},{3,11},{4,12},{5,13},{6,14},{7,15},{8,0},{9,1},... | collective-permute-start | bytes 208904 | tf_op jit(solution)/shard_map/ppermute | solution.py:411
  47.1 4.7 %collective-permute-start.20 = (f32[128,128]{1,0:T(8,128)S(1)}, f32[128,128]{1,0:T(8,128)S(1)}, u32[]{:S(2)}, u32[]{:S(2)}) collective-permute-start(f32[128,128]{1,0:T(8,128)S(1)} %get-tuple-element.223), channel_id=1, source_target_pairs={{0,2},{1,3},{2,0},{3,1},{4,6},{5,7},{6,4},{7,5},{8,10},{9,11},{10,... | collective-permute-start | bytes 196616 | tf_op jit(solution)/shard_map/ppermute | solution.py:411
  48.6 4.3 %collective-permute-start.21 = (f32[128,128]{1,0:T(8,128)S(1)}, f32[128,128]{1,0:T(8,128)S(1)}, u32[]{:S(2)}, u32[]{:S(2)}) collective-permute-start(f32[128,128]{1,0:T(8,128)S(1)} %get-tuple-element.234), channel_id=1, source_target_pairs={{0,2},{1,3},{2,0},{3,1},{4,6},{5,7},{6,4},{7,5},{8,10},{9,11},{10,... | collective-permute-start | bytes 196616 | tf_op jit(solution)/shard_map/ppermute | solution.py:411
  51.9 1.8 %collective-permute-start.23 = (f32[256,128]{1,0:T(8,128)S(1)}, f32[256,128]{1,0:T(8,128)S(1)}, u32[]{:S(2)}, u32[]{:S(2)}) collective-permute-start(f32[256,128]{1,0:T(8,128)S(1)} %get-tuple-element.245), channel_id=1, source_target_pairs={{0,1},{1,0},{2,3},{3,2},{4,5},{5,4},{6,7},{7,6},{8,9},{9,8},{10,11... | collective-permute-start | bytes 393224 | tf_op jit(solution)/shard_map/ppermute | solution.py:411
  53.0 1.4 %collective-permute-start.22 = (f32[256,128]{1,0:T(8,128)S(1)}, f32[256,128]{1,0:T(8,128)S(1)}, u32[]{:S(2)}, u32[]{:S(2)}) collective-permute-start(f32[256,128]{1,0:T(8,128)S(1)} %get-tuple-element.236), channel_id=1, source_target_pairs={{0,1},{1,0},{2,3},{3,2},{4,5},{5,4},{6,7},{7,6},{8,9},{9,8},{10,11... | collective-permute-start | bytes 393224 | tf_op jit(solution)/shard_map/ppermute | solution.py:411
  (2 other events, 11.2 us)
